TPU v7x, 32 devices: a whole 2x2x4 slice. The times are simulated.
32 devices in a mesh: dp: 16 (over z, y, core), tensor: 2 (over x).
Axes of the slice: x: 2, y: 2, z: 4, core: 2. Of those that a mesh axis runs over, the one named last changes fastest.
Arguments:
- hidden_in: bfloat16 [2, 16, 256, 2048], P(None, 'dp', 'tensor'), may hold values from -6 to 6
- segment_ids: int32 [2, 16, 256], P(None, 'dp'), may hold values from 0 to 1, never falling along the last dimension, each value on 1 to 192 neighbouring positions
- attn_gain: bfloat16 [2048], P('dp'), may hold values from 0.5 to 1.5
- mlp_gain: bfloat16 [2048], P('dp'), may hold values from 0.5 to 1.5
- w_query: bfloat16 [2048, 2048], P('dp', 'tensor'), may hold values from -0.125 to 0.125
- key_weight: bfloat16 [2048, 256], P('dp', 'tensor'), may hold values from -0.125 to 0.125
- value_weight: bfloat16 [2048, 256], P('dp', 'tensor'), may hold values from -0.125 to 0.125
- w_out: bfloat16 [2048, 2048], P('dp', 'tensor'), may hold values from -0.375 to 0.375
- w_gate: bfloat16 [2048, 5632], P('dp', 'tensor'), may hold values from -0.125 to 0.125
- w_up: bfloat16 [2048, 5632], P('dp', 'tensor'), may hold values from -0.125 to 0.125
- w_down: bfloat16 [2048, 5632], P('dp', 'tensor'), may hold values from -0.078125 to 0.078125
- out_cotangent: bfloat16 [2, 16, 256, 2048], P(None, 'dp', 'tensor'), may hold values from -6 to 6
Outputs:
- block_out: bfloat16 [2, 16, 256, 2048], P(None, 'dp', 'tensor')
- input_grad: float32 [2, 16, 256, 2048], P(None, 'dp', 'tensor')
- attn_gain_grad: float32 [2048], P('dp')
- mlp_gain_grad: float32 [2048], P('dp')
- w_query_grad: float32 [2048, 2048], P('dp', 'tensor')
- w_key_grad: float32 [2048, 256], P('dp', 'tensor')
- w_value_grad: float32 [2048, 256], P('dp', 'tensor')
- w_out_grad: float32 [2048, 2048], P('dp', 'tensor')
- w_gate_grad: float32 [2048, 5632], P('dp', 'tensor')
- w_up_grad: float32 [2048, 5632], P('dp', 'tensor')
- w_down_grad: float32 [2048, 5632], P('dp', 'tensor')
Inputs may be any that keep to these rules, and one draw needn't show every extreme that they name: `segment_ids`: along each group's 256 tokens the ids never fall; every group holds 2 sequences, each of 64 to 192 tokens, together 256.
All inputs are finite; a program needn't handle non-finite values.
Results may differ from a plain program's by a relative error of at most 0.014.
Values may be sent and summed in bfloat16 or wider, within the bound.
No kernel may reach another device: no remote copies, remote signals or barrier semaphores. Data moves between devices by JAX's collectives and lax.ppermute only.
A program may use at most 320 MiB of HBM per device.

v0:
```python
import jax
import jax.numpy as jnp
from jax import lax
from jax.sharding import PartitionSpec as P

HEAD_SIZE = 64


norm_eps = 1e-05


def rotary_tables(segment_row, head_dim):
    length_total = segment_row.shape[0]
    same_seq = segment_row[:, None] == segment_row[None, :]
    row_ids = lax.broadcasted_iota(jnp.int32, (length_total, length_total), 0)
    col_ids = lax.broadcasted_iota(jnp.int32, (length_total, length_total), 1)
    earlier = jnp.logical_and(same_seq, col_ids < row_ids)
    places = jnp.sum(earlier.astype(jnp.float32), axis=1)
    allowed = jnp.logical_and(same_seq, col_ids <= row_ids)
    freq_index = jnp.arange(head_dim // 2, dtype=jnp.float32)
    inverse = 10000.0 ** (-2.0 * freq_index / head_dim)
    angles = places[:, None] * inverse[None, :]
    cosine_table = jnp.concatenate([jnp.cos(angles), jnp.cos(angles)], axis=1)
    sine_table = jnp.concatenate([jnp.sin(angles), jnp.sin(angles)], axis=1)
    return (allowed, cosine_table, sine_table)


def rotate_pairs(values_in, cosine_table, sine_table):
    half_width = values_in.shape[-1] // 2
    turned = jnp.concatenate([-values_in[..., half_width:], values_in[..., :half_width]], axis=-1)
    return values_in * cosine_table[:, None, :] + turned * sine_table[:, None, :]


def rotate_back(grads_in, cosine_table, sine_table):
    half_width = grads_in.shape[-1] // 2
    weighted = grads_in * sine_table[:, None, :]
    turned = jnp.concatenate([weighted[..., half_width:], -weighted[..., :half_width]], axis=-1)
    return grads_in * cosine_table[:, None, :] + turned


def contract_rows(left, right):
    return lax.dot_general(
        left, right, (((0,), (0,)), ((), ())), preferred_element_type=jnp.float32
    )


def contract_cols(left, right):
    return lax.dot_general(
        left, right, (((1,), (1,)), ((), ())), preferred_element_type=jnp.float32
    )


def norm_back(d_normed, unit_rows, gain, scale_rows):
    d_unit = d_normed * gain
    return scale_rows * (d_unit - unit_rows * jnp.mean(d_unit * unit_rows, axis=-1, keepdims=True))


def on_device(
    hidden_in,
    segment_ids,
    attn_gain,
    mlp_gain,
    w_query,
    key_weight,
    value_weight,
    w_out,
    w_gate,
    w_up,
    w_down,
    out_cotangent,
):
    shards = (w_query, key_weight, value_weight, w_out, w_gate, w_up, w_down, attn_gain, mlp_gain)
    micro_count = hidden_in.shape[0]
    score_scale = HEAD_SIZE ** (-0.5)
    block_list = []
    grad_list = []
    totals = None
    whole_run = None
    whole_run = (
        lax.all_gather(shards[0], "dp", axis=0, tiled=True),
        lax.all_gather(shards[1], "dp", axis=0, tiled=True),
        lax.all_gather(shards[2], "dp", axis=0, tiled=True),
        lax.all_gather(shards[3], "dp", axis=0, tiled=True),
        lax.all_gather(shards[4], "dp", axis=0, tiled=True),
        lax.all_gather(shards[5], "dp", axis=0, tiled=True),
        lax.all_gather(shards[6], "dp", axis=0, tiled=True),
        lax.all_gather(shards[7], "dp", axis=0, tiled=True),
        lax.all_gather(shards[8], "dp", axis=0, tiled=True),
    )
    for micro_index in range(micro_count):
        (
            query_full,
            key_full,
            value_full,
            out_full,
            gate_full,
            up_full,
            down_full,
            gain_a,
            gain_m,
        ) = whole_run
        gain_a = gain_a.astype(jnp.float32)
        gain_m = gain_m.astype(jnp.float32)
        row_block = hidden_in[micro_index, 0].astype(jnp.float32)
        allowed, cosine_table, sine_table = rotary_tables(segment_ids[micro_index, 0], HEAD_SIZE)
        scale_a = lax.rsqrt(jnp.mean(row_block * row_block, axis=-1, keepdims=True) + norm_eps)
        unit_a = row_block * scale_a
        attention_normed = (unit_a * gain_a).astype(jnp.bfloat16)
        normed_a_all = lax.all_gather(attention_normed, "tensor", axis=0, tiled=True)
        length_total = normed_a_all.shape[0]
        head_count = query_full.shape[1] // HEAD_SIZE
        kv_count = key_full.shape[1] // HEAD_SIZE
        group_length = head_count // kv_count
        query_linear = jnp.dot(
            normed_a_all, query_full, preferred_element_type=jnp.float32
        ).reshape(length_total, head_count, HEAD_SIZE)
        key_linear = jnp.dot(normed_a_all, key_full, preferred_element_type=jnp.float32).reshape(
            length_total, kv_count, HEAD_SIZE
        )
        value_rows = (
            jnp.dot(normed_a_all, value_full, preferred_element_type=jnp.float32)
            .astype(jnp.bfloat16)
            .reshape(length_total, kv_count, HEAD_SIZE)
        )
        query_rows = (
            rotate_pairs(query_linear, cosine_table, sine_table)
            .astype(jnp.bfloat16)
            .reshape(length_total, kv_count, group_length, HEAD_SIZE)
        )
        keys = rotate_pairs(key_linear, cosine_table, sine_table).astype(jnp.bfloat16)
        scores = (
            jnp.einsum("qkgd,skd->kgqs", query_rows, keys, preferred_element_type=jnp.float32)
            * score_scale
        )
        scores = jnp.where(allowed[None, None], scores, -1e30)
        score_top = jnp.max(scores, axis=-1, keepdims=True)
        exponent = jnp.exp(scores - score_top)
        prob_total = jnp.sum(exponent, axis=-1, keepdims=True)
        probs = exponent / prob_total
        log_total = score_top + jnp.log(prob_total)
        attended = jnp.einsum(
            "kgqs,skd->qkgd",
            probs.astype(jnp.bfloat16),
            value_rows,
            preferred_element_type=jnp.float32,
        )
        attended = attended.reshape(length_total, head_count * HEAD_SIZE).astype(jnp.bfloat16)
        attn_rows = lax.psum_scatter(
            contract_cols(attended, out_full), "tensor", scatter_dimension=0, tiled=True
        )
        mid = row_block + attn_rows
        scale_m = lax.rsqrt(jnp.mean(mid * mid, axis=-1, keepdims=True) + norm_eps)
        unit_m = mid * scale_m
        normed_m = (unit_m * gain_m).astype(jnp.bfloat16)
        normed_m_all = lax.all_gather(normed_m, "tensor", axis=0, tiled=True)
        gate_lin = jnp.dot(normed_m_all, gate_full, preferred_element_type=jnp.float32)
        up_lin = jnp.dot(normed_m_all, up_full, preferred_element_type=jnp.float32)
        gate_sigmoid = jax.nn.sigmoid(gate_lin)
        gate_silu = gate_lin * gate_sigmoid
        inner_act = (gate_silu * up_lin).astype(jnp.bfloat16)
        mlp_rows = lax.psum_scatter(
            contract_cols(inner_act, down_full).astype(jnp.bfloat16),
            "tensor",
            scatter_dimension=0,
            tiled=True,
        ).astype(jnp.float32)
        block_list.append((mid + mlp_rows).astype(jnp.bfloat16))
        cot_rows = out_cotangent[micro_index, 0]
        cot_all = lax.all_gather(cot_rows, "tensor", axis=0, tiled=True)
        d_inner = jnp.dot(cot_all, down_full, preferred_element_type=jnp.float32)
        grad_down = contract_rows(cot_all, inner_act)
        d_gate = (d_inner * up_lin * gate_sigmoid * (1.0 + gate_lin * (1.0 - gate_sigmoid))).astype(
            jnp.bfloat16
        )
        d_up = (d_inner * gate_silu).astype(jnp.bfloat16)
        grad_gate = contract_rows(normed_m_all, d_gate)
        grad_up = contract_rows(normed_m_all, d_up)
        back_mlp = contract_cols(d_gate, gate_full) + contract_cols(d_up, up_full)
        d_normed_m = lax.psum_scatter(back_mlp, "tensor", scatter_dimension=0, tiled=True)
        gain_m_part = jnp.sum(d_normed_m * unit_m, axis=0)
        d_mid = cot_rows.astype(jnp.float32) + norm_back(d_normed_m, unit_m, gain_m, scale_m)
        d_mid_low = d_mid.astype(jnp.bfloat16)
        d_mid_all = lax.all_gather(d_mid_low, "tensor", axis=0, tiled=True)
        d_att = jnp.dot(d_mid_all, out_full, preferred_element_type=jnp.float32).astype(
            jnp.bfloat16
        )
        grad_out = contract_rows(d_mid_all, attended)
        d_att_heads = d_att.reshape(length_total, kv_count, group_length, HEAD_SIZE)
        again_scores = (
            jnp.einsum("qkgd,skd->kgqs", query_rows, keys, preferred_element_type=jnp.float32)
            * score_scale
        )
        again_probs = jnp.exp(jnp.where(allowed[None, None], again_scores, -1e30) - log_total)
        d_probs = jnp.einsum(
            "qkgd,skd->kgqs", d_att_heads, value_rows, preferred_element_type=jnp.float32
        )
        inner_sum = jnp.sum(again_probs * d_probs, axis=-1, keepdims=True)
        d_scores = (again_probs * (d_probs - inner_sum)).astype(jnp.bfloat16)
        d_queries = (
            jnp.einsum("kgqs,skd->qkgd", d_scores, keys, preferred_element_type=jnp.float32)
            * score_scale
        )
        d_keys = (
            jnp.einsum("kgqs,qkgd->skd", d_scores, query_rows, preferred_element_type=jnp.float32)
            * score_scale
        )
        d_values = jnp.einsum(
            "kgqs,qkgd->skd",
            again_probs.astype(jnp.bfloat16),
            d_att_heads,
            preferred_element_type=jnp.float32,
        )
        d_q_lin = (
            rotate_back(
                d_queries.reshape(length_total, head_count, HEAD_SIZE), cosine_table, sine_table
            )
            .reshape(length_total, head_count * HEAD_SIZE)
            .astype(jnp.bfloat16)
        )
        d_k_lin = (
            rotate_back(d_keys, cosine_table, sine_table)
            .reshape(length_total, kv_count * HEAD_SIZE)
            .astype(jnp.bfloat16)
        )
        d_v_lin = d_values.reshape(length_total, kv_count * HEAD_SIZE).astype(jnp.bfloat16)
        grad_query = contract_rows(normed_a_all, d_q_lin)
        grad_key = contract_rows(normed_a_all, d_k_lin)
        grad_value = contract_rows(normed_a_all, d_v_lin)
        back_attn = (
            contract_cols(d_q_lin, query_full)
            + contract_cols(d_k_lin, key_full)
            + contract_cols(d_v_lin, value_full)
        )
        d_normed_a = lax.psum_scatter(
            back_attn.astype(jnp.bfloat16), "tensor", scatter_dimension=0, tiled=True
        ).astype(jnp.float32)
        gain_a_part = jnp.sum(d_normed_a * unit_a, axis=0)
        grad_list.append(d_mid + norm_back(d_normed_a, unit_a, gain_a, scale_a))
        grad_terms = (
            grad_query,
            grad_key,
            grad_value,
            grad_out,
            grad_gate,
            grad_up,
            grad_down,
            gain_a_part,
            gain_m_part,
        )
        if totals is None:
            totals = tuple(grad_terms)
        else:
            totals = tuple(
                (left_sum + right_sum for left_sum, right_sum in zip(totals, grad_terms))
            )
    totals = lax.psum_scatter(totals, "dp", scatter_dimension=0, tiled=True)
    gain_totals = lax.psum((totals[7], totals[8]), "tensor")
    block_out = jnp.stack(block_list, axis=0)[:, None]
    input_grad = jnp.stack(grad_list, axis=0)[:, None]
    return (
        block_out,
        input_grad,
        gain_totals[0],
        gain_totals[1],
        totals[0],
        totals[1],
        totals[2],
        totals[3],
        totals[4],
        totals[5],
        totals[6],
    )


def solution(mesh):
    in_specs = (
        P(None, "dp", "tensor", None),
        P(None, "dp", None),
        P("dp"),
        P("dp"),
        P("dp", "tensor"),
        P("dp", "tensor"),
        P("dp", "tensor"),
        P("dp", "tensor"),
        P("dp", "tensor"),
        P("dp", "tensor"),
        P("dp", "tensor"),
        P(None, "dp", "tensor", None),
    )
    out_specs = (
        P(None, "dp", "tensor", None),
        P(None, "dp", "tensor", None),
        P("dp"),
        P("dp"),
        P("dp", "tensor"),
        P("dp", "tensor"),
        P("dp", "tensor"),
        P("dp", "tensor"),
        P("dp", "tensor"),
        P("dp", "tensor"),
        P("dp", "tensor"),
    )
    return jax.shard_map(
        on_device, mesh=mesh, in_specs=in_specs, out_specs=out_specs, check_vma=False
    )
```

profile of v0, /device:TPU:0, one launch (start us, length us, event | category | flops | bytes accessed | tf_op | source)
XLA Modules:
  0.0 1925.1 jit_solution(16385299962227997949)
XLA Ops:
  7.3 23.3 %all-gather.2 = bf16[16,1,128]{2,1,0:T(2,128)(2,1)S(1)} all-gather(bf16[1,1,128]{2,1,0:T(2,128)(2,1)} %bitcast.333), channel_id=1, replica_groups=mesh['dp'=16,'tensor'=2] {'dp'}, dimensions={0}, use_global_device_ids=true | all-gather | bytes 4352 | tf_op jit(solution)/shard_map/all_gather | solution.py:87
  36.8 18.9 all_gather.53
  55.7 20.8 %all_gather.54 = bf16[2048,128]{1,0:T(8,128)(2,1)S(1)} all-gather(bf16[128,128]{1,0:T(8,128)(2,1)S(1)} %copy-done.77), channel_id=1, replica_groups=mesh['dp'=16,'tensor'=2] {'dp'}, dimensions={0}, use_global_device_ids=true | all-gather | bytes 557056 | tf_op jit(solution)/shard_map/all_gather | solution.py:81
  81.9 25.0 %all-gather.20.cloned.1.call-done = bf16[2048,1024]{1,0:T(8,128)(2,1)} async-done(((bf16[128,1024]{1,0:T(8,128)(2,1)}), bf16[2048,1024]{1,0:T(8,128)(2,1)}) %all-gather.20.cloned.1.call-update) | async-done | bytes 4194320 | tf_op jit(solution)/shard_map/all_gather | solution.py:80
  116.0 42.0 %all-gather.22.cloned.1.call-done = bf16[2048,1024]{1,0:T(8,128)(2,1)} async-done(((bf16[128,1024]{1,0:T(8,128)(2,1)}), bf16[2048,1024]{1,0:T(8,128)(2,1)}) %all-gather.22.cloned.1.call-update) | async-done | bytes 4194320 | tf_op jit(solution)/shard_map/all_gather | solution.py:83
  196.2 21.3 %all-gather.3 = bf16[16,1,128]{2,1,0:T(2,128)(2,1)S(1)} all-gather(bf16[1,1,128]{2,1,0:T(2,128)(2,1)S(1)} %bitcast.334), channel_id=1, replica_groups=mesh['dp'=16,'tensor'=2] {'dp'}, dimensions={0}, use_global_device_ids=true | all-gather | bytes 4352 | tf_op jit(solution)/shard_map/all_gather | solution.py:88
  217.5 30.9 %reduce-scatter.20.cloned.1.call-done = f32[128,2048]{1,0:T(8,128)} async-done(((f32[256,2048]{1,0:T(8,128)}), f32[128,2048]{1,0:T(8,128)}) %reduce-scatter.20.cloned.1.call-update) | async-done | bytes 1048592 | tf_op jit(solution)/shard_map/reduce_scatter | solution.py:148
  273.0 96.3 %all-gather.26.cloned.1.call-done = bf16[2048,2816]{1,0:T(8,128)(2,1)} async-done(((bf16[128,2816]{1,0:T(8,128)(2,1)}), bf16[2048,2816]{1,0:T(8,128)(2,1)}) %all-gather.26.cloned.1.call-update) | async-done | bytes 11534352 | tf_op jit(solution)/shard_map/all_gather | solution.py:84
  378.7 85.2 %all-gather.28.cloned.1.call-done = bf16[2048,2816]{1,0:T(8,128)(2,1)} async-done(((bf16[128,2816]{1,0:T(8,128)(2,1)}), bf16[2048,2816]{1,0:T(8,128)(2,1)}) %all-gather.28.cloned.1.call-update) | async-done | bytes 11534352 | tf_op jit(solution)/shard_map/all_gather | solution.py:85
  485.4 96.3 %all-gather.30.cloned.1.call-done = bf16[2048,2816]{1,0:T(8,128)(2,1)} async-done(((bf16[128,2816]{1,0:T(8,128)(2,1)}), bf16[2048,2816]{1,0:T(8,128)(2,1)}) %all-gather.30.cloned.1.call-update) | async-done | bytes 11534352 | tf_op jit(solution)/shard_map/all_gather | solution.py:86
  609.0 30.0 %reduce-scatter.24.cloned.1.call-done = f32[128,2048]{1,0:T(8,128)} async-done(((f32[256,2048]{1,0:T(8,128)}), f32[128,2048]{1,0:T(8,128)}) %reduce-scatter.24.cloned.1.call-update) | async-done | bytes 1048592 | tf_op jit(solution)/shard_map/reduce_scatter | solution.py:179
  642.6 20.8 %all-gather.34.cloned.1.call-done = bf16[256,2048]{1,0:T(8,128)(2,1)} async-done(((bf16[128,2048]{1,0:T(8,128)(2,1)}), bf16[256,2048]{1,0:T(8,128)(2,1)}) %all-gather.34.cloned.1.call-update) | async-done | bytes 1048592 | tf_op jit(solution)/shard_map/all_gather | solution.py:155
  723.2 22.6 %reduce-scatter.28.cloned.1.call-done = f32[128,2048]{1,0:T(8,128)} async-done(((f32[256,2048]{1,0:T(8,128)}), f32[128,2048]{1,0:T(8,128)}) %reduce-scatter.28.cloned.1.call-update) | async-done | bytes 1048592 | tf_op jit(solution)/shard_map/reduce_scatter | solution.py:179
  747.9 21.0 %reduce-scatter.22.cloned.1.call-done = bf16[128,2048]{1,0:T(8,128)(2,1)} async-done(((bf16[256,2048]{1,0:T(8,128)(2,1)}), bf16[128,2048]{1,0:T(8,128)(2,1)}) %reduce-scatter.22.cloned.1.call-update) | async-done | bytes 524304 | tf_op jit(solution)/shard_map/reduce_scatter | solution.py:161
  772.9 20.8 %all-gather.36.cloned.1.call-done = bf16[256,2048]{1,0:T(8,128)(2,1)} async-done(((bf16[128,2048]{1,0:T(8,128)(2,1)}), bf16[256,2048]{1,0:T(8,128)(2,1)}) %all-gather.36.cloned.1.call-update) | async-done | bytes 1048592 | tf_op jit(solution)/shard_map/all_gather | solution.py:183
  899.0 23.9 %convolution_add_fusion.1 = f32[2048,2816]{1,0:T(8,128)} fusion(f32[2048,2816]{1,0:T(8,128)} %fusion.113, bf16[256,2048]{1,0:T(8,128)(2,1)S(1)} %copy-done.17, bf16[256,2816]{1,0:T(8,128)(2,1)S(1)} %copy-done.41), kind=kOutput, calls=%fused_computation.2 | convolution fusion | flops 2958557184 | bytes 48627712 | tf_op jit(solution)/shard_map/dot_general | solution.py:42
  953.3 66.2 %all-reduce.2 = (f32[2048]{0:T(1024)S(1)}, f32[2048]{0:T(1024)S(1)}) all-reduce(f32[2048]{0:T(1024)S(1)} %add.230, f32[2048]{0:T(1024)S(1)} %add.231), channel_id=12, replica_groups=mesh['dp'=16,'tensor'=2] {'dp'}, use_global_device_ids=true, to_apply=%region_26.27.clone | all-reduce | flops 4096 | bytes 32768
  1030.9 87.5 %reduce-scatter.44.cloned.1.call-done = f32[128,2816]{0,1:T(8,128)} async-done(((f32[2048,2816]{0,1:T(8,128)}), f32[128,2816]{0,1:T(8,128)}) %reduce-scatter.44.cloned.1.call-update) | async-done | bytes 1441808 | tf_op jit(solution)/shard_map/reduce_scatter | solution.py:256
  1121.2 58.1 %reduce-scatter.34.cloned.1.call-done = f32[128,128]{1,0:T(8,128)} async-done(((f32[2048,128]{1,0:T(8,128)}), f32[128,128]{1,0:T(8,128)}) %reduce-scatter.34.cloned.1.call-update) | async-done | bytes 65552 | tf_op jit(solution)/shard_map/reduce_scatter | solution.py:256
  1179.3 60.6 %reduce-scatter.36.cloned.1.call-done = f32[128,128]{1,0:T(8,128)} async-done(((f32[2048,128]{1,0:T(8,128)}), f32[128,128]{1,0:T(8,128)}) %reduce-scatter.36.cloned.1.call-update) | async-done | bytes 65552 | tf_op jit(solution)/shard_map/reduce_scatter | solution.py:256
  1240.0 107.1 %reduce-scatter.32.cloned.1.call-done = f32[128,1024]{1,0:T(8,128)} async-done(((f32[2048,1024]{1,0:T(8,128)}), f32[128,1024]{1,0:T(8,128)}) %reduce-scatter.32.cloned.1.call-update) | async-done | bytes 524304 | tf_op jit(solution)/shard_map/reduce_scatter | solution.py:256
  1347.1 107.6 %reduce-scatter.38.cloned.1.call-done = f32[128,1024]{1,0:T(8,128)} async-done(((f32[2048,1024]{1,0:T(8,128)}), f32[128,1024]{1,0:T(8,128)}) %reduce-scatter.38.cloned.1.call-update) | async-done | bytes 524304 | tf_op jit(solution)/shard_map/reduce_scatter | solution.py:256
  1454.7 231.8 %reduce-scatter.40.cloned.1.call-done = f32[128,2816]{1,0:T(8,128)} async-done(((f32[2048,2816]{1,0:T(8,128)}), f32[128,2816]{1,0:T(8,128)}) %reduce-scatter.40.cloned.1.call-update) | async-done | bytes 1441808 | tf_op jit(solution)/shard_map/reduce_scatter | solution.py:256
  1686.5 231.3 %reduce-scatter.42.cloned.1.call-done = f32[128,2816]{1,0:T(8,128)} async-done(((f32[2048,2816]{1,0:T(8,128)}), f32[128,2816]{1,0:T(8,128)}) %reduce-scatter.42.cloned.1.call-update) | async-done | bytes 1441808 | tf_op jit(solution)/shard_map/reduce_scatter | solution.py:256
  (379 shorter events, 358.8 us)
Async XLA Ops:
  7.2 71.2 %all-gather.18.cloned.1.call-start = ((), (), s32[]{:S(2)}) async-start(), calls=%async_computation.15 | async-start | bytes 1572864 | tf_op jit(solution)/shard_map/all_gather | solution.py:109
  34.6 72.3 %all-gather.20.cloned.1.call-start = ((), (), s32[]{:S(2)}) async-start(), calls=%async_computation.16 | async-start | bytes 4456448 | tf_op jit(solution)/shard_map/all_gather | solution.py:80
  35.4 122.6 %all-gather.22.cloned.1.call-start = ((), (), s32[]{:S(2)}) async-start(), calls=%async_computation.17 | async-start | bytes 4456448 | tf_op jit(solution)/shard_map/all_gather | solution.py:83
  36.1 143.7 %all-gather.32.cloned.1.call-start = ((), (), s32[]{:S(2)}) async-start(), calls=%async_computation.24 | async-start | bytes 1572864 | tf_op jit(solution)/shard_map/all_gather | solution.py:109
  36.7 180.9 %reduce-scatter.16.cloned.1.call-start = ((), (), s32[]{:S(2)}) async-start(), calls=%async_computation.18 | async-start | bytes 3145728 | tf_op jit(solution)/shard_map/reduce_scatter | solution.py:148
  162.9 85.6 %reduce-scatter.20.cloned.1.call-start = ((), (), s32[]{:S(2)}) async-start(), calls=%async_computation.25 | async-start | bytes 3145728 | tf_op jit(solution)/shard_map/reduce_scatter | solution.py:148
  196.1 76.9 %all-gather.24.cloned.1.call-start = ((), (), s32[]{:S(2)}) async-start(), calls=%async_computation.19 | async-start | bytes 1572864 | tf_op jit(solution)/shard_map/all_gather | solution.py:155
  251.6 117.7 %all-gather.26.cloned.1.call-start = ((), (), s32[]{:S(2)}) async-start(), calls=%async_computation.20 | async-start | bytes 12255232 | tf_op jit(solution)/shard_map/all_gather | solution.py:84
  252.3 211.5 %all-gather.28.cloned.1.call-start = ((), (), s32[]{:S(2)}) async-start(), calls=%async_computation.21 | async-start | bytes 12255232 | tf_op jit(solution)/shard_map/all_gather | solution.py:85
  253.1 232.3 %all-gather.40.cloned.1.call-start = ((), (), s32[]{:S(2)}) async-start(), calls=%async_computation.41 | async-start | bytes 1572864 | tf_op jit(solution)/shard_map/all_gather | solution.py:169
  255.4 326.3 %all-gather.30.cloned.1.call-start = ((), (), s32[]{:S(2)}) async-start(), calls=%async_computation.22 | async-start | bytes 12255232 | tf_op jit(solution)/shard_map/all_gather | solution.py:86
  256.1 382.8 %reduce-scatter.24.cloned.1.call-start = ((), (), s32[]{:S(2)}) async-start(), calls=%async_computation.28 | async-start | bytes 3145728 | tf_op jit(solution)/shard_map/reduce_scatter | solution.py:179
  642.6 103.2 %reduce-scatter.28.cloned.1.call-start = ((), (), s32[]{:S(2)}) async-start(), calls=%async_computation.31 | async-start | bytes 3145728 | tf_op jit(solution)/shard_map/reduce_scatter | solution.py:179
  723.1 70.6 %all-gather.36.cloned.1.call-start = ((), (), s32[]{:S(2)}) async-start(), calls=%async_computation.29 | async-start | bytes 1572864 | tf_op jit(solution)/shard_map/all_gather | solution.py:183
  772.9 178.3 %reduce-scatter.26.cloned.1.call-start = ((), (), s32[]{:S(2)}) async-start(), calls=%async_computation.30 | async-start | bytes 1572864 | tf_op jit(solution)/shard_map/reduce_scatter | solution.py:234
  810.0 141.1 %reduce-scatter.30.cloned.1.call-start = ((), (), s32[]{:S(2)}) async-start(), calls=%async_computation.33 | async-start | bytes 1572864 | tf_op jit(solution)/shard_map/reduce_scatter | solution.py:234
  832.8 192.2 %reduce-scatter.18.cloned.1.call-start = ((), (), s32[]{:S(2)}) async-start(), calls=%async_computation.23 | async-start | bytes 1572864 | tf_op jit(solution)/shard_map/reduce_scatter | solution.py:161
  841.4 276.9 %reduce-scatter.44.cloned.1.call-start = ((), (), s32[]{:S(2)}) async-start(), calls=%async_computation.40 | async-start | bytes 24510464 | tf_op jit(solution)/shard_map/reduce_scatter | solution.py:256
  868.0 311.3 %reduce-scatter.34.cloned.1.call-start = ((), (), s32[]{:S(2)}) async-start(), calls=%async_computation.35 | async-start | bytes 1114112 | tf_op jit(solution)/shard_map/reduce_scatter | solution.py:256
  871.2 368.7 %reduce-scatter.36.cloned.1.call-start = ((), (), s32[]{:S(2)}) async-start(), calls=%async_computation.36 | async-start | bytes 1114112 | tf_op jit(solution)/shard_map/reduce_scatter | solution.py:256
  873.3 473.8 %reduce-scatter.32.cloned.1.call-start = ((), (), s32[]{:S(2)}) async-start(), calls=%async_computation.34 | async-start | bytes 8912896 | tf_op jit(solution)/shard_map/reduce_scatter | solution.py:256
  879.3 575.4 %reduce-scatter.38.cloned.1.call-start = ((), (), s32[]{:S(2)}) async-start(), calls=%async_computation.37 | async-start | bytes 8912896 | tf_op jit(solution)/shard_map/reduce_scatter | solution.py:256
  886.6 799.8 %reduce-scatter.40.cloned.1.call-start = ((), (), s32[]{:S(2)}) async-start(), calls=%async_computation.38 | async-start | bytes 24510464 | tf_op jit(solution)/shard_map/reduce_scatter | solution.py:256
  922.9 994.9 %reduce-scatter.42.cloned.1.call-start = ((), (), s32[]{:S(2)}) async-start(), calls=%async_computation.39 | async-start | bytes 24510464 | tf_op jit(solution)/shard_map/reduce_scatter | solution.py:256
  (100 other events, 4128.8 us)
Sparse Core Ops, SparseCore 0:
  55.5 51.3 all-gather.19
  109.1 48.8 all-gather.21
  182.5 31.8 reduce-scatter.15
  216.5 31.8 reduce-scatter.19
  251.7 21.2 all-gather.23
  275.3 93.9 all-gather.25
  371.6 92.2 all-gather.27
  487.7 93.9 all-gather.29
  608.8 30.1 reduce-scatter.23
  642.1 21.2 all-gather.33
  665.4 21.2 all-gather.41
  713.8 31.8 reduce-scatter.27
  748.4 20.3 reduce-scatter.21
  772.4 21.2 all-gather.35
  795.7 21.2 all-gather.37
  819.8 20.3 reduce-scatter.25
  865.6 20.3 reduce-scatter.17
  890.1 228.2 reduce-scatter.43
  1122.5 56.7 reduce-scatter.33
  1183.4 56.5 reduce-scatter.35
  1244.6 102.4 reduce-scatter.31
  1351.6 103.0 reduce-scatter.37
  1459.2 227.1 reduce-scatter.39
  1691.1 226.5 reduce-scatter.41
  (4 shorter events, 78.0 us)
where the time goes:
time: 1930 us
  waiting for transfers between devices  1440 us (75%)
  matrix products  261 us (14%)
  blocking collectives  156 us (8%)
  other arithmetic  31.2 us (2%)
  local copies, waits for them, and re-layouts  21.3 us (1%)
    reduce_scatter x7, waiting for transfers between devices, on_device(): totals = lax.psum_scatter(totals, 'dp', scatter_dimension=0, tiled=True)  884 us
    dot_general x14, matrix products, contract_rows(): lax.dot_general(left, right, (((0,), (0,)), ((), ())), preferred_element_...  102 us
    all_gather x1, waiting for transfers between devices, on_device(): lax.all_gather(shards[6], 'dp', axis=0, tiled=True)  96.3 us
    all_gather x1, waiting for transfers between devices, on_device(): lax.all_gather(shards[4], 'dp', axis=0, tiled=True)  96.3 us
    all_gather x1, waiting for transfers between devices, on_device(): lax.all_gather(shards[5], 'dp', axis=0, tiled=True)  85.2 us
    unnamed x1, blocking collectives  66.2 us
    dot_general x14, matrix products, contract_cols(): lax.dot_general(left, right, (((1,), (1,)), ((), ())), preferred_element_...  63.1 us
    reduce_scatter x2, waiting for transfers between devices, on_device(): lax.psum_scatter(back_mlp, 'tensor', scatter_dimension=0, tiled=True)  52.6 us
  transfers between devices with their start and end apart: 28, of which 23 were waited for; matrix products, arithmetic and copies ran while one was open for 12% of the time, Pallas kernels for 0%

commit v1 on v0

v1 whole, which is shorter than its diff:
```python
import jax
import jax.numpy as jnp
from jax import lax
from jax.sharding import Mesh
from jax.sharding import PartitionSpec as P

HEAD_SIZE = 64
EPS = 1e-05
BF = jnp.bfloat16
F32 = jnp.float32


def swap_x(a):
    return lax.ppermute(a, "x", [(0, 1), (1, 0)])


def swap_y(a):
    return lax.ppermute(a, "y", [(0, 1), (1, 0)])


def swap_c(a):
    return lax.ppermute(a, "c", [(0, 1), (1, 0)])


def swap_z(a, bit):
    n = lax.axis_size("z")
    return lax.ppermute(a, "z", [(i, i ^ bit) for i in range(n)])


def far_bits():
    n = lax.axis_size("z")
    bits = []
    bit = n // 2
    while bit:
        bits.append(bit)
        bit //= 2
    return bits


def z_order():
    order = [0]
    for bit in far_bits():
        order = order + [r ^ bit for r in order]
    return order


def gather_tokens(own):
    half = own.shape[-1] // 2
    from_x = swap_x(own)
    from_y = swap_y(own)
    diag_low = swap_y(from_x[..., :half])
    diag_high = swap_x(from_y[..., half:])
    diag = jnp.concatenate([diag_low, diag_high], axis=-1)
    return jnp.concatenate([own, from_x, from_y, diag], axis=1)


def scatter_tokens(part):
    m, rows, f = part.shape
    half = f // 2
    part = part.reshape(m, 4, rows // 4, f)
    diag = part[:, 3]
    low = swap_y(diag[..., :half])
    high = swap_x(diag[..., half:])
    to_x = part[:, 1]
    to_y = part[:, 2]
    to_x = jnp.concatenate(
        [(to_x[..., :half].astype(F32) + low.astype(F32)).astype(BF), to_x[..., half:]], axis=-1
    )
    to_y = jnp.concatenate(
        [to_y[..., :half], (to_y[..., half:].astype(F32) + high.astype(F32)).astype(BF)], axis=-1
    )
    from_x = swap_x(to_x)
    from_y = swap_y(to_y)
    return part[:, 0].astype(F32) + from_x.astype(F32) + from_y.astype(F32)


def column_part(a, index):
    width = a.shape[1] // 2
    return lax.dynamic_slice_in_dim(a, index * width, width, axis=1)


def gather_rows(mine, from_y, y):
    first = y == 0
    own = jnp.concatenate([jnp.where(first, mine, from_y), jnp.where(first, from_y, mine)], axis=0)
    pieces = [own]
    for bit in far_bits():
        pieces = pieces + [swap_z(p, bit) for p in pieces]
    return pieces + [swap_c(p) for p in pieces]


def reduce_rows(grad):
    half = grad.shape[0] // 2
    got = swap_c(grad[half:])
    grad = grad[:half].astype(F32) + got.astype(F32)
    for bit in reversed(far_bits()):
        half = grad.shape[0] // 2
        got = swap_z(grad[half:].astype(BF), bit)
        grad = grad[:half] + got.astype(F32)
    return grad


def finish_rows(grad, y):
    block = grad.shape[0] // 2
    mine = lax.dynamic_slice_in_dim(grad, y * block, block, axis=0)
    send = lax.dynamic_slice_in_dim(grad, (1 - y) * block, block, axis=0)
    return mine, swap_y(send.astype(BF)).astype(F32)


def join(mine, got, y):
    first = y == 0
    return jnp.concatenate([jnp.where(first, mine, got), jnp.where(first, got, mine)], axis=1)


def rows_rows(left, right):
    return lax.dot_general(left, right, (((0,), (0,)), ((), ())), preferred_element_type=F32)


def cols_cols(left, right):
    return lax.dot_general(left, right, (((1,), (1,)), ((), ())), preferred_element_type=F32)


def rotate(v, cos, sin):
    half = v.shape[-1] // 2
    turned = jnp.concatenate([-v[..., half:], v[..., :half]], axis=-1)
    return v * cos + turned * sin


def rotate_back(v, cos, sin):
    half = v.shape[-1] // 2
    w = v * sin
    turned = jnp.concatenate([w[..., half:], -w[..., :half]], axis=-1)
    return v * cos + turned


def norm_back(d_normed, unit, gain, scale):
    d_unit = d_normed * gain
    return scale * (d_unit - unit * jnp.mean(d_unit * unit, axis=-1, keepdims=True))


def on_device(
    hidden_in,
    segment_ids,
    attn_gain,
    mlp_gain,
    w_query,
    key_weight,
    value_weight,
    w_out,
    w_gate,
    w_up,
    w_down,
    out_cotangent,
):
    z, y, c, x = (lax.axis_index(n) for n in ("z", "y", "c", "x"))
    nz = lax.axis_size("z")
    micro = hidden_in.shape[0]
    toks = hidden_in.shape[2]
    width = hidden_in.shape[3]
    block = w_query.shape[0]
    scale = HEAD_SIZE ** (-0.5)
    order = z_order()
    spots = [
        (((z ^ rz) * 2 + yy) * 2 + (c ^ rc)) for rc in range(2) for rz in order for yy in range(2)
    ]

    def to_rel(a):
        return jnp.concatenate(
            [lax.dynamic_slice_in_dim(a, s * block, block, axis=a.ndim - 1) for s in spots], axis=-1
        )

    where_c = [z * 0 + (cc ^ c) for cc in range(2)]
    rank = jnp.array([order.index(r) for r in range(nz)], jnp.int32)

    def from_rel(a):
        parts = []
        for zz in range(nz):
            for yy in range(2):
                for cc in range(2):
                    spot = ((where_c[cc] * nz) + rank[z ^ zz]) * 2 + yy
                    parts.append(
                        lax.dynamic_slice_in_dim(a, spot * block, block, axis=a.ndim - 1)
                    )
        return jnp.concatenate(parts, axis=-1)

    def pack_attn(index):
        pads = jnp.zeros((16 - 2, block), BF)
        gains = jnp.concatenate([attn_gain[None], mlp_gain[None], pads], axis=0)
        body = jnp.concatenate(
            [
                column_part(w_query, index),
                column_part(key_weight, index),
                column_part(value_weight, index),
                column_part(w_out, index),
            ],
            axis=1,
        )
        gains = jnp.pad(gains, ((0, 0), (0, body.shape[1] - block)))
        return jnp.concatenate([body, gains], axis=0)

    hid = to_rel(hidden_in[:, 0])
    hid_all = gather_tokens(hid)
    other_ids = swap_y(segment_ids[:, 0])

    attn_pieces = gather_rows(pack_attn(y), swap_y(pack_attn(1 - y)), y)
    gu_mine = jnp.concatenate([column_part(w_gate, y), column_part(w_up, y)], axis=1)
    gu_send = jnp.concatenate([column_part(w_gate, 1 - y), column_part(w_up, 1 - y)], axis=1)
    gu_pieces = gather_rows(gu_mine, swap_y(gu_send), y)
    down_pieces = gather_rows(column_part(w_down, y), swap_y(column_part(w_down, 1 - y)), y)

    tall = block + 16
    body = [p[s * tall : s * tall + block] for p in attn_pieces for s in range(2)]
    attn_w = jnp.concatenate(body, axis=0)
    gains = jnp.concatenate(
        [p[s * tall + block : s * tall + block + 2, :block] for p in attn_pieces for s in range(2)],
        axis=1,
    ).astype(F32)
    gain_a, gain_m = gains[0], gains[1]
    q_cols = w_query.shape[1] // 2
    kv_cols = key_weight.shape[1] // 2
    qkv_cols = q_cols + 2 * kv_cols
    qkv_w = attn_w[:, :qkv_cols]
    out_w = attn_w[:, qkv_cols:]
    gu_w = jnp.concatenate(gu_pieces, axis=0)
    down_w = jnp.concatenate(down_pieces, axis=0)
    cot = to_rel(out_cotangent[:, 0])
    cot_all = gather_tokens(cot)

    length = 2 * toks
    groups = micro * 2
    ids = jnp.stack([segment_ids[:, 0], other_ids], axis=1).reshape(groups, length)
    ids = jnp.where(x == 0, ids, jnp.roll(ids, toks, axis=1))
    pos = (jnp.arange(length, dtype=jnp.int32) + toks * x) % length
    same = ids[:, :, None] == ids[:, None, :]
    allowed = jnp.logical_and(same, (pos[None, :] <= pos[:, None])[None])
    places = jnp.sum(allowed.astype(F32), axis=2) - 1.0
    freq = jnp.arange(HEAD_SIZE // 2, dtype=F32)
    inverse = 10000.0 ** (-2.0 * freq / HEAD_SIZE)
    angles = places[:, :, None] * inverse
    cos = jnp.concatenate([jnp.cos(angles)] * 2, axis=-1)
    sin = jnp.concatenate([jnp.sin(angles)] * 2, axis=-1)

    rows = micro * 4 * toks
    hid32 = hid_all.astype(F32).reshape(rows, width)
    scale_a = lax.rsqrt(jnp.mean(hid32 * hid32, axis=-1, keepdims=True) + EPS)
    unit_a_all = hid32 * scale_a
    normed_a = (unit_a_all * gain_a).astype(BF)
    qkv = jnp.dot(normed_a, qkv_w, preferred_element_type=F32)
    heads = q_cols // HEAD_SIZE
    q_lin = qkv[:, :q_cols].reshape(groups, length, heads, HEAD_SIZE)
    k_lin = qkv[:, q_cols : q_cols + kv_cols].reshape(groups, length, HEAD_SIZE)
    values = qkv[:, q_cols + kv_cols :].astype(BF).reshape(groups, length, HEAD_SIZE)
    queries = rotate(q_lin, cos[:, :, None], sin[:, :, None]).astype(BF)
    keys = rotate(k_lin, cos, sin).astype(BF)
    scores = jnp.einsum("gqhd,gsd->ghqs", queries, keys, preferred_element_type=F32) * scale
    scores = jnp.where(allowed[:, None], scores, -1e30)
    top = jnp.max(scores, axis=-1, keepdims=True)
    expo = jnp.exp(scores - top)
    probs = expo / jnp.sum(expo, axis=-1, keepdims=True)
    attended = jnp.einsum("ghqs,gsd->gqhd", probs.astype(BF), values, preferred_element_type=F32)
    attended = attended.reshape(rows, q_cols).astype(BF)
    attn_part = cols_cols(attended, out_w).astype(BF).reshape(micro, 4 * toks, width)
    mid = hid.astype(F32) + scatter_tokens(attn_part)

    scale_m = lax.rsqrt(jnp.mean(mid * mid, axis=-1, keepdims=True) + EPS)
    unit_m = mid * scale_m
    normed_m = gather_tokens((unit_m * gain_m).astype(BF)).reshape(rows, width)
    gu = jnp.dot(normed_m, gu_w, preferred_element_type=F32)
    ff = gu.shape[1] // 2
    gate, up = gu[:, :ff], gu[:, ff:]
    sig = jax.nn.sigmoid(gate)
    silu = gate * sig
    inner = (silu * up).astype(BF)
    cot_rows = cot_all.reshape(rows, width)
    g_down = rows_rows(cot_rows, inner).astype(BF)
    g_down = reduce_rows(g_down)
    d_inner = jnp.dot(cot_rows, down_w, preferred_element_type=F32)
    d_gate = (d_inner * up * sig * (1.0 + gate * (1.0 - sig))).astype(BF)
    d_up = (d_inner * silu).astype(BF)
    d_gu = jnp.concatenate([d_gate, d_up], axis=1)
    back_mlp = cols_cols(d_gu, gu_w).astype(BF).reshape(micro, 4 * toks, width)
    d_normed_m = scatter_tokens(back_mlp)
    g_gu = reduce_rows(rows_rows(normed_m, d_gu).astype(BF))
    mlp_part = cols_cols(inner, down_w).astype(BF).reshape(micro, 4 * toks, width)
    block_out = (mid + scatter_tokens(mlp_part)).astype(BF)
    gain_m_part = jnp.sum(d_normed_m * unit_m, axis=(0, 1))
    d_mid = cot.astype(F32) + norm_back(d_normed_m, unit_m, gain_m, scale_m)

    d_mid_all = gather_tokens(d_mid.astype(BF)).reshape(rows, width)
    d_att = jnp.dot(d_mid_all, out_w, preferred_element_type=F32).astype(BF)
    g_out = rows_rows(d_mid_all, attended).astype(BF)
    d_att = d_att.reshape(groups, length, heads, HEAD_SIZE)
    d_probs = jnp.einsum("gqhd,gsd->ghqs", d_att, values, preferred_element_type=F32)
    inner_sum = jnp.sum(probs * d_probs, axis=-1, keepdims=True)
    d_scores = (probs * (d_probs - inner_sum)).astype(BF)
    d_queries = jnp.einsum("ghqs,gsd->gqhd", d_scores, keys, preferred_element_type=F32) * scale
    d_keys = jnp.einsum("ghqs,gqhd->gsd", d_scores, queries, preferred_element_type=F32) * scale
    d_values = jnp.einsum("ghqs,gqhd->gsd", probs.astype(BF), d_att, preferred_element_type=F32)
    d_q = rotate_back(d_queries, cos[:, :, None], sin[:, :, None]).reshape(rows, q_cols)
    d_k = rotate_back(d_keys, cos, sin).reshape(rows, kv_cols)
    d_v = d_values.reshape(rows, kv_cols)
    d_qkv = jnp.concatenate([d_q, d_k, d_v], axis=1).astype(BF)
    back_attn = cols_cols(d_qkv, qkv_w)
    gain_a_part = jnp.sum(back_attn * unit_a_all, axis=0)
    g_qkv = rows_rows(normed_a, d_qkv).astype(BF)

    g_out = reduce_rows(g_out)
    g_qkv = reduce_rows(g_qkv)
    d_normed_a = scatter_tokens(back_attn.astype(BF).reshape(micro, 4 * toks, width))
    unit_a = unit_a_all.reshape(micro, 4 * toks, width)[:, :toks]
    sc_a = scale_a.reshape(micro, 4 * toks, 1)[:, :toks]
    input_grad = d_mid + norm_back(d_normed_a, unit_a, gain_a, sc_a)

    gain_parts = jnp.stack([gain_a_part, gain_m_part]).reshape(2, 2 * nz, 2 * block)
    gain_parts = gain_parts.transpose(1, 0, 2).reshape(2 * nz * 2, 2 * block)
    half = gain_parts.shape[0] // 2
    gsum = gain_parts[:half] + swap_c(gain_parts[half:])
    for bit in reversed(far_bits()):
        half = gsum.shape[0] // 2
        gsum = gsum[:half] + swap_z(gsum[half:], bit)
    gsum = gsum.reshape(2, 2, block)
    keep = lax.dynamic_slice_in_dim(gsum, y, 1, axis=1)[:, 0]
    give = lax.dynamic_slice_in_dim(gsum, 1 - y, 1, axis=1)[:, 0]
    keep = keep + swap_y(give)
    keep = keep + swap_x(keep)

    down_m, down_r = finish_rows(g_down, y)
    gu_m, gu_r = finish_rows(g_gu, y)
    out_m, out_r = finish_rows(g_out, y)
    qkv_m, qkv_r = finish_rows(g_qkv, y)

    def cut(lo, hi):
        return join(qkv_m[:, lo:hi], qkv_r[:, lo:hi], y)

    return (
        from_rel(block_out)[:, None],
        from_rel(input_grad)[:, None],
        keep[0],
        keep[1],
        cut(0, q_cols),
        cut(q_cols, q_cols + kv_cols),
        cut(q_cols + kv_cols, qkv_cols),
        join(out_m, out_r, y),
        join(gu_m[:, :ff], gu_r[:, :ff], y),
        join(gu_m[:, ff:], gu_r[:, ff:], y),
        join(down_m, down_r, y),
    )


def solution(mesh):
    n_dp, n_tensor = mesh.shape["dp"], mesh.shape["tensor"]
    grid = Mesh(mesh.devices.reshape(n_dp // 4, 2, 2, n_tensor), ("z", "y", "c", "x"))
    dp = ("z", "y", "c")
    token = P(None, dp, "x", None)
    weight = P(dp, "x")
    gain = P(dp)
    in_specs = (token, P(None, dp, None), gain, gain) + (weight,) * 7 + (token,)
    out_specs = (token, token, gain, gain) + (weight,) * 7
    return jax.shard_map(
        on_device, mesh=grid, in_specs=in_specs, out_specs=out_specs, check_vma=False
    )
```

time: 1930 us -> 867 us (0.45)
  waiting for transfers between devices: 1440 us -> 430 us
  blocking collectives: 156 us -> 0 us
  matrix products: 261 us -> 139 us
  local copies, waits for them, and re-layouts: 21.3 us -> 125 us
  starting transfers between devices: 3.03 us -> 79.3 us
  other arithmetic: 31.2 us -> 78.2 us
    reduce_scatter x15 -> x0, waiting for transfers between devices: 989 us -> none  [the longest x7 884 us: on_device(): totals = lax.psum_scatter(totals, 'dp', scatter_dimension=0, tiled=True)]
    all_gather x13 -> x0, waiting for transfers between devices: 442 us -> none  [the longest x1 96.3 us: on_device(): lax.all_gather(shards[6], 'dp', axis=0, tiled=True)]
    ppermute x0 -> x78, waiting for transfers between devices: none -> 430 us  [the longest x19 260 us: swap_z(): return lax.ppermute(a, 'z', [(i, i ^ bit) for i in range(n)])]
    dot_general x54 -> x17, matrix products: 261 us -> 132 us  [the longest x4 45.9 us: cols_cols(): lax.dot_general(left, right, (((1,), (1,)), ((), ())), preferred_element_...]
    all_gather x4 -> x0, blocking collectives: 84.4 us -> none  [the longest x1 23.3 us: on_device(): lax.all_gather(shards[7], 'dp', axis=0, tiled=True)]
    ppermute x0 -> x78, starting transfers between devices: none -> 79.3 us  [the longest x19 30 us: swap_z(): return lax.ppermute(a, 'z', [(i, i ^ bit) for i in range(n)])]
    unnamed x1 -> x0, blocking collectives: 66.2 us -> none
    unnamed x196 -> x269, local copies, waits for them, and re-layouts: 18.7 us -> 75.6 us
  transfers between devices with their start and end apart: 28 -> 78, of which waited for: 23 -> 36; matrix products, arithmetic and copies ran while one was open for 12% -> 28% of each run, Pallas kernels for 0% -> 0%
where the time goes in v1:
time: 867 us; the launch traced here: 860 us
  waiting for transfers between devices  430 us (50%)
  matrix products  139 us (16%)
  local copies, waits for them, and re-layouts  125 us (14%)
  starting transfers between devices  79.3 us (9%)
  other arithmetic  78.2 us (9%)
    ppermute x19, waiting for transfers between devices, swap_z(): return lax.ppermute(a, 'z', [(i, i ^ bit) for i in range(n)])  260 us
    ppermute x25, waiting for transfers between devices, swap_y(): return lax.ppermute(a, 'y', [(0, 1), (1, 0)])  130 us
    unnamed x269, local copies, waits for them, and re-layouts  75.6 us
    dot_general x4, matrix products, cols_cols(): lax.dot_general(left, right, (((1,), (1,)), ((), ())), preferred_element_...  45.9 us
    ppermute x17, waiting for transfers between devices, swap_x(): return lax.ppermute(a, 'x', [(0, 1), (1, 0)])  36.8 us
    dot_general x4, matrix products, rows_rows(): lax.dot_general(left, right, (((0,), (0,)), ((), ())), preferred_element_...  36.4 us
    ppermute x19, starting transfers between devices, swap_z(): return lax.ppermute(a, 'z', [(i, i ^ bit) for i in range(n)])  30 us
    ppermute x25, starting transfers between devices, swap_y(): return lax.ppermute(a, 'y', [(0, 1), (1, 0)])  29.4 us
  transfers between devices with their start and end apart: 78, of which 36 were waited for; matrix products, arithmetic and copies ran while one was open for 28% of the time, Pallas kernels for 0%

profile of v1, /device:TPU:0, one launch (start us, length us, event | category | flops | bytes accessed | tf_op | source)
XLA Modules:
  0.0 860.1 jit_solution(15941260214561330302)
XLA Ops:
  85.7 13.1 %collective-permute-done.21 = bf16[128,2816]{1,0:T(8,128)(2,1)S(1)} collective-permute-done((bf16[128,2816]{1,0:T(8,128)(2,1)S(1)}, bf16[128,2816]{1,0:T(8,128)(2,1)S(1)}, u32[]{:S(2)}, u32[]{:S(2)}) %collective-permute-start.21) | collective-permute-done | bytes 720928 | tf_op jit(solution)/shard_map/ppermute | solution.py:18
  104.6 22.0 %collective-permute-done.5 = bf16[288,1152]{1,0:T(8,128)(2,1)S(1)} collective-permute-done((bf16[288,1152]{1,0:T(8,128)(2,1)S(1)}, bf16[288,1152]{1,0:T(8,128)(2,1)S(1)}, u32[]{:S(2)}, u32[]{:S(2)}) %collective-permute-start.5) | collective-permute-done | bytes 663584 | tf_op jit(solution)/shard_map/ppermute | solution.py:27
  127.3 15.1 %collective-permute-done.6 = bf16[288,1152]{1,0:T(8,128)(2,1)S(1)} collective-permute-done((bf16[288,1152]{1,0:T(8,128)(2,1)S(1)}, bf16[288,1152]{1,0:T(8,128)(2,1)S(1)}, u32[]{:S(2)}, u32[]{:S(2)}) %collective-permute-start.6) | collective-permute-done | bytes 663584 | tf_op jit(solution)/shard_map/ppermute | solution.py:27
  151.2 26.1 %collective-permute-done.30 = bf16[256,1408]{1,0:T(8,128)(2,1)} collective-permute-done((bf16[256,1408]{1,0:T(8,128)(2,1)}, bf16[256,1408]{1,0:T(8,128)(2,1)}, u32[]{:S(2)}, u32[]{:S(2)}) %collective-permute-start.30) | collective-permute-done | bytes 720928 | tf_op jit(solution)/shard_map/ppermute | solution.py:27
  237.7 37.9 %collective-permute-done.32 = bf16[256,1408]{1,0:T(8,128)(2,1)} collective-permute-done((bf16[256,1408]{1,0:T(8,128)(2,1)}, bf16[256,1408]{1,0:T(8,128)(2,1)}, u32[]{:S(2)}, u32[]{:S(2)}) %collective-permute-start.32) | collective-permute-done | bytes 720928 | tf_op jit(solution)/shard_map/ppermute | solution.py:27
  302.4 16.4 %collective-permute-done.24 = bf16[256,2816]{1,0:T(8,128)(2,1)S(1)} collective-permute-done((bf16[256,2816]{1,0:T(8,128)(2,1)}, bf16[256,2816]{1,0:T(8,128)(2,1)S(1)}, u32[]{:S(2)}, u32[]{:S(2)}) %collective-permute-start.24) | collective-permute-done | bytes 1441824 | tf_op jit(solution)/shard_map/ppermute | solution.py:27
  324.3 21.7 %collective-permute-done.18 = bf16[2,128,2048]{2,1,0:T(8,128)(2,1)S(1)} collective-permute-done((bf16[2,128,2048]{2,1,0:T(8,128)(2,1)S(1)}, bf16[2,128,2048]{2,1,0:T(8,128)(2,1)S(1)}, u32[]{:S(2)}, u32[]{:S(2)}) %collective-permute-start.18) | collective-permute-done | bytes 1048608 | tf_op jit(solution)/shard_map/ppermute | solution.py:18
  349.0 10.0 %collective-permute-done.20 = bf16[2,128,1024]{2,1,0:T(8,128)(2,1)S(1)} collective-permute-done((bf16[2,128,1024]{2,1,0:T(8,128)(2,1)S(1)}, bf16[2,128,1024]{2,1,0:T(8,128)(2,1)S(1)}, u32[]{:S(2)}, u32[]{:S(2)}) %collective-permute-start.20) | collective-permute-done | bytes 524320 | tf_op jit(solution)/shard_map/ppermute | solution.py:14
  361.3 14.9 %fusion.85 = f32[1024,2816]{1,0:T(8,128)} fusion(bf16[1024,2048]{1,0:T(8,128)(2,1)S(1)} %bitcast.314, bf16[2048,2816]{1,0:T(8,128)(2,1)S(1)} %constant_dynamic-update-slice_fusion.32), kind=kOutput, calls=%fused_computation.370 | convolution fusion | flops 11811160064 | bytes 27262976 | tf_op jit(solution)/shard_map/dot_general | solution.py:267
  376.2 15.1 %multiply_convert_fusion.2 = (bf16[1024,1408]{1,0:T(8,128)(2,1)}, bf16[1024,1408]{1,0:T(8,128)(2,1)}, bf16[1024,1408]{1,0:T(8,128)(2,1)}) fusion(f32[1024,2816]{1,0:T(8,128)} %fusion.85, bf16[1024,2048]{1,0:T(8,128)(2,1)S(1)} %bitcast.308, bf16[2048,1408]{1,0:T(8,128)(2,1)} %constant_dynamic-update-slice_fusion.41), kind=kOutput, calls=%fused_computation.21 | convolution fusion | flops 5927206912 | bytes 30146560 | tf_op jit(solution)/shard_map/dot_general | solution.py:276
  391.3 16.7 %convolution_convert_fusion.2 = bf16[1024,2048]{1,0:T(8,128)(2,1)S(1)} fusion(bf16[2048,2816]{1,0:T(8,128)(2,1)} %copy-done.51, bf16[1024,1408]{1,0:T(8,128)(2,1)} %get-tuple-element.48, bf16[1024,1408]{1,0:T(8,128)(2,1)} %get-tuple-element.47), kind=kOutput, calls=%fused_computation.33 | convolution fusion | flops 11824791552 | bytes 21495808 | tf_op jit(solution)/shard_map/dot_general | solution.py:119
  408.0 17.6 %convolution_convert_fusion = bf16[2048,2816]{1,0:T(8,128)(2,1)} fusion(bf16[1024,2048]{1,0:T(8,128)(2,1)S(1)} %bitcast.315, bf16[1024,1408]{1,0:T(8,128)(2,1)} %get-tuple-element.48, bf16[1024,1408]{1,0:T(8,128)(2,1)} %get-tuple-element.47), kind=kOutput, calls=%fused_computation.2 | convolution fusion | flops 11828461568 | bytes 21495808 | tf_op jit(solution)/shard_map/dot_general | solution.py:115
  427.7 8.7 %convolution_convert_fusion.3 = bf16[1024,2048]{1,0:T(8,128)(2,1)S(1)} fusion(bf16[1024,1408]{1,0:T(8,128)(2,1)S(1)} %copy-done.65, bf16[2048,1408]{1,0:T(8,128)(2,1)} %constant_dynamic-update-slice_fusion.41), kind=kOutput, calls=%fused_computation.34 | convolution fusion | flops 5907677184 | bytes 12845056 | tf_op jit(solution)/shard_map/dot_general | solution.py:119
  443.8 8.1 collective-permute-done.39
  476.0 18.3 %collective-permute-done.40 = bf16[2,128,2048]{2,1,0:T(8,128)(2,1)} collective-permute-done((bf16[2,128,2048]{2,1,0:T(8,128)(2,1)}, bf16[2,128,2048]{2,1,0:T(8,128)(2,1)}, u32[]{:S(2)}, u32[]{:S(2)}) %collective-permute-start.40) | collective-permute-done | bytes 1048608 | tf_op jit(solution)/shard_map/ppermute | solution.py:18
  501.5 20.0 %collective-permute-done.50 = bf16[2,128,2048]{2,1,0:T(8,128)(2,1)S(1)} collective-permute-done((bf16[2,128,2048]{2,1,0:T(8,128)(2,1)S(1)}, bf16[2,128,2048]{2,1,0:T(8,128)(2,1)S(1)}, u32[]{:S(2)}, u32[]{:S(2)}) %collective-permute-start.50) | collective-permute-done | bytes 1048608 | tf_op jit(solution)/shard_map/ppermute | solution.py:18
  560.3 16.1 %multiply_reduce_fusion = (f32[2048]{0:T(1024)S(1)}, bf16[1024,2048]{1,0:T(8,128)(2,1)}) fusion(f32[1024]{0:T(1024)S(1)} %bitcast.340, bf16[2,128,1024]{2,1,0:T(8,128)(2,1)S(1)} %copy-done.17, bf16[2,128,1024]{2,1,0:T(8,128)(2,1)S(1)} %copy-done.19, bf16[2,128,2048]{2,1,0:T(8,128)(2,1)S(1)} %copy-done.6, bf16[2,128,2048]{2,1,0:T(8,128)(2,1)S(1)} %copy-done.8, ...), kind=kOutput, calls=%fused_computation.10 | convolution fusion | flops 2713712640 | bytes 12333056 | tf_op jit(solution)/shard_map/dot_general | solution.py:119
  592.4 25.5 %collective-permute-done.58 = f32[4,256]{1,0:T(4,128)S(1)} collective-permute-done((f32[4,256]{1,0:T(4,128)S(1)}, f32[4,256]{1,0:T(4,128)S(1)}, u32[]{:S(2)}, u32[]{:S(2)}) %collective-permute-start.58) | collective-permute-done | bytes 4128 | tf_op jit(solution)/shard_map/ppermute | solution.py:27
  656.2 9.6 %collective-permute-done.56 = bf16[2,128,2048]{2,1,0:T(8,128)(2,1)S(1)} collective-permute-done((bf16[2,128,2048]{2,1,0:T(8,128)(2,1)S(1)}, bf16[2,128,2048]{2,1,0:T(8,128)(2,1)S(1)}, u32[]{:S(2)}, u32[]{:S(2)}) %collective-permute-start.56) | collective-permute-done | bytes 1048608 | tf_op jit(solution)/shard_map/ppermute | solution.py:18
  672.8 9.8 %convert_add_fusion = f32[1024,2816]{1,0:T(8,128)} fusion(bf16[1024,2816]{1,0:T(8,128)(2,1)} %collective-permute-done.70, bf16[2048,2816]{1,0:T(8,128)(2,1)} %convolution_convert_fusion), kind=kLoop, calls=%fused_computation.1 | loop fusion | flops 8650752 | bytes 23068672 | tf_op jit(solution)/shard_map/add | solution.py:94
  696.5 56.4 %collective-permute-done.68 = bf16[256,512]{0,1:T(8,128)(2,1)S(1)} collective-permute-done((bf16[256,512]{0,1:T(8,128)(2,1)S(1)}, bf16[256,512]{0,1:T(8,128)(2,1)S(1)}, u32[]{:S(2)}, u32[]{:S(2)}) %collective-permute-start.68) | collective-permute-done | bytes 262176 | tf_op jit(solution)/shard_map/ppermute | solution.py:27
  771.4 35.6 %collective-permute-done.64 = bf16[256,640]{0,1:T(8,128)(2,1)} collective-permute-done((bf16[256,640]{0,1:T(8,128)(2,1)}, bf16[256,640]{0,1:T(8,128)(2,1)}, u32[]{:S(2)}, u32[]{:S(2)}) %collective-permute-start.64) | collective-permute-done | bytes 327712 | tf_op jit(solution)/shard_map/ppermute | solution.py:27
  813.7 21.9 %collective-permute-done.72 = bf16[256,2816]{1,0:T(8,128)(2,1)} collective-permute-done((bf16[256,2816]{1,0:T(8,128)(2,1)}, bf16[256,2816]{1,0:T(8,128)(2,1)}, u32[]{:S(2)}, u32[]{:S(2)}) %collective-permute-start.72) | collective-permute-done | bytes 1441824 | tf_op jit(solution)/shard_map/ppermute | solution.py:27
  843.8 12.3 %collective-permute-done.73 = bf16[128,2816]{1,0:T(8,128)(2,1)} collective-permute-done((bf16[128,2816]{1,0:T(8,128)(2,1)}, bf16[128,2816]{1,0:T(8,128)(2,1)}, u32[]{:S(2)}, u32[]{:S(2)}) %collective-permute-start.73) | collective-permute-done | bytes 720928 | tf_op jit(solution)/shard_map/ppermute | solution.py:18
  (603 shorter events, 382.9 us)
Async XLA Ops:
  15.5 130.4 %collective-permute-start.1 = (bf16[2,128,2048]{2,1,0:T(8,128)(2,1)S(1)}, bf16[2,128,2048]{2,1,0:T(8,128)(2,1)S(1)}, u32[]{:S(2)}, u32[]{:S(2)}) collective-permute-start(bf16[2,128,2048]{2,1,0:T(8,128)(2,1)S(1)} %constant_dynamic-update-slice_fusion), channel_id=1, source_target_pairs={{0,4},{4,0},{1,5},{5,1},{2,6},{6,2},{3,7},{7,3},{8,12},{12,8},{9,1... | collective-permute-start | bytes 3145736 | tf_op jit(solution)/shard_map/ppermute | solution.py:18
  18.5 129.2 %collective-permute-start = (bf16[2,128,2048]{2,1,0:T(8,128)(2,1)S(1)}, bf16[2,128,2048]{2,1,0:T(8,128)(2,1)S(1)}, u32[]{:S(2)}, u32[]{:S(2)}) collective-permute-start(bf16[2,128,2048]{2,1,0:T(8,128)(2,1)S(1)} %constant_dynamic-update-slice_fusion), channel_id=1, source_target_pairs={{0,1},{1,0},{2,3},{3,2},{4,5},{5,4},{6,7},{7,6},{8,9},{9,8},{10,11... | collective-permute-start | bytes 3145736 | tf_op jit(solution)/shard_map/ppermute | solution.py:14
  42.1 106.3 %collective-permute-start.42 = (bf16[2,128,2048]{2,1,0:T(8,128)(2,1)}, bf16[2,128,2048]{2,1,0:T(8,128)(2,1)}, u32[]{:S(2)}, u32[]{:S(2)}) collective-permute-start(bf16[2,128,2048]{2,1,0:T(8,128)(2,1)} %constant_dynamic-update-slice_fusion.66), channel_id=1, source_target_pairs={{0,4},{4,0},{1,5},{5,1},{2,6},{6,2},{3,7},{7,3},{8,12},{12,8},{9,1... | collective-permute-start | bytes 3145736 | tf_op jit(solution)/shard_map/ppermute | solution.py:18
  42.6 107.4 %collective-permute-start.41 = (bf16[2,128,2048]{2,1,0:T(8,128)(2,1)}, bf16[2,128,2048]{2,1,0:T(8,128)(2,1)}, u32[]{:S(2)}, u32[]{:S(2)}) collective-permute-start(bf16[2,128,2048]{2,1,0:T(8,128)(2,1)} %constant_dynamic-update-slice_fusion.66), channel_id=1, source_target_pairs={{0,1},{1,0},{2,3},{3,2},{4,5},{5,4},{6,7},{7,6},{8,9},{9,8},{10,11... | collective-permute-start | bytes 3145736 | tf_op jit(solution)/shard_map/ppermute | solution.py:14
  142.4 34.9 %collective-permute-start.30 = (bf16[256,1408]{1,0:T(8,128)(2,1)}, bf16[256,1408]{1,0:T(8,128)(2,1)}, u32[]{:S(2)}, u32[]{:S(2)}) collective-permute-start(bf16[256,1408]{1,0:T(8,128)(2,1)} %pad_maximum_fusion.17), channel_id=1, source_target_pairs={{0,16},{8,24},{16,0},{24,8},{1,17},{9,25},{17,1},{25,9},{2,18},{10... | collective-permute-start | bytes 2162696 | tf_op jit(solution)/shard_map/ppermute | solution.py:27
  150.1 50.8 %collective-permute-start.8 = (bf16[288,1152]{1,0:T(8,128)(2,1)S(1)}, bf16[288,1152]{1,0:T(8,128)(2,1)S(1)}, u32[]{:S(2)}, u32[]{:S(2)}) collective-permute-start(bf16[288,1152]{1,0:T(8,128)(2,1)S(1)} %pad_maximum_fusion.18), channel_id=1, source_target_pairs={{0,2},{2,0},{1,3},{3,1},{4,6},{6,4},{5,7},{7,5},{8,10},{10,8},{9,1... | collective-permute-start | bytes 1990664 | tf_op jit(solution)/shard_map/ppermute | solution.py:22
  177.3 100.9 %collective-permute-start.33 = (bf16[256,1408]{1,0:T(8,128)(2,1)}, bf16[256,1408]{1,0:T(8,128)(2,1)}, u32[]{:S(2)}, u32[]{:S(2)}) collective-permute-start(bf16[256,1408]{1,0:T(8,128)(2,1)} %pad_maximum_fusion.17), channel_id=1, source_target_pairs={{0,2},{2,0},{1,3},{3,1},{4,6},{6,4},{5,7},{7,5},{8,10},{10,8},{9,1... | collective-permute-start | bytes 2162696 | tf_op jit(solution)/shard_map/ppermute | solution.py:22
  193.5 89.4 %collective-permute-start.22 = (bf16[256,2816]{1,0:T(8,128)(2,1)}, bf16[256,2816]{1,0:T(8,128)(2,1)}, u32[]{:S(2)}, u32[]{:S(2)}) collective-permute-start(bf16[256,2816]{1,0:T(8,128)(2,1)} %pad_maximum_fusion.3), channel_id=1, source_target_pairs={{0,16},{8,24},{16,0},{24,8},{1,17},{9,25},{17,1},{25,9},{2,18},{10... | collective-permute-start | bytes 4325384 | tf_op jit(solution)/shard_map/ppermute | solution.py:27
  196.9 102.5 %collective-permute-start.23 = (bf16[256,2816]{1,0:T(8,128)(2,1)}, bf16[256,2816]{1,0:T(8,128)(2,1)}, u32[]{:S(2)}, u32[]{:S(2)}) collective-permute-start(bf16[256,2816]{1,0:T(8,128)(2,1)} %pad_maximum_fusion.3), channel_id=1, source_target_pairs={{0,8},{8,0},{16,24},{24,16},{1,9},{9,1},{17,25},{25,17},{2,10},{10... | collective-permute-start | bytes 4325384 | tf_op jit(solution)/shard_map/ppermute | solution.py:27
  202.9 72.8 %collective-permute-start.32 = (bf16[256,1408]{1,0:T(8,128)(2,1)}, bf16[256,1408]{1,0:T(8,128)(2,1)}, u32[]{:S(2)}, u32[]{:S(2)}) collective-permute-start(bf16[256,1408]{1,0:T(8,128)(2,1)} %collective-permute-done.30), channel_id=1, source_target_pairs={{0,8},{8,0},{16,24},{24,16},{1,9},{9,1},{17,25},{25,17},{2,10},{10... | collective-permute-start | bytes 2162696 | tf_op jit(solution)/shard_map/ppermute | solution.py:27
  206.7 73.5 %collective-permute-start.34 = (bf16[256,1408]{1,0:T(8,128)(2,1)}, bf16[256,1408]{1,0:T(8,128)(2,1)}, u32[]{:S(2)}, u32[]{:S(2)}) collective-permute-start(bf16[256,1408]{1,0:T(8,128)(2,1)} %collective-permute-done.30), channel_id=1, source_target_pairs={{0,2},{2,0},{1,3},{3,1},{4,6},{6,4},{5,7},{7,5},{8,10},{10,8},{9,1... | collective-permute-start | bytes 2162696 | tf_op jit(solution)/shard_map/ppermute | solution.py:22
  440.9 34.3 %collective-permute-start.48 = (bf16[2,128,2048]{2,1,0:T(8,128)(2,1)}, bf16[2,128,2048]{2,1,0:T(8,128)(2,1)S(1)}, u32[]{:S(2)}, u32[]{:S(2)}) collective-permute-start(bf16[2,128,2048]{2,1,0:T(8,128)(2,1)} %pad_maximum_fusion.12), channel_id=1, source_target_pairs={{0,4},{4,0},{1,5},{5,1},{2,6},{6,2},{3,7},{7,3},{8,12},{12,8},{9,1... | collective-permute-start | bytes 3145736 | tf_op jit(solution)/shard_map/ppermute | solution.py:18
  453.1 41.3 %collective-permute-start.40 = (bf16[2,128,2048]{2,1,0:T(8,128)(2,1)}, bf16[2,128,2048]{2,1,0:T(8,128)(2,1)}, u32[]{:S(2)}, u32[]{:S(2)}) collective-permute-start(bf16[2,128,2048]{2,1,0:T(8,128)(2,1)} %pad_maximum_fusion.10), channel_id=1, source_target_pairs={{0,4},{4,0},{1,5},{5,1},{2,6},{6,2},{3,7},{7,3},{8,12},{12,8},{9,1... | collective-permute-start | bytes 3145736 | tf_op jit(solution)/shard_map/ppermute | solution.py:18
  454.3 40.0 %collective-permute-start.38 = (bf16[2,128,2048]{2,1,0:T(8,128)(2,1)S(1)}, bf16[2,128,2048]{2,1,0:T(8,128)(2,1)}, u32[]{:S(2)}, u32[]{:S(2)}) collective-permute-start(bf16[2,128,2048]{2,1,0:T(8,128)(2,1)S(1)} %pad_maximum_fusion.9), channel_id=1, source_target_pairs={{0,1},{1,0},{2,3},{3,2},{4,5},{5,4},{6,7},{7,6},{8,9},{9,8},{10,11... | collective-permute-start | bytes 3145736 | tf_op jit(solution)/shard_map/ppermute | solution.py:14
  470.7 202.1 %collective-permute-start.70 = (bf16[1024,2816]{1,0:T(8,128)(2,1)}, bf16[1024,2816]{1,0:T(8,128)(2,1)}, u32[]{:S(2)}, u32[]{:S(2)}) collective-permute-start(bf16[1024,2816]{1,0:T(8,128)(2,1)} %slice.715), channel_id=1, source_target_pairs={{0,2},{2,0},{1,3},{3,1},{4,6},{6,4},{5,7},{7,5},{8,10},{10,8},{9,1... | collective-permute-start | bytes 17301512 | tf_op jit(solution)/shard_map/ppermute | solution.py:22
  475.1 101.4 %collective-permute-start.74 = (bf16[1024,1408]{1,0:T(8,128)(2,1)}, bf16[1024,1408]{1,0:T(8,128)(2,1)}, u32[]{:S(2)}, u32[]{:S(2)}) collective-permute-start(bf16[1024,1408]{1,0:T(8,128)(2,1)} %slice.723), channel_id=1, source_target_pairs={{0,2},{2,0},{1,3},{3,1},{4,6},{6,4},{5,7},{7,5},{8,10},{10,8},{9,1... | collective-permute-start | bytes 8650760 | tf_op jit(solution)/shard_map/ppermute | solution.py:22
  583.5 65.3 %collective-permute-start.75 = (bf16[512,1408]{1,0:T(8,128)(2,1)}, bf16[512,1408]{1,0:T(8,128)(2,1)}, u32[]{:S(2)}, u32[]{:S(2)}) collective-permute-start(bf16[512,1408]{1,0:T(8,128)(2,1)} %slice.864), channel_id=1, source_target_pairs={{0,8},{8,0},{16,24},{24,16},{1,9},{9,1},{17,25},{25,17},{2,10},{10... | collective-permute-start | bytes 4325384 | tf_op jit(solution)/shard_map/ppermute | solution.py:27
  648.8 41.7 %collective-permute-start.67 = (bf16[512,512]{0,1:T(8,128)(2,1)}, bf16[512,512]{0,1:T(8,128)(2,1)}, u32[]{:S(2)}, u32[]{:S(2)}) collective-permute-start(bf16[512,512]{0,1:T(8,128)(2,1)} %slice.868), channel_id=1, source_target_pairs={{0,8},{8,0},{16,24},{24,16},{1,9},{9,1},{17,25},{25,17},{2,10},{10... | collective-permute-start | bytes 1572872 | tf_op jit(solution)/shard_map/ppermute | solution.py:27
  652.7 100.9 %collective-permute-start.76 = (bf16[256,1408]{1,0:T(8,128)(2,1)}, bf16[256,1408]{1,0:T(8,128)(2,1)}, u32[]{:S(2)}, u32[]{:S(2)}) collective-permute-start(bf16[256,1408]{1,0:T(8,128)(2,1)} %slice.866), channel_id=1, source_target_pairs={{0,16},{8,24},{16,0},{24,8},{1,17},{9,25},{17,1},{25,9},{2,18},{10... | collective-permute-start | bytes 2162696 | tf_op jit(solution)/shard_map/ppermute | solution.py:27
  665.8 91.4 %collective-permute-start.63 = (bf16[512,640]{0,1:T(8,128)(2,1)}, bf16[512,640]{0,1:T(8,128)(2,1)}, u32[]{:S(2)}, u32[]{:S(2)}) collective-permute-start(bf16[512,640]{0,1:T(8,128)(2,1)} %slice.867), channel_id=1, source_target_pairs={{0,8},{8,0},{16,24},{24,16},{1,9},{9,1},{17,25},{25,17},{2,10},{10... | collective-permute-start | bytes 1966088 | tf_op jit(solution)/shard_map/ppermute | solution.py:27
  685.5 77.2 %collective-permute-start.71 = (bf16[512,2816]{1,0:T(8,128)(2,1)S(1)}, bf16[512,2816]{1,0:T(8,128)(2,1)}, u32[]{:S(2)}, u32[]{:S(2)}) collective-permute-start(bf16[512,2816]{1,0:T(8,128)(2,1)S(1)} %slice.863), channel_id=1, source_target_pairs={{0,8},{8,0},{16,24},{24,16},{1,9},{9,1},{17,25},{25,17},{2,10},{10... | collective-permute-start | bytes 8650760 | tf_op jit(solution)/shard_map/ppermute | solution.py:27
  692.6 60.3 %collective-permute-start.68 = (bf16[256,512]{0,1:T(8,128)(2,1)S(1)}, bf16[256,512]{0,1:T(8,128)(2,1)S(1)}, u32[]{:S(2)}, u32[]{:S(2)}) collective-permute-start(bf16[256,512]{0,1:T(8,128)(2,1)S(1)} %slice.870), channel_id=1, source_target_pairs={{0,16},{8,24},{16,0},{24,8},{1,17},{9,25},{17,1},{25,9},{2,18},{10... | collective-permute-start | bytes 786440 | tf_op jit(solution)/shard_map/ppermute | solution.py:27
  759.3 47.7 %collective-permute-start.64 = (bf16[256,640]{0,1:T(8,128)(2,1)}, bf16[256,640]{0,1:T(8,128)(2,1)}, u32[]{:S(2)}, u32[]{:S(2)}) collective-permute-start(bf16[256,640]{0,1:T(8,128)(2,1)} %slice.869), channel_id=1, source_target_pairs={{0,16},{8,24},{16,0},{24,8},{1,17},{9,25},{17,1},{25,9},{2,18},{10... | collective-permute-start | bytes 983048 | tf_op jit(solution)/shard_map/ppermute | solution.py:27
  768.8 66.9 %collective-permute-start.72 = (bf16[256,2816]{1,0:T(8,128)(2,1)}, bf16[256,2816]{1,0:T(8,128)(2,1)}, u32[]{:S(2)}, u32[]{:S(2)}) collective-permute-start(bf16[256,2816]{1,0:T(8,128)(2,1)} %slice.865), channel_id=1, source_target_pairs={{0,16},{8,24},{16,0},{24,8},{1,17},{9,25},{17,1},{25,9},{2,18},{10... | collective-permute-start | bytes 4325384 | tf_op jit(solution)/shard_map/ppermute | solution.py:27
  (133 other events, 2688.9 us)

commit v2 on v1

v2 whole, which is shorter than its diff:
```python
import jax
import jax.numpy as jnp
import numpy as np
from jax import lax
from jax.experimental import pallas as pl
from jax.experimental.pallas import tpu as pltpu
from jax.sharding import Mesh
from jax.sharding import PartitionSpec as P

HEAD_SIZE = 64
EPS = 1e-05
BF = jnp.bfloat16
F32 = jnp.float32


def swap_x(a):
    return lax.ppermute(a, "x", [(0, 1), (1, 0)])


def swap_y(a):
    return lax.ppermute(a, "y", [(0, 1), (1, 0)])


def swap_c(a):
    return lax.ppermute(a, "c", [(0, 1), (1, 0)])


def swap_z(a, bit):
    n = lax.axis_size("z")
    return lax.ppermute(a, "z", [(i, i ^ bit) for i in range(n)])


def far_bits():
    n = lax.axis_size("z")
    bits = []
    bit = n // 2
    while bit:
        bits.append(bit)
        bit //= 2
    return bits


def z_order():
    order = [0]
    for bit in far_bits():
        order = order + [r ^ bit for r in order]
    return order


def meet(*values):
    return lax.optimization_barrier(values)


def single(work, *args):
    shapes = jax.eval_shape(work, *args)
    return lax.cond(
        lax.axis_index("z") >= 0,
        work,
        lambda *_: jax.tree.map(lambda s: jnp.zeros(s.shape, s.dtype), shapes),
        *args,
    )


def gather_near(own):
    return own, swap_x(own), swap_y(own)


def gather_diag(near):
    _, from_x, from_y = near
    half = from_x.shape[-1] // 2
    return swap_y(from_x[..., :half]), swap_x(from_y[..., half:])


def gather_join(near, diag):
    return jnp.concatenate(tuple(near) + (jnp.concatenate(diag, axis=-1),), axis=1)


def gather_far(near):
    return gather_join(near, gather_diag(near))


def scatter_far(part):
    m, rows, f = part.shape
    diag = part[:, 3 * rows // 4 :]
    return swap_y(diag[..., : f // 2]), swap_x(diag[..., f // 2 :])


def scatter_prep(part, far):
    m, rows, f = part.shape
    half = f // 2
    low, high = far
    part = part.reshape(m, 4, rows // 4, f)
    to_x = part[:, 1]
    to_y = part[:, 2]
    to_x = jnp.concatenate(
        [(to_x[..., :half].astype(F32) + low.astype(F32)).astype(BF), to_x[..., half:]], axis=-1
    )
    to_y = jnp.concatenate(
        [to_y[..., :half], (to_y[..., half:].astype(F32) + high.astype(F32)).astype(BF)], axis=-1
    )
    return to_x, to_y


def scatter_near(to_x, to_y):
    return swap_x(to_x), swap_y(to_y)


def scatter_sum(part, near):
    rows = part.shape[1] // 4
    return part[:, :rows].astype(F32) + near[0].astype(F32) + near[1].astype(F32)


def column_part(a, index):
    width = a.shape[1] // 2
    return lax.dynamic_slice_in_dim(a, index * width, width, axis=1)


def pick(a, axis, index):
    return lax.dynamic_index_in_dim(a, index, axis, keepdims=False)


def z_first(*shards):
    held = jnp.stack(shards)[None]
    return held, swap_z(held, far_bits()[0])


def z_rest(pair):
    held = jnp.concatenate(pair, axis=0)
    bits = far_bits()[1:]
    for bit in bits[:-1]:
        held = jnp.concatenate([held, swap_z(held, bit)], axis=0)
    return held, swap_z(held, bits[-1])


def both(pair):
    return jnp.concatenate(pair, axis=0)


def assemble(streams, z, y, extra=0, split=()):
    order = np.array(z_order() + [0], np.int32)
    n, rows, cols = streams[0].shape
    block = rows - extra
    last = np.arange(n + 1) == n
    where = jnp.where(jnp.asarray(last), y, jnp.asarray(order) ^ z)

    edges = (0,) + tuple(split) + (cols,)
    spans = list(zip(edges[:-1], edges[1:]))

    def kernel(where_ref, own, own_c, peer, peer_c, *more):
        yy = where_ref[n]
        for ref, at_c, at_y in ((own, 0, yy), (own_c, 1, yy), (peer, 0, 1 - yy), (peer_c, 1, 1 - yy)):
            if not extra:
                more[0][at_c, 0, at_y] = ref[0]
                continue
            for out, (lo, hi) in zip(more, spans):
                out[at_c, 0, at_y] = ref[0, :block, lo:hi]
            more[-1][at_c, 0, at_y] = ref[0, block:, :128]

    out_shape = [jax.ShapeDtypeStruct((2, n, 2, block, hi - lo), BF) for lo, hi in spans]
    out_specs = [
        pl.BlockSpec((2, 1, 2, block, hi - lo), lambda i, at: (0, at[i], 0, 0, 0)) for lo, hi in spans
    ]
    if extra:
        out_shape.append(jax.ShapeDtypeStruct((2, n, 2, extra, 128), BF))
        out_specs.append(pl.BlockSpec((2, 1, 2, extra, 128), lambda i, at: (0, at[i], 0, 0, 0)))
    moved = 4 * n * rows * cols * 4
    return pl.pallas_call(
        kernel,
        out_shape=out_shape,
        grid_spec=pltpu.PrefetchScalarGridSpec(
            num_scalar_prefetch=1,
            grid=(n,),
            in_specs=[pl.BlockSpec((1, rows, cols), lambda i, at: (i, 0, 0))] * 4,
            out_specs=out_specs,
        ),
        cost_estimate=pl.CostEstimate(flops=0, bytes_accessed=moved, transcendentals=0),
    )(where, *streams)


def grad_half(index, left, right):
    nz = lax.axis_size("z")
    half = left.shape[1] // 2
    part = rows_rows(left[:, index * half : (index + 1) * half], right).astype(BF)
    return part.reshape(nz, 2, half // (2 * nz), right.shape[1])


def add(a, b):
    return a.astype(F32) + b.astype(F32)


def reduce_step(grad, z, bit):
    n, _, block, cols = grad.shape
    pairs = grad.reshape(n // 2, 2, 2, block, cols)
    here = (z // bit) % 2
    return pick(pairs, 1, here), swap_z(pick(pairs, 1, 1 - here).astype(BF), bit)


def reduce_near(pair, z):
    return reduce_step(add(*pair), z, 1)


def reduce_far(pair, z):
    grad = add(*pair)
    bits = far_bits()[:-1][::-1]
    for bit in bits[:-1]:
        grad = add(*reduce_step(grad, z, bit))
    return reduce_step(grad, z, bits[-1])


def reduce_y(pair, y):
    grad = add(*pair)[0]
    return pick(grad, 0, y), swap_y(pick(grad, 0, 1 - y).astype(BF)).astype(F32)


def join(parts, y):
    mine, got = parts
    first = y == 0
    return jnp.concatenate([jnp.where(first, mine, got), jnp.where(first, got, mine)], axis=1)


def regroup(a, block, c, back=False):
    m, rows, width = a.shape
    half = width // 2
    count = half // block
    if block % 128:
        first = c == 0
        if back:
            own, other = (p.reshape(m, rows, count, block) for p in (a[..., :half], a[..., half:]))
            pair = jnp.stack([jnp.where(first, own, other), jnp.where(first, other, own)], axis=3)
            return pair.reshape(m, rows, width)
        pair = a.reshape(m, rows, count, 2, block)
        even, odd = pair[:, :, :, 0].reshape(m, rows, half), pair[:, :, :, 1].reshape(m, rows, half)
        return jnp.concatenate([jnp.where(first, even, odd), jnp.where(first, odd, even)], axis=-1)

    def kernel(core_ref, src, out):
        for core in range(2):

            @pl.when(core_ref[0] == core)
            def _():
                for i in range(count):
                    for r in range(2):
                        apart = pl.ds(r * half + i * block, block)
                        mixed = pl.ds((2 * i + (core ^ r)) * block, block)
                        if back:
                            out[:, mixed] = src[:, apart]
                        else:
                            out[:, apart] = src[:, mixed]

    step = 128
    total = m * rows
    out = pl.pallas_call(
        kernel,
        out_shape=jax.ShapeDtypeStruct((total, width), a.dtype),
        grid_spec=pltpu.PrefetchScalarGridSpec(
            num_scalar_prefetch=1,
            grid=(total // step,),
            in_specs=[pl.BlockSpec((step, width), lambda i, core: (i, 0))],
            out_specs=pl.BlockSpec((step, width), lambda i, core: (i, 0)),
        ),
        cost_estimate=pl.CostEstimate(
            flops=0, bytes_accessed=2 * total * width * a.dtype.itemsize, transcendentals=0
        ),
    )(c.reshape(1).astype(jnp.int32), a.reshape(total, width))
    return out.reshape(a.shape)


def reduce_z(grad, z, y):
    bit = 1
    for _ in far_bits():
        n, _, block, cols = grad.shape
        pairs = grad.reshape(n // 2, 2, 2, block, cols)
        here = (z // bit) % 2
        got = swap_z(pick(pairs, 1, 1 - here).astype(BF), bit)
        grad = pick(pairs, 1, here) + got.astype(F32)
        bit *= 2
    mine = pick(grad[0], 0, y)
    return mine, swap_y(pick(grad[0], 0, 1 - y).astype(BF)).astype(F32)


def join(parts, y):
    mine, got = parts
    first = y == 0
    return jnp.concatenate([jnp.where(first, mine, got), jnp.where(first, got, mine)], axis=1)


def rows_rows(left, right):
    return lax.dot_general(left, right, (((0,), (0,)), ((), ())), preferred_element_type=F32)


def cols_cols(left, right):
    return lax.dot_general(left, right, (((1,), (1,)), ((), ())), preferred_element_type=F32)


def rotate(v, cos, sin):
    half = v.shape[-1] // 2
    turned = jnp.concatenate([-v[..., half:], v[..., :half]], axis=-1)
    return v * cos + turned * sin


def rotate_back(v, cos, sin):
    half = v.shape[-1] // 2
    w = v * sin
    turned = jnp.concatenate([w[..., half:], -w[..., :half]], axis=-1)
    return v * cos + turned


def norm_back(d_normed, unit, gain, scale):
    d_unit = d_normed * gain
    return scale * (d_unit - unit * jnp.mean(d_unit * unit, axis=-1, keepdims=True))


def on_device(
    hidden_in,
    segment_ids,
    attn_gain,
    mlp_gain,
    w_query,
    key_weight,
    value_weight,
    w_out,
    w_gate,
    w_up,
    w_down,
    out_cotangent,
):
    z, y, c, x = (lax.axis_index(n) for n in ("z", "y", "c", "x"))
    nz = lax.axis_size("z")
    micro = hidden_in.shape[0]
    toks = hidden_in.shape[2]
    width = hidden_in.shape[3]
    block = w_query.shape[0]
    scale = HEAD_SIZE ** (-0.5)
    extra = 16

    def pack_attn(index):
        gains = jnp.stack([attn_gain, mlp_gain])
        body = jnp.concatenate(
            [
                column_part(w_query, index),
                column_part(key_weight, index),
                column_part(value_weight, index),
                column_part(w_out, index),
            ],
            axis=1,
        )
        gains = jnp.pad(gains, ((0, extra - 2), (0, body.shape[1] - block)))
        return jnp.concatenate([body, gains], axis=0)

    def pack_gu(index):
        return jnp.concatenate([column_part(w_gate, index), column_part(w_up, index)], axis=1)

    def pack_down(index):
        return column_part(w_down, index)

    q_cols = w_query.shape[1] // 2
    kv_cols = key_weight.shape[1] // 2
    qkv_cols = q_cols + 2 * kv_cols
    own_far = z_first(pack_attn(y))
    attn_theirs = swap_y(pack_attn(1 - y))
    other_ids = swap_y(segment_ids[:, 0])
    attn_theirs, other_ids, hid, *own_far = meet(attn_theirs, other_ids, hidden_in[:, 0], *own_far)
    peer_far = z_first(attn_theirs)
    hid = regroup(hid, block, c)
    hid_near = gather_near(hid)
    attn_own = z_rest(own_far)
    more = meet(*hid_near, *peer_far, pack_gu(y), pack_gu(1 - y))
    hid_near, peer_far, gu_mine, gu_give = more[:3], more[3:5], more[5], more[6]
    hid_diag = gather_diag(hid_near)
    attn_peer = z_rest(peer_far)
    gu_far = z_first(gu_mine)
    more = meet(out_cotangent[:, 0], pack_down(1 - y), gu_give, *hid_diag, *attn_own, *attn_peer, *gu_far)
    cot, down_give, gu_give, hid_diag = *more[:3], more[3:5]
    attn_own, attn_peer, gu_far = both(more[5:7])[:, 0], both(more[7:9])[:, 0], more[9:]
    attn_streams = (attn_own, swap_c(attn_own), attn_peer, swap_c(attn_peer))
    gu_theirs = swap_y(gu_give)
    hid_all = gather_join(hid_near, hid_diag)
    attn_w = assemble(attn_streams, z, y, extra, (qkv_cols,))
    qkv_w, out_w, gains = attn_w
    qkv_w, out_w = qkv_w.reshape(width, -1), out_w.reshape(width, -1)
    gains = gains[:, :, :, :2, :block].astype(F32)
    gain_a = gains[:, :, :, 0].reshape(width)
    gain_m = gains[:, :, :, 1].reshape(width)
    hid_all, gu_theirs, qkv_w, out_w, gain_a, gain_m = meet(hid_all, gu_theirs, qkv_w, out_w, gain_a, gain_m)
    gu_own = z_rest(gu_far)
    gu_far = z_first(gu_theirs)
    down_theirs = swap_y(down_give)
    cot = regroup(cot, block, c)
    cot_near = gather_near(cot)

    length = 2 * toks
    groups = micro * 2
    ids = jnp.stack([segment_ids[:, 0], other_ids], axis=1).reshape(groups, length)
    ids = jnp.where(x == 0, ids, jnp.roll(ids, toks, axis=1))
    pos = (jnp.arange(length, dtype=jnp.int32) + toks * x) % length
    same = ids[:, :, None] == ids[:, None, :]
    allowed = jnp.logical_and(same, (pos[None, :] <= pos[:, None])[None])
    places = jnp.sum(allowed.astype(F32), axis=2) - 1.0
    freq = jnp.arange(HEAD_SIZE // 2, dtype=F32)
    inverse = 10000.0 ** (-2.0 * freq / HEAD_SIZE)
    angles = places[:, :, None] * inverse
    cos = jnp.concatenate([jnp.cos(angles)] * 2, axis=-1)
    sin = jnp.concatenate([jnp.sin(angles)] * 2, axis=-1)

    rows = micro * 4 * toks
    heads = q_cols // HEAD_SIZE

    def attention(hid_all, gain_a, qkv_w, out_w, cos, sin, allowed):
        hid32 = hid_all.astype(F32).reshape(rows, width)
        scale_a = lax.rsqrt(jnp.mean(hid32 * hid32, axis=-1, keepdims=True) + EPS)
        normed_a = (hid32 * scale_a * gain_a).astype(BF)
        qkv = jnp.dot(normed_a, qkv_w, preferred_element_type=F32)
        q_lin = qkv[:, :q_cols].reshape(groups, length, heads, HEAD_SIZE)
        k_lin = qkv[:, q_cols : q_cols + kv_cols].reshape(groups, length, HEAD_SIZE)
        values = qkv[:, q_cols + kv_cols :].astype(BF).reshape(groups, length, HEAD_SIZE)
        queries = rotate(q_lin, cos[:, :, None], sin[:, :, None]).astype(BF)
        keys = rotate(k_lin, cos, sin).astype(BF)
        scores = jnp.einsum("gqhd,gsd->ghqs", queries, keys, preferred_element_type=F32) * scale
        scores = jnp.where(allowed[:, None], scores, -1e30)
        top = jnp.max(scores, axis=-1, keepdims=True)
        expo = jnp.exp(scores - top)
        probs = expo / jnp.sum(expo, axis=-1, keepdims=True)
        attended = jnp.einsum("ghqs,gsd->gqhd", probs.astype(BF), values, preferred_element_type=F32)
        attended = attended.reshape(rows, q_cols).astype(BF)
        attn_part = cols_cols(attended, out_w).astype(BF).reshape(micro, 4 * toks, width)
        return scale_a, normed_a, queries, keys, values, probs, attended, attn_part

    scale_a, normed_a, queries, keys, values, probs, attended, attn_part = single(
        attention, hid_all, gain_a, qkv_w, out_w, cos, sin, allowed
    )
    more = meet(attn_part, down_theirs, pack_down(y), *cot_near, *gu_own, *gu_far)
    attn_part, down_theirs, down_mine, cot_near = *more[:3], more[3:6]
    gu_own, gu_far = more[6:8], more[8:]
    attn_far = scatter_far(attn_part)
    gu_peer = z_rest(gu_far)
    down_far = z_first(down_mine, down_theirs)
    attn_near = scatter_near(*scatter_prep(attn_part, attn_far))
    more = meet(*attn_near, *gu_peer, *down_far, *gu_own, *cot_near)
    attn_near, gu_peer, down_far, gu_own = more[:2], both(more[2:4])[:, 0], more[4:6], both(more[6:8])[:, 0]
    cot_near = more[8:]
    mid = hid.astype(F32) + scatter_sum(attn_part, attn_near)

    scale_m = lax.rsqrt(jnp.mean(mid * mid, axis=-1, keepdims=True) + EPS)
    unit_m = mid * scale_m
    normed_near = gather_near((unit_m * gain_m).astype(BF))
    down = z_rest(down_far)
    gu_streams = (gu_own, swap_c(gu_own), gu_peer, swap_c(gu_peer))
    more = meet(*gu_streams, *down, *normed_near, *cot_near)
    gu_streams, down, normed_near, cot_near = more[:4], both(more[4:6]), more[6:9], more[9:]
    normed_m = gather_far(normed_near).reshape(rows, width)
    cot_diag = gather_diag(cot_near)
    gu_w = assemble(gu_streams, z, y)[0].reshape(width, -1)
    down_c = swap_c(down)
    normed_m, gu_w, *cot_diag = meet(normed_m, gu_w, *cot_diag)
    cot_rows = gather_join(cot_near, cot_diag).reshape(rows, width)

    def feed(normed_m, gu_w, cot_rows):
        gu = jnp.dot(normed_m, gu_w, preferred_element_type=F32)
        ff = gu.shape[1] // 2
        inner = (jax.nn.silu(gu[:, :ff]) * gu[:, ff:]).astype(BF)
        return gu, inner, grad_half(1, cot_rows, inner)

    gu, inner, down_send = single(feed, normed_m, gu_w, cot_rows)
    down_send, down_c = meet(down_send, down_c)
    down_got = swap_c(down_send)
    down_w = assemble((down[:, 0], down_c[:, 0], down[:, 1], down_c[:, 1]), z, y)[0].reshape(width, -1)

    def feed_back(gu, inner, cot_rows, down_w, gu_w):
        d_inner = jnp.dot(cot_rows, down_w, preferred_element_type=F32)
        ff = gu.shape[1] // 2
        gate, up = gu[:, :ff], gu[:, ff:]
        sig = jax.nn.sigmoid(gate)
        d_gate = (d_inner * up * sig * (1.0 + gate * (1.0 - sig))).astype(BF)
        d_up = (d_inner * gate * sig).astype(BF)
        d_gu = jnp.concatenate([d_gate, d_up], axis=1)
        back = cols_cols(d_gu, gu_w).astype(BF)
        return d_gate, d_up, back.reshape(micro, 4 * toks, width), grad_half(0, cot_rows, inner)

    d_gate, d_up, back_mlp, down_keep = single(feed_back, gu, inner, cot_rows, down_w, gu_w)
    back_mlp, down_keep, down_got = meet(back_mlp, down_keep, down_got)
    back_far = scatter_far(back_mlp)

    def gate_grads(normed_m, d_gate):
        return grad_half(1, normed_m, d_gate), grad_half(0, normed_m, d_gate)

    gate_send, gate_keep = single(gate_grads, normed_m, d_gate)
    gate_send, gate_keep, *back_far = meet(gate_send, gate_keep, *back_far)
    gate_got = swap_c(gate_send)
    *ready, d_up, gate_keep, gate_got = meet(*scatter_prep(back_mlp, back_far), d_up, gate_keep, gate_got)
    back_near = scatter_near(*ready)
    down_sum = reduce_near((down_keep, down_got), z)
    gate_sum = reduce_near((gate_keep, gate_got), z)

    def up_grads(normed_m, d_up, inner, down_w):
        part = cols_cols(inner, down_w).astype(BF).reshape(micro, 4 * toks, width)
        return grad_half(1, normed_m, d_up), grad_half(0, normed_m, d_up), part

    up_send, up_keep, mlp_part = single(up_grads, normed_m, d_up, inner, down_w)
    up_send, up_keep, mlp_part, *back_near = meet(up_send, up_keep, mlp_part, *back_near)
    up_got = swap_c(up_send)
    d_normed_m = scatter_sum(back_mlp, back_near)
    gain_m_part = jnp.sum(d_normed_m * unit_m, axis=(0, 1))
    d_mid = cot.astype(F32) + norm_back(d_normed_m, unit_m, gain_m, scale_m)

    d_mid_near = gather_near(d_mid.astype(BF))
    more = meet(up_keep, up_got, *d_mid_near, *down_sum, *gate_sum)
    up_keep, up_got, d_mid_near, down_sum, gate_sum = *more[:2], more[2:5], more[5:7], more[7:]
    d_mid_diag = gather_diag(d_mid_near)
    up_sum = reduce_near((up_keep, up_got), z)
    down_sum = reduce_far(down_sum, z)
    more = meet(mlp_part, *d_mid_diag, *d_mid_near)
    mlp_part, d_mid_diag, d_mid_near = more[0], more[1:3], more[3:]
    gate_sum = reduce_far(gate_sum, z)
    mlp_far = scatter_far(mlp_part)
    d_mid_all = gather_join(d_mid_near, d_mid_diag).reshape(rows, width)

    def attention_back(d_mid_all, out_w, values, probs, attended):
        d_att = jnp.dot(d_mid_all, out_w, preferred_element_type=F32).astype(BF)
        d_att = d_att.reshape(groups, length, heads, HEAD_SIZE)
        d_probs = jnp.einsum("gqhd,gsd->ghqs", d_att, values, preferred_element_type=F32)
        inner_sum = jnp.sum(probs * d_probs, axis=-1, keepdims=True)
        d_scores = (probs * (d_probs - inner_sum)).astype(BF)
        return d_att, d_scores, grad_half(1, d_mid_all, attended), grad_half(0, d_mid_all, attended)

    d_att, d_scores, out_send, out_keep = single(attention_back, d_mid_all, out_w, values, probs, attended)
    d_scores, out_send, out_keep, *more = meet(d_scores, out_send, out_keep, *mlp_far, *up_sum, *down_sum)
    mlp_far, up_sum, down_sum = more[:2], more[2:4], more[4:]
    out_got = swap_c(out_send)
    down_parts = reduce_y(down_sum, y)
    up_sum = reduce_far(up_sum, z)
    mlp_near = scatter_near(*scatter_prep(mlp_part, mlp_far))
    out_sum = reduce_near((out_keep, out_got), z)

    def qkv_back(d_scores, d_att, probs, queries, keys, cos, sin, qkv_w, hid_all, scale_a):
        d_queries = jnp.einsum("ghqs,gsd->gqhd", d_scores, keys, preferred_element_type=F32) * scale
        d_keys = jnp.einsum("ghqs,gqhd->gsd", d_scores, queries, preferred_element_type=F32) * scale
        d_values = jnp.einsum("ghqs,gqhd->gsd", probs.astype(BF), d_att, preferred_element_type=F32)
        d_q = rotate_back(d_queries, cos[:, :, None], sin[:, :, None]).reshape(rows, q_cols)
        d_k = rotate_back(d_keys, cos, sin).reshape(rows, kv_cols)
        d_v = d_values.reshape(rows, kv_cols)
        d_qkv = jnp.concatenate([d_q, d_k, d_v], axis=1).astype(BF)
        back = cols_cols(d_qkv, qkv_w)
        unit_a = hid_all.astype(F32).reshape(rows, width) * scale_a
        return d_qkv, back.astype(BF).reshape(micro, 4 * toks, width), jnp.sum(back * unit_a, axis=0)

    d_qkv, back_attn, gain_a_part = single(
        qkv_back, d_scores, d_att, probs, queries, keys, cos, sin, qkv_w, hid_all, scale_a
    )
    gain_rows = jnp.stack([gain_a_part, gain_m_part]).reshape(2, 2, nz, 2, block)
    gain_rows = gain_rows.transpose(1, 2, 3, 0, 4)
    gain_rows = jnp.pad(gain_rows, ((0, 0),) * 3 + ((0, extra - 2), (0, qkv_cols - block))).astype(BF)
    qkv_send = jnp.concatenate([grad_half(1, normed_a, d_qkv), gain_rows[1]], axis=2)
    back_attn, qkv_send, d_qkv, *more = meet(
        back_attn, qkv_send, d_qkv, *mlp_near, *gate_sum, *up_sum, *out_sum
    )
    mlp_near, gate_sum, up_sum, out_sum = more[:2], more[2:4], more[4:6], more[6:]
    qkv_got = swap_c(qkv_send)
    attn_far = scatter_far(back_attn)
    qkv_keep = jnp.concatenate([grad_half(0, normed_a, d_qkv), gain_rows[0]], axis=2)
    qkv_keep, qkv_got = meet(qkv_keep, qkv_got)
    qkv_sum = reduce_near((qkv_keep, qkv_got), z)
    more = meet(*attn_far, *qkv_sum)
    attn_far, qkv_sum = more[:2], more[2:]
    attn_near = scatter_near(*scatter_prep(back_attn, attn_far))
    qkv_sum = reduce_far(qkv_sum, z)
    out_sum = reduce_far(out_sum, z)
    attn_near0, attn_near1, *more = meet(*attn_near, *qkv_sum, *out_sum, *mlp_near, *gate_sum, *up_sum)
    attn_near, qkv_sum, out_sum = (attn_near0, attn_near1), more[:2], more[2:4]
    mlp_near, gate_sum, up_sum = more[4:6], more[6:8], more[8:]
    qkv_parts = reduce_y(qkv_sum, y)
    gate_parts = reduce_y(gate_sum, y)
    up_parts = reduce_y(up_sum, y)
    out_parts = reduce_y(out_sum, y)
    block_out = (mid + scatter_sum(mlp_part, mlp_near)).astype(BF)
    d_normed_a = scatter_sum(back_attn, attn_near)
    sc_a = scale_a.reshape(micro, 4 * toks, 1)[:, :toks]
    unit_a = hid.astype(F32) * sc_a
    input_grad = d_mid + norm_back(d_normed_a, unit_a, gain_a, sc_a)

    keep = (qkv_parts[0] + qkv_parts[1])[block : block + 2, :block]
    keep = keep + swap_x(keep)
    qkv_parts = tuple(p[:block] for p in qkv_parts)

    def cut(parts, lo, hi):
        return join((parts[0][:, lo:hi], parts[1][:, lo:hi]), y)

    return (
        regroup(block_out, block, c, True)[:, None],
        regroup(input_grad, block, c, True)[:, None],
        keep[0],
        keep[1],
        cut(qkv_parts, 0, q_cols),
        cut(qkv_parts, q_cols, q_cols + kv_cols),
        cut(qkv_parts, q_cols + kv_cols, qkv_cols),
        join(out_parts, y),
        join(gate_parts, y),
        join(up_parts, y),
        join(down_parts, y),
    )


def solution(mesh):
    n_dp, n_tensor = mesh.shape["dp"], mesh.shape["tensor"]
    grid = Mesh(mesh.devices.reshape(n_dp // 4, 2, 2, n_tensor), ("z", "y", "c", "x"))
    dp = ("z", "y", "c")
    token = P(None, dp, "x", None)
    weight = P(dp, "x")
    gain = P(dp)
    in_specs = (token, P(None, dp, None), gain, gain) + (weight,) * 7 + (token,)
    out_specs = (token, token, gain, gain) + (weight,) * 7
    return jax.shard_map(
        on_device, mesh=grid, in_specs=in_specs, out_specs=out_specs, check_vma=False
    )
```

time: 867 us -> 696 us (0.80)
  waiting for transfers between devices: 430 us -> 220 us
  other arithmetic: 78.2 us -> 114 us
  Pallas kernels: 0 us -> 30.5 us
  local copies, waits for them, and re-layouts: 125 us -> 97 us
  matrix products: 139 us -> 153 us
  starting transfers between devices: 79.3 us -> 67.9 us
    ppermute x19 -> x20, waiting for transfers between devices: 260 us -> 136 us  [swap_z(): return lax.ppermute(a, 'z', [(i, i ^ bit) for i in range(n)])]
    ppermute x25, waiting for transfers between devices: 130 us -> 40.6 us  [swap_y(): return lax.ppermute(a, 'y', [(0, 1), (1, 0)])]
    unnamed x269 -> x153, local copies, waits for them, and re-layouts: 75.6 us -> 16.1 us
    pallas_call x0 -> x7, Pallas kernels: none -> 30.5 us  [the longest x3 21.3 us: assemble(): pl.pallas_call(kernel, out_shape=out_shape, grid_spec=pltpu.PrefetchScala...]
    squeeze x4 -> x20, local copies, waits for them, and re-layouts: 1.2 us -> 18 us  [the longest x11 6.97 us: pick(): return lax.dynamic_index_in_dim(a, index, axis, keepdims=False)]
    dot_general x4 -> x10, matrix products: 36.4 us -> 51.7 us  [rows_rows(): lax.dot_general(left, right, (((0,), (0,)), ((), ())), preferred_element_...]
    convert_element_type x5 -> x17, local copies, waits for them, and re-layouts: 2.59 us -> 13.4 us  [the longest x10 7.03 us: reduce_step(): pick(pairs, 1, 1 - here).astype(BF)]
    cond x0 -> x47, local copies, waits for them, and re-layouts: none -> 9.33 us
  transfers between devices with their start and end apart: 78 -> 72, of which waited for: 36 -> 32; matrix products, arithmetic and copies ran while one was open for 28% -> 47% of each run, Pallas kernels for 0% -> 4%
where the time goes in v2:
time: 696 us; the launch traced here: 686 us
  waiting for transfers between devices  220 us (32%)
  matrix products  153 us (22%)
  other arithmetic  114 us (16%)
  local copies, waits for them, and re-layouts  97 us (14%)
  starting transfers between devices  67.9 us (10%)
  Pallas kernels  30.5 us (4%)
    ppermute x20, waiting for transfers between devices, swap_z(): return lax.ppermute(a, 'z', [(i, i ^ bit) for i in range(n)])  136 us
    dot_general x10, matrix products, rows_rows(): lax.dot_general(left, right, (((0,), (0,)), ((), ())), preferred_element_...  51.7 us
    ppermute x17, waiting for transfers between devices, swap_x(): return lax.ppermute(a, 'x', [(0, 1), (1, 0)])  43.6 us
    ppermute x25, waiting for transfers between devices, swap_y(): return lax.ppermute(a, 'y', [(0, 1), (1, 0)])  40.6 us
    dot_general x4, matrix products, cols_cols(): lax.dot_general(left, right, (((1,), (1,)), ((), ())), preferred_element_...  39.2 us
    ppermute x25, starting transfers between devices, swap_y(): return lax.ppermute(a, 'y', [(0, 1), (1, 0)])  26.1 us
    ppermute x20, starting transfers between devices, swap_z(): return lax.ppermute(a, 'z', [(i, i ^ bit) for i in range(n)])  24.7 us
    add x15, other arithmetic, add(): return a.astype(F32) + b.astype(F32)  21.9 us
  transfers between devices with their start and end apart: 72, of which 32 were waited for; matrix products, arithmetic and copies ran while one was open for 47% of the time, Pallas kernels for 4%

profile of v2, /device:TPU:0, one launch (start us, length us, event | category | flops | bytes accessed | tf_op | source)
XLA Modules:
  0.0 685.7 jit_solution(1109747767299326700)
XLA Ops:
  15.7 9.2 %collective-permute-done.2 = bf16[1,1,144,1152]{3,2,0,1:T(8,128)(2,1)} collective-permute-done((bf16[1,1,144,1152]{3,2,0,1:T(8,128)(2,1)S(1)}, bf16[1,1,144,1152]{3,2,0,1:T(8,128)(2,1)}, u32[]{:S(2)}, u32[]{:S(2)}) %collective-permute-start.2) | collective-permute-done | bytes 331808 | tf_op jit(solution)/shard_map/ppermute | solution.py:30
  35.8 11.3 %collective-permute-done.5 = bf16[1,1,144,1152]{3,2,0,1:T(8,128)(2,1)S(1)} collective-permute-done((bf16[1,1,144,1152]{3,2,0,1:T(8,128)(2,1)}, bf16[1,1,144,1152]{3,2,0,1:T(8,128)(2,1)S(1)}, u32[]{:S(2)}, u32[]{:S(2)}) %collective-permute-start.5) | collective-permute-done | bytes 331808 | tf_op jit(solution)/shard_map/ppermute | solution.py:30
  61.9 10.6 %collective-permute-done.6 = bf16[2,128,1024]{2,1,0:T(8,128)(2,1)} collective-permute-done((bf16[2,128,1024]{2,1,0:T(8,128)(2,1)}, bf16[2,128,1024]{2,1,0:T(8,128)(2,1)}, u32[]{:S(2)}, u32[]{:S(2)}) %collective-permute-start.6) | collective-permute-done | bytes 524320 | tf_op jit(solution)/shard_map/ppermute | solution.py:21
  73.5 8.4 %collective-permute-done.9 = bf16[2,1,144,1152]{3,2,0,1:T(8,128)(2,1)} collective-permute-done((bf16[2,1,144,1152]{3,2,0,1:T(8,128)(2,1)S(1)}, bf16[2,1,144,1152]{3,2,0,1:T(8,128)(2,1)}, u32[]{:S(2)}, u32[]{:S(2)}) %collective-permute-start.9) | collective-permute-done | bytes 663584 | tf_op jit(solution)/shard_map/ppermute | solution.py:30
  115.5 46.2 %conditional.7 = (f32[1024,1]{0,1:T(1,128)}, bf16[1024,2048]{1,0:T(8,128)(2,1)S(1)}, bf16[4,256,8,64]{1,3,2,0:T(8,128)(2,1)}, bf16[4,256,64]{1,2,0:T(8,128)(2,1)...) conditional(s32[]{:T(128)} %convert_element_type.396, () %tuple.87, ...), branch_computations={%region_1.2_spmd, %region_2.6_spmd} | conditional | flops 5406032896 | bytes 196342176 | solution.py:56
  184.0 30.9 %collective-permute-done.24 = bf16[1,2,128,1408]{3,2,0,1:T(8,128)(2,1)S(1)} collective-permute-done((bf16[1,2,128,1408]{3,2,0,1:T(8,128)(2,1)S(1)}, bf16[1,2,128,1408]{3,2,0,1:T(8,128)(2,1)S(1)}, u32[]{:S(2)}, u32[]{:S(2)}) %collective-permute-start.24) | collective-permute-done | bytes 720928 | tf_op jit(solution)/shard_map/ppermute | solution.py:30
  224.4 22.9 %collective-permute-done.28 = bf16[2,128,2048]{2,1,0:T(8,128)(2,1)S(1)} collective-permute-done((bf16[2,128,2048]{2,1,0:T(8,128)(2,1)S(1)}, bf16[2,128,2048]{2,1,0:T(8,128)(2,1)S(1)}, u32[]{:S(2)}, u32[]{:S(2)}) %collective-permute-start.28) | collective-permute-done | bytes 1048608 | tf_op jit(solution)/shard_map/ppermute | solution.py:17
  263.8 9.3 %shard_map.260 = bf16[2,4,2,128,2816]{4,3,2,1,0:T(8,128)(2,1)} custom-call(s32[5]{0:T(128)} %xor_select_fusion.where_ref, bf16[4,128,2816]{2,1,0:T(8,128)(2,1)} %copy-done.16, bf16[4,128,2816]{2,1,0:T(8,128)(2,1)} %copy-done.53, bf16[4,128,2816]{2,1,0:T(8,128)(2,1)} %copy-done.15, bf16[4,128,2816]{2,1,0:T(8,128)(2,1)} %copy-done.52), custom_call_target="tpu_custom_call" | custom-call | bytes 23068672 | tf_op jit(solution)/shard_map/pallas_call | solution.py:167
  285.9 28.0 %conditional.8 = (f32[1024,2816]{1,0:T(8,128)}, bf16[1024,1408]{1,0:T(8,128)(2,1)}, bf16[4,2,128,1408]{3,2,1,0:T(8,128)(2,1)}) conditional(s32[]{:T(128)} %convert_element_type.396, () %tuple.98, (bf16[1024,2048]{1,0:T(8,128)(2,1)S(1)}, bf16[2048,2816]{1,0:T(8,128)(2,1)S(1)}, bf16[1024,2048]{1,0:T(8,128)(2,1)S(1)}) %tuple.210), branch_computations={%region_7.8_spmd, %region_8.9_spmd} | conditional | flops 14774042624 | bytes 49545240 | solution.py:56
  285.9 15.0 %fusion.135 = f32[1024,2816]{1,0:T(8,128)} fusion(bf16[1024,2048]{1,0:T(8,128)(2,1)S(1)} %get-tuple-element.81, bf16[2048,2816]{1,0:T(8,128)(2,1)S(1)} %get-tuple-element.82), kind=kOutput, calls=%fused_computation.319 | convolution fusion | flops 11811160064 | bytes 27262976 | tf_op jit(solution)/shard_map/cond/branch_1_fun/dot_general | solution.py:457
  325.6 38.0 %conditional.9 = (bf16[1024,1408]{1,0:T(8,128)(2,1)S(1)}, bf16[1024,1408]{1,0:T(8,128)(2,1)}, bf16[2,512,2048]{2,1,0:T(8,128)(2,1)S(1)}, bf16[4,2,128,1408]{3,2,1,0:T(8,128)(2,1)S(1)}) conditional(s32[]{:T(128)} %convert_element_type.396, () %tuple.97, (bf16[1024,2048]{1,0:T(8,128)(2,1)}, bf16[2048,1408]{1,0:T(8,128)(2,1)}, ...), branch_computations={%region_9.10_spmd, %region_10.11_spmd} | conditional | flops 20703346688 | bytes 79691864 | solution.py:56
  325.6 15.1 %multiply_convert_fusion = (bf16[1024,1408]{1,0:T(8,128)(2,1)}, bf16[1024,1408]{1,0:T(8,128)(2,1)S(1)}) fusion(f32[1024,2816]{1,0:T(8,128)} %get-tuple-element.86, bf16[1024,2048]{1,0:T(8,128)(2,1)} %get-tuple-element.84, bf16[2048,1408]{1,0:T(8,128)(2,1)} %get-tuple-element.85), kind=kOutput, calls=%fused_computation.43 | convolution fusion | flops 5924323328 | bytes 27262976 | tf_op jit(solution)/shard_map/cond/branch_1_fun/dot_general | solution.py:468
  340.6 16.9 %fusion.32 = bf16[1024,2048]{1,0:T(8,128)(2,1)S(1)} fusion(bf16[2048,2816]{1,0:T(8,128)(2,1)} %get-tuple-element.87, bf16[1024,1408]{1,0:T(8,128)(2,1)} %get-tuple-element.681, bf16[1024,1408]{1,0:T(8,128)(2,1)S(1)} %get-tuple-element.680), kind=kOutput, calls=%fused_computation.46 | convolution fusion | flops 11824791552 | bytes 21495808 | tf_op jit(solution)/shard_map/cond/branch_1_fun/dot_general | solution.py:291
  367.5 11.6 %conditional.10 = (bf16[4,2,128,1408]{3,2,1,0:T(8,128)(2,1)}, bf16[4,2,128,1408]{3,2,1,0:T(8,128)(2,1)}) conditional(s32[]{:T(128)} %convert_element_type.396, () %tuple.103, (bf16[1024,2048]{1,0:T(8,128)(2,1)}, bf16[1024,1408]{1,0:T(8,128)(2,1)S(1)}) %tuple.208), branch_computations={%region_11.12_spmd, %region_12.13_spmd} | conditional | flops 5908463616 | bytes 32505900 | solution.py:56
  393.5 20.8 %conditional.11 = (bf16[4,2,128,1408]{3,2,1,0:T(8,128)(2,1)}, bf16[4,2,128,1408]{3,2,1,0:T(8,128)(2,1)S(1)}, bf16[2,512,2048]{2,1,0:T(8,128)(2,1)S(1)}) conditional(s32[]{:T(128)} %convert_element_type.396, () %tuple.94, (bf16[1024,2048]{1,0:T(8,128)(2,1)S(1)}, bf16[1024,1408]{1,0:T(8,128)(2,1)}, bf16[1024,1408]{1,0:T(8,128)(2,1)}, ...), branch_computations={%region_13.14_spmd, %region_14.15_spmd} | conditional | flops 11816140800 | bytes 28573720 | solution.py:56
  406.0 8.3 %convolution_convert_fusion.5 = bf16[1024,2048]{1,0:T(8,128)(2,1)S(1)} fusion(bf16[1024,1408]{1,0:T(8,128)(2,1)} %get-tuple-element.93, bf16[2048,1408]{1,0:T(8,128)(2,1)S(1)} %get-tuple-element.94), kind=kOutput, calls=%fused_computation.54 | convolution fusion | flops 5907677184 | bytes 12845056 | tf_op jit(solution)/shard_map/cond/branch_1_fun/dot_general | solution.py:291
  437.6 18.7 %collective-permute-done.45 = bf16[2,2,128,1408]{3,2,1,0:T(8,128)(2,1)} collective-permute-done((bf16[2,2,128,1408]{3,2,1,0:T(8,128)(2,1)}, bf16[2,2,128,1408]{3,2,1,0:T(8,128)(2,1)}, u32[]{:S(2)}, u32[]{:S(2)}) %collective-permute-start.45) | collective-permute-done | bytes 1441824 | tf_op jit(solution)/shard_map/ppermute | solution.py:30
  488.9 25.5 %conditional.12 = (bf16[4,256,8,64]{1,0,3,2:T(4,128)(2,1)S(1)}, bf16[4,8,256,256]{2,3,1,0:T(8,128)(2,1)}, bf16[4,2,128,512]{3,2,1,0:T(8,128)(2,1)}, bf16[4,2,128,512]{3,2,1,0:T(8,128)(2,1)}) conditional(s32[]{:T(128)} %convert_element_type.396, () %tuple.112, (bf16[2,512,2048]{2,1,0:T(8,128)(2,1)S(1)}, bf16[2048,512]{1,0:T(8,128)(2,1)S(1)}, ...), branch_computations={%region_16.17_spmd, %region_17.19_spmd} | conditional | flops 4841807872 | bytes 75628688 | solution.py:56
  496.5 10.0 %fusion.43 = bf16[4,8,256,256]{2,3,1,0:T(8,128)(2,1)} fusion(f32[4,8,256,256]{2,3,1,0:T(8,128)} %get-tuple-element.97, bf16[4,256,8,64]{1,0,3,2:T(4,128)(2,1)S(1)} %reshape.379, bf16[4,256,64,1]{1,0,2,3:T(4,128)(2,1)S(1)} %bitcast.360), kind=kOutput, calls=%fused_computation.63 | convolution fusion | flops 545267968 | bytes 13762560 | tf_op jit(solution)/shard_map/cond/branch_1_fun/sub | solution.py:521
  514.4 14.0 %collective-permute-done.50 = bf16[2,2,128,1408]{3,2,1,0:T(8,128)(2,1)} collective-permute-done((bf16[2,2,128,1408]{3,2,1,0:T(8,128)(2,1)}, bf16[2,2,128,1408]{3,2,1,0:T(8,128)(2,1)}, u32[]{:S(2)}, u32[]{:S(2)}) %collective-permute-start.50) | collective-permute-done | bytes 1441824 | tf_op jit(solution)/shard_map/ppermute | solution.py:30
  542.2 29.8 %conditional.13 = (bf16[1024,640]{0,1:T(8,128)(2,1)}, bf16[2,512,2048]{2,1,0:T(8,128)(2,1)}, bf16[1,2,4,2,128]{4,3,2,1,0:T(2,128)(2,1)S(1)}) conditional(s32[]{:T(128)} %convert_element_type.396, () %tuple.111, (bf16[4,256,64]{1,2,0:T(8,128)(2,1)S(1)}, bf16[4,8,256,256]{2,3,1,0:T(8,128)(2,1)}, f32[4,256,64]{1,2,0:T(8,128)S(1)}, ...), branch_computations={%region_19.20_spmd, %region_20.22_spmd} | conditional | flops 3503650816 | bytes 80879672 | solution.py:56
  581.7 11.3 %collective-permute-done.57 = bf16[2,2,128,512]{3,2,1,0:T(8,128)(2,1)S(1)} collective-permute-done((bf16[2,2,128,512]{3,2,1,0:T(8,128)(2,1)S(1)}, bf16[2,2,128,512]{3,2,1,0:T(8,128)(2,1)S(1)}, u32[]{:S(2)}, u32[]{:S(2)}) %collective-permute-start.57) | collective-permute-done | bytes 524320 | tf_op jit(solution)/shard_map/ppermute | solution.py:30
  604.3 10.2 %collective-permute-done.58 = bf16[2,128,1024]{2,1,0:T(8,128)(2,1)S(1)} collective-permute-done((bf16[2,128,1024]{2,1,0:T(8,128)(2,1)S(1)}, bf16[2,128,1024]{2,1,0:T(8,128)(2,1)S(1)}, u32[]{:S(2)}, u32[]{:S(2)}) %collective-permute-start.58) | collective-permute-done | bytes 524320 | tf_op jit(solution)/shard_map/ppermute | solution.py:21
  626.9 15.7 %collective-permute-done.64 = bf16[1,2,144,640]{3,2,1,0:T(8,128)(2,1)S(1)} collective-permute-done((bf16[1,2,144,640]{3,2,1,0:T(8,128)(2,1)S(1)}, bf16[1,2,144,640]{3,2,1,0:T(8,128)(2,1)S(1)}, u32[]{:S(2)}, u32[]{:S(2)}) %collective-permute-start.64) | collective-permute-done | bytes 368672 | tf_op jit(solution)/shard_map/ppermute | solution.py:30
  (551 shorter events, 444.7 us)
Async XLA Ops:
  94.0 67.7 %collective-permute-start.17 = (bf16[2,1,128,2816]{3,2,0,1:T(8,128)(2,1)}, bf16[2,1,128,2816]{3,2,0,1:T(8,128)(2,1)}, u32[]{:S(2)}, u32[]{:S(2)}) collective-permute-start(bf16[2,1,128,2816]{3,2,0,1:T(8,128)(2,1)} %constant_dynamic-update-slice_fusion.7), channel_id=1, source_target_pairs={{0,8},{8,0},{16,24},{24,16},{1,9},{9,1},{17,25},{25,17},{2,10},{10... | collective-permute-start | bytes 4325384 | tf_op jit(solution)/shard_map/ppermute | solution.py:30
  96.2 65.5 %collective-permute-start.15 = (bf16[2,128,2048]{2,1,0:T(8,128)(2,1)}, bf16[2,128,2048]{2,1,0:T(8,128)(2,1)}, u32[]{:S(2)}, u32[]{:S(2)}) collective-permute-start(bf16[2,128,2048]{2,1,0:T(8,128)(2,1)} %bitcast.49), channel_id=1, source_target_pairs={{0,1},{1,0},{2,3},{3,2},{4,5},{5,4},{6,7},{7,6},{8,9},{9,8},{10,11... | collective-permute-start | bytes 3145736 | tf_op jit(solution)/shard_map/ppermute | solution.py:17
  100.3 61.3 %collective-permute-start.16 = (bf16[2,128,2048]{2,1,0:T(8,128)(2,1)}, bf16[2,128,2048]{2,1,0:T(8,128)(2,1)}, u32[]{:S(2)}, u32[]{:S(2)}) collective-permute-start(bf16[2,128,2048]{2,1,0:T(8,128)(2,1)} %bitcast.49), channel_id=1, source_target_pairs={{0,4},{4,0},{1,5},{5,1},{2,6},{6,2},{3,7},{7,3},{8,12},{12,8},{9,1... | collective-permute-start | bytes 3145736 | tf_op jit(solution)/shard_map/ppermute | solution.py:21
  111.0 50.7 %collective-permute-start.18 = (bf16[1,1,128,2816]{3,2,0,1:T(8,128)(2,1)}, bf16[1,1,128,2816]{3,2,0,1:T(8,128)(2,1)}, u32[]{:S(2)}, u32[]{:S(2)}) collective-permute-start(bf16[1,1,128,2816]{3,2,0,1:T(8,128)(2,1)} %bitcast.50), channel_id=1, source_target_pairs={{0,16},{8,24},{16,0},{24,8},{1,17},{9,25},{17,1},{25,9},{2,18},{10... | collective-permute-start | bytes 2162696 | tf_op jit(solution)/shard_map/ppermute | solution.py:30
  113.9 47.8 %collective-permute-start.14 = (bf16[128,1408]{1,0:T(8,128)(2,1)}, bf16[128,1408]{1,0:T(8,128)(2,1)}, u32[]{:S(2)}, u32[]{:S(2)}) collective-permute-start(bf16[128,1408]{1,0:T(8,128)(2,1)} %get-tuple-element.316), channel_id=1, source_target_pairs={{0,4},{4,0},{1,5},{5,1},{2,6},{6,2},{3,7},{7,3},{8,12},{12,8},{9,1... | collective-permute-start | bytes 1081352 | tf_op jit(solution)/shard_map/ppermute | solution.py:21
  164.6 50.4 %collective-permute-start.23 = (bf16[2,1,128,2816]{3,2,0,1:T(8,128)(2,1)S(1)}, bf16[2,1,128,2816]{3,2,0,1:T(8,128)(2,1)S(1)}, u32[]{:S(2)}, u32[]{:S(2)}) collective-permute-start(bf16[2,1,128,2816]{3,2,0,1:T(8,128)(2,1)S(1)} %constant_dynamic-update-slice_fusion.9), channel_id=1, source_target_pairs={{0,8},{8,0},{16,24},{24,16},{1,9},{9,1},{17,25},{25,17},{2,10},{10... | collective-permute-start | bytes 4325384 | tf_op jit(solution)/shard_map/ppermute | solution.py:30
  180.1 34.8 %collective-permute-start.22 = (bf16[2,128,2048]{2,1,0:T(8,128)(2,1)S(1)}, bf16[2,128,2048]{2,1,0:T(8,128)(2,1)S(1)}, u32[]{:S(2)}, u32[]{:S(2)}) collective-permute-start(bf16[2,128,2048]{2,1,0:T(8,128)(2,1)S(1)} %pad_maximum_fusion.6), channel_id=1, source_target_pairs={{0,4},{4,0},{1,5},{5,1},{2,6},{6,2},{3,7},{7,3},{8,12},{12,8},{9,1... | collective-permute-start | bytes 3145736 | tf_op jit(solution)/shard_map/ppermute | solution.py:21
  182.0 33.0 %collective-permute-start.20 = (bf16[2,128,2048]{2,1,0:T(8,128)(2,1)S(1)}, bf16[2,128,2048]{2,1,0:T(8,128)(2,1)S(1)}, u32[]{:S(2)}, u32[]{:S(2)}) collective-permute-start(bf16[2,128,2048]{2,1,0:T(8,128)(2,1)S(1)} %pad_maximum_fusion.5), channel_id=1, source_target_pairs={{0,1},{1,0},{2,3},{3,2},{4,5},{5,4},{6,7},{7,6},{8,9},{9,8},{10,11... | collective-permute-start | bytes 3145736 | tf_op jit(solution)/shard_map/ppermute | solution.py:17
  215.2 37.4 %collective-permute-start.26 = (bf16[4,128,2816]{2,1,0:T(8,128)(2,1)S(1)}, bf16[4,128,2816]{2,1,0:T(8,128)(2,1)S(1)}, u32[]{:S(2)}, u32[]{:S(2)}) collective-permute-start(bf16[4,128,2816]{2,1,0:T(8,128)(2,1)S(1)} %maximum_bitcast_fusion.1.peer), channel_id=1, source_target_pairs={{0,2},{2,0},{1,3},{3,1},{4,6},{6,4},{5,7},{7,5},{8,10},{10,8},{9,1... | collective-permute-start | bytes 8650760 | tf_op jit(solution)/shard_map/ppermute | solution.py:25
  218.3 34.3 %collective-permute-start.25 = (bf16[4,128,2816]{2,1,0:T(8,128)(2,1)S(1)}, bf16[4,128,2816]{2,1,0:T(8,128)(2,1)S(1)}, u32[]{:S(2)}, u32[]{:S(2)}) collective-permute-start(bf16[4,128,2816]{2,1,0:T(8,128)(2,1)S(1)} %maximum_bitcast_fusion.own), channel_id=1, source_target_pairs={{0,2},{2,0},{1,3},{3,1},{4,6},{6,4},{5,7},{7,5},{8,10},{10,8},{9,1... | collective-permute-start | bytes 8650760 | tf_op jit(solution)/shard_map/ppermute | solution.py:25
  218.6 34.0 %collective-permute-start.27 = (bf16[2,2,128,1408]{3,2,0,1:T(8,128)(2,1)S(1)}, bf16[2,2,128,1408]{3,2,0,1:T(8,128)(2,1)S(1)}, u32[]{:S(2)}, u32[]{:S(2)}) collective-permute-start(bf16[2,2,128,1408]{3,2,0,1:T(8,128)(2,1)S(1)} %constant_dynamic-update-slice_fusion.11), channel_id=1, source_target_pairs={{0,8},{8,0},{16,24},{24,16},{1,9},{9,1},{17,25},{25,17},{2,10},{10... | collective-permute-start | bytes 4325384 | tf_op jit(solution)/shard_map/ppermute | solution.py:30
  253.0 60.9 %collective-permute-start.34 = (bf16[4,2,128,1408]{3,2,0,1:T(8,128)(2,1)S(1)}, bf16[4,2,128,1408]{3,2,0,1:T(8,128)(2,1)}, u32[]{:S(2)}, u32[]{:S(2)}) collective-permute-start(bf16[4,2,128,1408]{3,2,0,1:T(8,128)(2,1)S(1)} %constant_dynamic-update-slice_fusion.13), channel_id=1, source_target_pairs={{0,2},{2,0},{1,3},{3,1},{4,6},{6,4},{5,7},{7,5},{8,10},{10,8},{9,1... | collective-permute-start | bytes 8650760 | tf_op jit(solution)/shard_map/ppermute | solution.py:25
  313.9 49.8 %collective-permute-start.35 = (bf16[4,2,128,1408]{3,2,1,0:T(8,128)(2,1)}, bf16[4,2,128,1408]{3,2,1,0:T(8,128)(2,1)}, u32[]{:S(2)}, u32[]{:S(2)}) collective-permute-start(bf16[4,2,128,1408]{3,2,1,0:T(8,128)(2,1)} %get-tuple-element.365), channel_id=1, source_target_pairs={{0,2},{2,0},{1,3},{3,1},{4,6},{6,4},{5,7},{7,5},{8,10},{10,8},{9,1... | collective-permute-start | bytes 8650760 | tf_op jit(solution)/shard_map/ppermute | solution.py:25
  392.0 45.6 %collective-permute-start.44 = (bf16[2,2,128,1408]{3,2,1,0:T(8,128)(2,1)}, bf16[2,2,128,1408]{3,2,1,0:T(8,128)(2,1)}, u32[]{:S(2)}, u32[]{:S(2)}) collective-permute-start(bf16[2,2,128,1408]{3,2,1,0:T(8,128)(2,1)} %fusion.104), channel_id=1, source_target_pairs={{0,8},{8,0},{16,24},{24,16},{1,9},{9,1},{17,25},{25,17},{2,10},{10... | collective-permute-start | bytes 4325384 | tf_op jit(solution)/shard_map/ppermute | solution.py:30
  416.4 39.9 %collective-permute-start.41 = (bf16[4,2,128,1408]{3,2,1,0:T(8,128)(2,1)}, bf16[4,2,128,1408]{3,2,1,0:T(8,128)(2,1)}, u32[]{:S(2)}, u32[]{:S(2)}) collective-permute-start(bf16[4,2,128,1408]{3,2,1,0:T(8,128)(2,1)} %get-tuple-element.383), channel_id=1, source_target_pairs={{0,2},{2,0},{1,3},{3,1},{4,6},{6,4},{5,7},{7,5},{8,10},{10,8},{9,1... | collective-permute-start | bytes 8650760 | tf_op jit(solution)/shard_map/ppermute | solution.py:25
  421.3 35.1 %collective-permute-start.45 = (bf16[2,2,128,1408]{3,2,1,0:T(8,128)(2,1)}, bf16[2,2,128,1408]{3,2,1,0:T(8,128)(2,1)}, u32[]{:S(2)}, u32[]{:S(2)}) collective-permute-start(bf16[2,2,128,1408]{3,2,1,0:T(8,128)(2,1)} %fusion.105), channel_id=1, source_target_pairs={{0,8},{8,0},{16,24},{24,16},{1,9},{9,1},{17,25},{25,17},{2,10},{10... | collective-permute-start | bytes 4325384 | tf_op jit(solution)/shard_map/ppermute | solution.py:30
  464.5 49.9 %collective-permute-start.51 = (bf16[1,2,128,1408]{3,2,1,0:T(8,128)(2,1)}, bf16[1,2,128,1408]{3,2,1,0:T(8,128)(2,1)}, u32[]{:S(2)}, u32[]{:S(2)}) collective-permute-start(bf16[1,2,128,1408]{3,2,1,0:T(8,128)(2,1)} %dynamic-slice_convert_fusion.3), channel_id=1, source_target_pairs={{0,16},{8,24},{16,0},{24,8},{1,17},{9,25},{17,1},{25,9},{2,18},{10... | collective-permute-start | bytes 2162696 | tf_op jit(solution)/shard_map/ppermute | solution.py:30
  464.7 63.7 %collective-permute-start.50 = (bf16[2,2,128,1408]{3,2,1,0:T(8,128)(2,1)}, bf16[2,2,128,1408]{3,2,1,0:T(8,128)(2,1)}, u32[]{:S(2)}, u32[]{:S(2)}) collective-permute-start(bf16[2,2,128,1408]{3,2,1,0:T(8,128)(2,1)} %fusion.106), channel_id=1, source_target_pairs={{0,8},{8,0},{16,24},{24,16},{1,9},{9,1},{17,25},{25,17},{2,10},{10... | collective-permute-start | bytes 4325384 | tf_op jit(solution)/shard_map/ppermute | solution.py:30
  472.5 108.4 %collective-permute-start.54 = (bf16[1,2,128,1408]{3,2,1,0:T(8,128)(2,1)}, bf16[1,2,128,1408]{3,2,1,0:T(8,128)(2,1)}, u32[]{:S(2)}, u32[]{:S(2)}) collective-permute-start(bf16[1,2,128,1408]{3,2,1,0:T(8,128)(2,1)} %dynamic-slice_convert_fusion.2), channel_id=1, source_target_pairs={{0,16},{8,24},{16,0},{24,8},{1,17},{9,25},{17,1},{25,9},{2,18},{10... | collective-permute-start | bytes 2162696 | tf_op jit(solution)/shard_map/ppermute | solution.py:30
  528.4 48.8 %collective-permute-start.56 = (bf16[4,2,128,512]{3,2,1,0:T(8,128)(2,1)}, bf16[4,2,128,512]{3,2,1,0:T(8,128)(2,1)}, u32[]{:S(2)}, u32[]{:S(2)}) collective-permute-start(bf16[4,2,128,512]{3,2,1,0:T(8,128)(2,1)} %get-tuple-element.425), channel_id=1, source_target_pairs={{0,2},{2,0},{1,3},{3,1},{4,6},{6,4},{5,7},{7,5},{8,10},{10,8},{9,1... | collective-permute-start | bytes 3145736 | tf_op jit(solution)/shard_map/ppermute | solution.py:25
  532.0 49.7 %collective-permute-start.55 = (bf16[1,2,128,1408]{3,2,1,0:T(8,128)(2,1)}, bf16[1,2,128,1408]{3,2,1,0:T(8,128)(2,1)}, u32[]{:S(2)}, u32[]{:S(2)}) collective-permute-start(bf16[1,2,128,1408]{3,2,1,0:T(8,128)(2,1)} %dynamic-slice_convert_fusion.1), channel_id=1, source_target_pairs={{0,16},{8,24},{16,0},{24,8},{1,17},{9,25},{17,1},{25,9},{2,18},{10... | collective-permute-start | bytes 2162696 | tf_op jit(solution)/shard_map/ppermute | solution.py:30
  535.1 46.5 %collective-permute-start.53 = (bf16[2,128,2048]{2,1,0:T(8,128)(2,1)}, bf16[2,128,2048]{2,1,0:T(8,128)(2,1)}, u32[]{:S(2)}, u32[]{:S(2)}) collective-permute-start(bf16[2,128,2048]{2,1,0:T(8,128)(2,1)} %pad_maximum_fusion.10), channel_id=1, source_target_pairs={{0,4},{4,0},{1,5},{5,1},{2,6},{6,2},{3,7},{7,3},{8,12},{12,8},{9,1... | collective-permute-start | bytes 3145736 | tf_op jit(solution)/shard_map/ppermute | solution.py:21
  539.0 42.7 %collective-permute-start.52 = (bf16[2,128,2048]{2,1,0:T(8,128)(2,1)}, bf16[2,128,2048]{2,1,0:T(8,128)(2,1)}, u32[]{:S(2)}, u32[]{:S(2)}) collective-permute-start(bf16[2,128,2048]{2,1,0:T(8,128)(2,1)} %pad_maximum_fusion.9), channel_id=1, source_target_pairs={{0,1},{1,0},{2,3},{3,2},{4,5},{5,4},{6,7},{7,6},{8,9},{9,8},{10,11... | collective-permute-start | bytes 3145736 | tf_op jit(solution)/shard_map/ppermute | solution.py:17
  593.3 33.5 %collective-permute-start.65 = (bf16[1,2,128,512]{3,2,1,0:T(8,128)(2,1)S(1)}, bf16[1,2,128,512]{3,2,1,0:T(8,128)(2,1)S(1)}, u32[]{:S(2)}, u32[]{:S(2)}) collective-permute-start(bf16[1,2,128,512]{3,2,1,0:T(8,128)(2,1)S(1)} %dynamic-slice_convert_fusion.9), channel_id=1, source_target_pairs={{0,16},{8,24},{16,0},{24,8},{1,17},{9,25},{17,1},{25,9},{2,18},{10... | collective-permute-start | bytes 786440 | tf_op jit(solution)/shard_map/ppermute | solution.py:30
  (141 other events, 1668.0 us)

commit v3 on v2

--- a/solution.py
+++ b/solution.py
@@ -65,24 +65,27 @@
     return own, swap_x(own), swap_y(own)
 
 
-def gather_diag(near):
-    _, from_x, from_y = near
-    half = from_x.shape[-1] // 2
-    return swap_y(from_x[..., :half]), swap_x(from_y[..., half:])
+def diag_parts(near):
+    half = near[1].shape[-1] // 2
+    return near[1][..., :half], near[2][..., half:]
+
+
+def gather_diag(parts):
+    return swap_y(parts[0]), swap_x(parts[1])
 
 
 def gather_join(near, diag):
     return jnp.concatenate(tuple(near) + (jnp.concatenate(diag, axis=-1),), axis=1)
 
 
-def gather_far(near):
-    return gather_join(near, gather_diag(near))
-
-
-def scatter_far(part):
+def far_parts(part):
     m, rows, f = part.shape
     diag = part[:, 3 * rows // 4 :]
-    return swap_y(diag[..., : f // 2]), swap_x(diag[..., f // 2 :])
+    return diag[..., : f // 2], diag[..., f // 2 :]
+
+
+def scatter_far(parts):
+    return swap_y(parts[0]), swap_x(parts[1])
 
 
 def scatter_prep(part, far):
@@ -124,12 +127,20 @@
     return held, swap_z(held, far_bits()[0])
 
 
+def z_lead(pair):
+    bits = far_bits()[1:-1]
+    if not bits:
+        return pair
+    held = jnp.concatenate(pair, axis=0)
+    for bit in bits:
+        held = jnp.concatenate([held, swap_z(held, bit)], axis=0)
+    half = held.shape[0] // 2
+    return held[:half], held[half:]
+
+
 def z_rest(pair):
-    held = jnp.concatenate(pair, axis=0)
-    bits = far_bits()[1:]
-    for bit in bits[:-1]:
-        held = jnp.concatenate([held, swap_z(held, bit)], axis=0)
-    return held, swap_z(held, bits[-1])
+    held = jnp.concatenate(z_lead(pair), axis=0)
+    return held, swap_z(held, 1)
 
 
 def both(pair):
@@ -138,7 +149,7 @@
 
 def assemble(streams, z, y, extra=0, split=()):
     order = np.array(z_order() + [0], np.int32)
-    n, rows, cols = streams[0].shape
+    n, _, rows, cols = streams[0][0].shape
     block = rows - extra
     last = np.arange(n + 1) == n
     where = jnp.where(jnp.asarray(last), y, jnp.asarray(order) ^ z)
@@ -150,11 +161,11 @@
         yy = where_ref[n]
         for ref, at_c, at_y in ((own, 0, yy), (own_c, 1, yy), (peer, 0, 1 - yy), (peer_c, 1, 1 - yy)):
             if not extra:
-                more[0][at_c, 0, at_y] = ref[0]
+                more[0][at_c, 0, at_y] = ref[0, 0]
                 continue
             for out, (lo, hi) in zip(more, spans):
-                out[at_c, 0, at_y] = ref[0, :block, lo:hi]
-            more[-1][at_c, 0, at_y] = ref[0, block:, :128]
+                out[at_c, 0, at_y] = ref[0, 0, :block, lo:hi]
+            more[-1][at_c, 0, at_y] = ref[0, 0, block:, :128]
 
     out_shape = [jax.ShapeDtypeStruct((2, n, 2, block, hi - lo), BF) for lo, hi in spans]
     out_specs = [
@@ -170,11 +181,13 @@
         grid_spec=pltpu.PrefetchScalarGridSpec(
             num_scalar_prefetch=1,
             grid=(n,),
-            in_specs=[pl.BlockSpec((1, rows, cols), lambda i, at: (i, 0, 0))] * 4,
+            in_specs=[
+                pl.BlockSpec((1, 1, rows, cols), lambda i, at, k=k: (i, k, 0, 0)) for _, k in streams
+            ],
             out_specs=out_specs,
         ),
         cost_estimate=pl.CostEstimate(flops=0, bytes_accessed=moved, transcendentals=0),
-    )(where, *streams)
+    )(where, *(s for s, _ in streams))
 
 
 def grad_half(index, left, right):
@@ -188,32 +201,52 @@
     return a.astype(F32) + b.astype(F32)
 
 
-def reduce_step(grad, z, bit):
-    n, _, block, cols = grad.shape
-    pairs = grad.reshape(n // 2, 2, 2, block, cols)
+def halve(pair, z, bit):
+    n, _, block, cols = pair[0].shape
+    pairs = [p.reshape(n // 2, 2, 2, block, cols) for p in pair]
     here = (z // bit) % 2
-    return pick(pairs, 1, here), swap_z(pick(pairs, 1, 1 - here).astype(BF), bit)
-
-
-def reduce_near(pair, z):
-    return reduce_step(add(*pair), z, 1)
-
-
-def reduce_far(pair, z):
-    grad = add(*pair)
-    bits = far_bits()[:-1][::-1]
-    for bit in bits[:-1]:
-        grad = add(*reduce_step(grad, z, bit))
-    return reduce_step(grad, z, bits[-1])
+    keep = add(*(pick(p, 1, here) for p in pairs))
+    send = add(*(pick(p, 1, 1 - here) for p in pairs))
+    return keep, send.astype(pair[1].dtype)
+
+
+def halve_near(pair, z):
+    return halve(pair, z, 1)
+
+
+def far_last():
+    return far_bits()[0]
+
+
+def far_steps(pair, z):
+    for bit in far_bits()[1:-1][::-1]:
+        pair = swapped(halve(pair, z, bit), bit)
+    return pair
+
+
+def halve_far(pair, z):
+    return halve(far_steps(pair, z), z, far_last())
+
+
+def swapped(halves, bit):
+    return halves[0], swap_z(halves[1], bit)
 
 
 def reduce_y(pair, y):
-    grad = add(*pair)[0]
-    return pick(grad, 0, y), swap_y(pick(grad, 0, 1 - y).astype(BF)).astype(F32)
+    keep, send = (add(*(pick(p[0], 0, at) for p in pair)) for at in (y, 1 - y))
+    return keep, swap_y(send.astype(pair[1].dtype))
+
+
+def side_by_side(low, high):
+    return tuple(jnp.concatenate(p, axis=-1) for p in zip(low, high))
+
+
+def columns(halves, lo, hi):
+    return tuple(h[..., lo:hi] for h in halves)
 
 
 def join(parts, y):
-    mine, got = parts
+    mine, got = parts[0], parts[1].astype(F32)
     first = y == 0
     return jnp.concatenate([jnp.where(first, mine, got), jnp.where(first, got, mine)], axis=1)
 
@@ -275,12 +308,6 @@
         bit *= 2
     mine = pick(grad[0], 0, y)
     return mine, swap_y(pick(grad[0], 0, 1 - y).astype(BF)).astype(F32)
-
-
-def join(parts, y):
-    mine, got = parts
-    first = y == 0
-    return jnp.concatenate([jnp.where(first, mine, got), jnp.where(first, got, mine)], axis=1)
 
 
 def rows_rows(left, right):
@@ -358,34 +385,37 @@
     own_far = z_first(pack_attn(y))
     attn_theirs = swap_y(pack_attn(1 - y))
     other_ids = swap_y(segment_ids[:, 0])
-    attn_theirs, other_ids, hid, *own_far = meet(attn_theirs, other_ids, hidden_in[:, 0], *own_far)
+    own_far, attn_theirs, other_ids, hid = meet(own_far, attn_theirs, other_ids, hidden_in[:, 0])
     peer_far = z_first(attn_theirs)
+    attn_own = z_rest(own_far)
     hid = regroup(hid, block, c)
     hid_near = gather_near(hid)
-    attn_own = z_rest(own_far)
-    more = meet(*hid_near, *peer_far, pack_gu(y), pack_gu(1 - y))
-    hid_near, peer_far, gu_mine, gu_give = more[:3], more[3:5], more[5], more[6]
-    hid_diag = gather_diag(hid_near)
+    peer_far, attn_own, hid_near, hid_parts, gu_mine, gu_give = meet(
+        peer_far, attn_own, hid_near, diag_parts(hid_near), pack_gu(y), pack_gu(1 - y)
+    )
     attn_peer = z_rest(peer_far)
     gu_far = z_first(gu_mine)
-    more = meet(out_cotangent[:, 0], pack_down(1 - y), gu_give, *hid_diag, *attn_own, *attn_peer, *gu_far)
-    cot, down_give, gu_give, hid_diag = *more[:3], more[3:5]
-    attn_own, attn_peer, gu_far = both(more[5:7])[:, 0], both(more[7:9])[:, 0], more[9:]
-    attn_streams = (attn_own, swap_c(attn_own), attn_peer, swap_c(attn_peer))
+    hid_diag = gather_diag(hid_parts)
     gu_theirs = swap_y(gu_give)
+    attn_own = both(attn_own)
+    cot = regroup(out_cotangent[:, 0], block, c)
+    attn_peer, gu_far, hid_diag, gu_theirs, attn_own, cot, down_give = meet(
+        attn_peer, gu_far, hid_diag, gu_theirs, attn_own, cot, pack_down(1 - y)
+    )
+    attn_own_c = swap_c(attn_own)
+    attn_peer = both(attn_peer)
+    attn_peer_c = swap_c(attn_peer)
     hid_all = gather_join(hid_near, hid_diag)
-    attn_w = assemble(attn_streams, z, y, extra, (qkv_cols,))
-    qkv_w, out_w, gains = attn_w
+    gu_own = z_rest(gu_far)
+    gu_peer = z_first(gu_theirs)
+    cot_near = gather_near(cot)
+    down_theirs = swap_y(down_give)
+    attn_streams = ((attn_own, 0), (attn_own_c, 0), (attn_peer, 0), (attn_peer_c, 0))
+    qkv_w, out_w, gains = assemble(attn_streams, z, y, extra, (qkv_cols,))
     qkv_w, out_w = qkv_w.reshape(width, -1), out_w.reshape(width, -1)
     gains = gains[:, :, :, :2, :block].astype(F32)
     gain_a = gains[:, :, :, 0].reshape(width)
     gain_m = gains[:, :, :, 1].reshape(width)
-    hid_all, gu_theirs, qkv_w, out_w, gain_a, gain_m = meet(hid_all, gu_theirs, qkv_w, out_w, gain_a, gain_m)
-    gu_own = z_rest(gu_far)
-    gu_far = z_first(gu_theirs)
-    down_theirs = swap_y(down_give)
-    cot = regroup(cot, block, c)
-    cot_near = gather_near(cot)
 
     length = 2 * toks
     groups = micro * 2
@@ -422,49 +452,66 @@
         attended = jnp.einsum("ghqs,gsd->gqhd", probs.astype(BF), values, preferred_element_type=F32)
         attended = attended.reshape(rows, q_cols).astype(BF)
         attn_part = cols_cols(attended, out_w).astype(BF).reshape(micro, 4 * toks, width)
-        return scale_a, normed_a, queries, keys, values, probs, attended, attn_part
-
-    scale_a, normed_a, queries, keys, values, probs, attended, attn_part = single(
+        return scale_a, normed_a, queries, keys, values, probs, attended, attn_part, far_parts(attn_part)
+
+    scale_a, normed_a, queries, keys, values, probs, attended, attn_part, attn_far = single(
         attention, hid_all, gain_a, qkv_w, out_w, cos, sin, allowed
     )
-    more = meet(attn_part, down_theirs, pack_down(y), *cot_near, *gu_own, *gu_far)
-    attn_part, down_theirs, down_mine, cot_near = *more[:3], more[3:6]
-    gu_own, gu_far = more[6:8], more[8:]
-    attn_far = scatter_far(attn_part)
-    gu_peer = z_rest(gu_far)
-    down_far = z_first(down_mine, down_theirs)
-    attn_near = scatter_near(*scatter_prep(attn_part, attn_far))
-    more = meet(*attn_near, *gu_peer, *down_far, *gu_own, *cot_near)
-    attn_near, gu_peer, down_far, gu_own = more[:2], both(more[2:4])[:, 0], more[4:6], both(more[6:8])[:, 0]
-    cot_near = more[8:]
+    attn_part, attn_far, gu_own, gu_peer, cot_near, down_theirs, down_mine = meet(
+        attn_part, attn_far, gu_own, gu_peer, cot_near, down_theirs, pack_down(y)
+    )
+    attn_far = scatter_far(attn_far)
+    gu_lead = z_lead(gu_peer)
+    gu_low = swap_z(gu_lead[0], 1)
+    ready, gu_low, gu_own = meet(scatter_prep(attn_part, attn_far), gu_low, gu_own)
+    attn_near = scatter_near(*ready)
+    gu_high = swap_z(gu_lead[1], 1)
+    down_own = z_first(down_mine)
+    gu_own = both(gu_own)
+    gu_own_c = swap_c(gu_own)
+    attn_near, gu_high, down_own, gu_own_c = meet(attn_near, gu_high, down_own, gu_own_c)
+    gu_peer = jnp.concatenate([*gu_lead, gu_low, gu_high], axis=0)
     mid = hid.astype(F32) + scatter_sum(attn_part, attn_near)
 
     scale_m = lax.rsqrt(jnp.mean(mid * mid, axis=-1, keepdims=True) + EPS)
     unit_m = mid * scale_m
     normed_near = gather_near((unit_m * gain_m).astype(BF))
-    down = z_rest(down_far)
-    gu_streams = (gu_own, swap_c(gu_own), gu_peer, swap_c(gu_peer))
-    more = meet(*gu_streams, *down, *normed_near, *cot_near)
-    gu_streams, down, normed_near, cot_near = more[:4], both(more[4:6]), more[6:9], more[9:]
-    normed_m = gather_far(normed_near).reshape(rows, width)
-    cot_diag = gather_diag(cot_near)
+    gu_peer_c = swap_c(gu_peer)
+    down_peer = z_first(down_theirs)
+    down_own = z_rest(down_own)
+    normed_near, normed_parts, gu_peer_c, down_peer, down_own = meet(
+        normed_near, diag_parts(normed_near), gu_peer_c, down_peer, down_own
+    )
+    normed_diag = gather_diag(normed_parts)
+    down_peer = z_rest(down_peer)
+    gu_streams = ((gu_own, 0), (gu_own_c, 0), (gu_peer, 0), (gu_peer_c, 0))
     gu_w = assemble(gu_streams, z, y)[0].reshape(width, -1)
-    down_c = swap_c(down)
-    normed_m, gu_w, *cot_diag = meet(normed_m, gu_w, *cot_diag)
-    cot_rows = gather_join(cot_near, cot_diag).reshape(rows, width)
-
-    def feed(normed_m, gu_w, cot_rows):
+    down_own = both(down_own)
+    down_own_c = swap_c(down_own)
+    normed_diag, down_peer, gu_w, down_own_c, cot_parts = meet(
+        normed_diag, down_peer, gu_w, down_own_c, diag_parts(cot_near)
+    )
+    normed_m, cot_parts = meet(gather_join(normed_near, normed_diag).reshape(rows, width), cot_parts)
+    cot_diag = gather_diag(cot_parts)
+
+    def feed(normed_m, gu_w):
         gu = jnp.dot(normed_m, gu_w, preferred_element_type=F32)
         ff = gu.shape[1] // 2
-        inner = (jax.nn.silu(gu[:, :ff]) * gu[:, ff:]).astype(BF)
-        return gu, inner, grad_half(1, cot_rows, inner)
-
-    gu, inner, down_send = single(feed, normed_m, gu_w, cot_rows)
-    down_send, down_c = meet(down_send, down_c)
-    down_got = swap_c(down_send)
-    down_w = assemble((down[:, 0], down_c[:, 0], down[:, 1], down_c[:, 1]), z, y)[0].reshape(width, -1)
-
-    def feed_back(gu, inner, cot_rows, down_w, gu_w):
+        return gu, (jax.nn.silu(gu[:, :ff]) * gu[:, ff:]).astype(BF)
+
+    gu, inner = single(feed, normed_m, gu_w)
+    inner, cot_diag, down_peer = meet(inner, cot_diag, down_peer)
+    down_peer = both(down_peer)
+    down_peer_c = swap_c(down_peer)
+    cot_rows = gather_join(cot_near, cot_diag).reshape(rows, width)
+    down_got = swap_c(grad_half(1, cot_rows, inner))
+    down_streams = ((down_own, 0), (down_own_c, 0), (down_peer, 0), (down_peer_c, 0))
+    down_w = assemble(down_streams, z, y)[0].reshape(width, -1)
+    down_keep = single(lambda a, b: grad_half(0, a, b), cot_rows, inner)
+    gu, down_w, down_halves = meet(gu, down_w, halve_near((down_keep, down_got), z))
+    down_sum = swapped(down_halves, 1)
+
+    def feed_back(gu, cot_rows, down_w, gu_w):
         d_inner = jnp.dot(cot_rows, down_w, preferred_element_type=F32)
         ff = gu.shape[1] // 2
         gate, up = gu[:, :ff], gu[:, ff:]
@@ -473,45 +520,80 @@
         d_up = (d_inner * gate * sig).astype(BF)
         d_gu = jnp.concatenate([d_gate, d_up], axis=1)
         back = cols_cols(d_gu, gu_w).astype(BF)
-        return d_gate, d_up, back.reshape(micro, 4 * toks, width), grad_half(0, cot_rows, inner)
-
-    d_gate, d_up, back_mlp, down_keep = single(feed_back, gu, inner, cot_rows, down_w, gu_w)
-    back_mlp, down_keep, down_got = meet(back_mlp, down_keep, down_got)
-    back_far = scatter_far(back_mlp)
+        back = back.reshape(micro, 4 * toks, width)
+        return d_gate, d_up, back, far_parts(back)
+
+    ff = inner.shape[1]
+    cols = (ff // 256 + 1) * 128 if ff % 256 else ff // 2
+    far = far_bits()[0]
+    d_gate, d_up, back_mlp, back_far = single(feed_back, gu, cot_rows, down_w, gu_w)
+    ff = d_gate.shape[1]
+    cols = (ff // 256 + 1) * 128 if ff % 256 else ff // 2
+    far = far_bits()[0]
+    back_mlp, back_far, d_gate, down_sum = meet(back_mlp, back_far, d_gate, down_sum)
+    back_far = scatter_far(back_far)
 
     def gate_grads(normed_m, d_gate):
         return grad_half(1, normed_m, d_gate), grad_half(0, normed_m, d_gate)
 
     gate_send, gate_keep = single(gate_grads, normed_m, d_gate)
-    gate_send, gate_keep, *back_far = meet(gate_send, gate_keep, *back_far)
+    down_low = halve_far(columns(down_sum, 0, cols), z)
+    down_high = halve_far(columns(down_sum, cols, ff), z)
+    back_far, gate_send, gate_keep, down_low, down_high = meet(
+        back_far, gate_send, gate_keep, down_low, down_high
+    )
     gate_got = swap_c(gate_send)
-    *ready, d_up, gate_keep, gate_got = meet(*scatter_prep(back_mlp, back_far), d_up, gate_keep, gate_got)
+    ready, gate_got = meet(scatter_prep(back_mlp, back_far), gate_got)
     back_near = scatter_near(*ready)
-    down_sum = reduce_near((down_keep, down_got), z)
-    gate_sum = reduce_near((gate_keep, gate_got), z)
-
-    def up_grads(normed_m, d_up, inner, down_w):
+    down_low = swapped(down_low, far)
+    gate_pair = gate_keep, gate_got
+    d_up, gate_low, gate_high = meet(
+        d_up, halve_near(columns(gate_pair, 0, cols), z), halve_near(columns(gate_pair, cols, ff), z)
+    )
+    gate_low = swapped(gate_low, 1)
+
+    def up_grads(normed_m, d_up):
+        return grad_half(1, normed_m, d_up), grad_half(0, normed_m, d_up)
+
+    up_send, up_keep = single(up_grads, normed_m, d_up)
+    back_near, down_low, gate_low, gate_high, down_high, up_send, up_keep = meet(
+        back_near, down_low, gate_low, gate_high, down_high, up_send, up_keep
+    )
+    up_got = swap_c(up_send)
+
+    def mid_back(back_mlp, from_x, from_y, unit_m, scale_m, gain_m, cot):
+        d_normed_m = scatter_sum(back_mlp, (from_x, from_y))
+        d_mid = cot.astype(F32) + norm_back(d_normed_m, unit_m, gain_m, scale_m)
+        return d_mid, d_mid.astype(BF), jnp.sum(d_normed_m * unit_m, axis=(0, 1))
+
+    d_mid, d_mid_low, gain_m_part = single(mid_back, back_mlp, *back_near, unit_m, scale_m, gain_m, cot)
+
+    d_mid_low, up_got, inner = meet(d_mid_low, up_got, inner)
+    d_mid_near = gather_near(d_mid_low)
+    gate_high = swapped(gate_high, 1)
+    down_high = swapped(down_high, far)
+
+    def mlp_out(inner, down_w):
         part = cols_cols(inner, down_w).astype(BF).reshape(micro, 4 * toks, width)
-        return grad_half(1, normed_m, d_up), grad_half(0, normed_m, d_up), part
-
-    up_send, up_keep, mlp_part = single(up_grads, normed_m, d_up, inner, down_w)
-    up_send, up_keep, mlp_part, *back_near = meet(up_send, up_keep, mlp_part, *back_near)
-    up_got = swap_c(up_send)
-    d_normed_m = scatter_sum(back_mlp, back_near)
-    gain_m_part = jnp.sum(d_normed_m * unit_m, axis=(0, 1))
-    d_mid = cot.astype(F32) + norm_back(d_normed_m, unit_m, gain_m, scale_m)
-
-    d_mid_near = gather_near(d_mid.astype(BF))
-    more = meet(up_keep, up_got, *d_mid_near, *down_sum, *gate_sum)
-    up_keep, up_got, d_mid_near, down_sum, gate_sum = *more[:2], more[2:5], more[5:7], more[7:]
-    d_mid_diag = gather_diag(d_mid_near)
-    up_sum = reduce_near((up_keep, up_got), z)
-    down_sum = reduce_far(down_sum, z)
-    more = meet(mlp_part, *d_mid_diag, *d_mid_near)
-    mlp_part, d_mid_diag, d_mid_near = more[0], more[1:3], more[3:]
-    gate_sum = reduce_far(gate_sum, z)
-    mlp_far = scatter_far(mlp_part)
+        return part, far_parts(part)
+
+    mlp_part, mlp_far = single(mlp_out, inner, down_w)
+    up_pair = up_keep, up_got
+    up_halves = halve_near(up_pair, z)
+    gate_low = halve_far(gate_low, z)
+    d_mid_near, d_mid_parts, gate_high, down_high, up_halves, gate_low, mlp_part = meet(
+        d_mid_near, diag_parts(d_mid_near), gate_high, down_high, up_halves, gate_low, mlp_part
+    )
+    d_mid_diag = gather_diag(d_mid_parts)
+    up_sum = swapped(up_halves, 1)
+    gate_halves = side_by_side(gate_low, halve_far(gate_high, z))
+    mlp_far, d_mid_diag, gate_halves, down_sum = meet(
+        mlp_far, d_mid_diag, gate_halves, side_by_side(down_low, down_high)
+    )
     d_mid_all = gather_join(d_mid_near, d_mid_diag).reshape(rows, width)
+    mlp_far = scatter_far(mlp_far)
+    gate_sum = swapped(gate_halves, far)
+    down_parts = reduce_y(down_sum, y)
 
     def attention_back(d_mid_all, out_w, values, probs, attended):
         d_att = jnp.dot(d_mid_all, out_w, preferred_element_type=F32).astype(BF)
@@ -522,15 +604,22 @@
         return d_att, d_scores, grad_half(1, d_mid_all, attended), grad_half(0, d_mid_all, attended)
 
     d_att, d_scores, out_send, out_keep = single(attention_back, d_mid_all, out_w, values, probs, attended)
-    d_scores, out_send, out_keep, *more = meet(d_scores, out_send, out_keep, *mlp_far, *up_sum, *down_sum)
-    mlp_far, up_sum, down_sum = more[:2], more[2:4], more[4:]
+    d_scores, out_send, mlp_far, gate_sum, up_sum, down_parts = meet(
+        d_scores, out_send, mlp_far, gate_sum, up_sum, down_parts
+    )
     out_got = swap_c(out_send)
-    down_parts = reduce_y(down_sum, y)
-    up_sum = reduce_far(up_sum, z)
-    mlp_near = scatter_near(*scatter_prep(mlp_part, mlp_far))
-    out_sum = reduce_near((out_keep, out_got), z)
-
-    def qkv_back(d_scores, d_att, probs, queries, keys, cos, sin, qkv_w, hid_all, scale_a):
+    d_scores, ready, up_halves, out_halves = meet(
+        d_scores,
+        scatter_prep(mlp_part, mlp_far),
+        halve_far(up_sum, z),
+        halve_near((out_keep, out_got), z),
+    )
+    mlp_near = scatter_near(*ready)
+    up_sum = swapped(up_halves, far)
+    out_sum = swapped(out_halves, 1)
+    gate_parts = reduce_y(gate_sum, y)
+
+    def qkv_back(d_scores, d_att, probs, queries, keys, cos, sin, qkv_w, hid_all, scale_a, gain_m_part):
         d_queries = jnp.einsum("ghqs,gsd->gqhd", d_scores, keys, preferred_element_type=F32) * scale
         d_keys = jnp.einsum("ghqs,gqhd->gsd", d_scores, queries, preferred_element_type=F32) * scale
         d_values = jnp.einsum("ghqs,gqhd->gsd", probs.astype(BF), d_att, preferred_element_type=F32)
@@ -540,52 +629,76 @@
         d_qkv = jnp.concatenate([d_q, d_k, d_v], axis=1).astype(BF)
         back = cols_cols(d_qkv, qkv_w)
         unit_a = hid_all.astype(F32).reshape(rows, width) * scale_a
-        return d_qkv, back.astype(BF).reshape(micro, 4 * toks, width), jnp.sum(back * unit_a, axis=0)
-
-    d_qkv, back_attn, gain_a_part = single(
-        qkv_back, d_scores, d_att, probs, queries, keys, cos, sin, qkv_w, hid_all, scale_a
-    )
-    gain_rows = jnp.stack([gain_a_part, gain_m_part]).reshape(2, 2, nz, 2, block)
-    gain_rows = gain_rows.transpose(1, 2, 3, 0, 4)
-    gain_rows = jnp.pad(gain_rows, ((0, 0),) * 3 + ((0, extra - 2), (0, qkv_cols - block))).astype(BF)
-    qkv_send = jnp.concatenate([grad_half(1, normed_a, d_qkv), gain_rows[1]], axis=2)
-    back_attn, qkv_send, d_qkv, *more = meet(
-        back_attn, qkv_send, d_qkv, *mlp_near, *gate_sum, *up_sum, *out_sum
-    )
-    mlp_near, gate_sum, up_sum, out_sum = more[:2], more[2:4], more[4:6], more[6:]
+        gain_rows = jnp.stack([jnp.sum(back * unit_a, axis=0), gain_m_part]).reshape(2, 2, nz, 2, block)
+        gain_rows = gain_rows.transpose(1, 2, 3, 0, 4)
+        back = back.astype(BF).reshape(micro, 4 * toks, width)
+        return d_qkv, back, far_parts(back), gain_rows[1], gain_rows[0]
+
+    d_qkv, back_attn, attn_far, gain_send, gain_keep = single(
+        qkv_back, d_scores, d_att, probs, queries, keys, cos, sin, qkv_w, hid_all, scale_a, gain_m_part
+    )
+    back_attn, attn_far, d_qkv, gain_send, mlp_near, out_sum, up_sum, gate_parts = meet(
+        back_attn, attn_far, d_qkv, gain_send, mlp_near, out_sum, up_sum, gate_parts
+    )
+    attn_far = scatter_far(attn_far)
+    gain_got = swap_c(gain_send)
+    qkv_send = single(lambda a, b: grad_half(1, a, b), normed_a, d_qkv)
+    d_qkv, qkv_send = meet(d_qkv, qkv_send)
     qkv_got = swap_c(qkv_send)
-    attn_far = scatter_far(back_attn)
-    qkv_keep = jnp.concatenate([grad_half(0, normed_a, d_qkv), gain_rows[0]], axis=2)
-    qkv_keep, qkv_got = meet(qkv_keep, qkv_got)
-    qkv_sum = reduce_near((qkv_keep, qkv_got), z)
-    more = meet(*attn_far, *qkv_sum)
-    attn_far, qkv_sum = more[:2], more[2:]
-    attn_near = scatter_near(*scatter_prep(back_attn, attn_far))
-    qkv_sum = reduce_far(qkv_sum, z)
-    out_sum = reduce_far(out_sum, z)
-    attn_near0, attn_near1, *more = meet(*attn_near, *qkv_sum, *out_sum, *mlp_near, *gate_sum, *up_sum)
-    attn_near, qkv_sum, out_sum = (attn_near0, attn_near1), more[:2], more[2:4]
-    mlp_near, gate_sum, up_sum = more[4:6], more[6:8], more[8:]
-    qkv_parts = reduce_y(qkv_sum, y)
-    gate_parts = reduce_y(gate_sum, y)
+
+    def keep_halves(normed_a, d_qkv, out_sum):
+        return grad_half(0, normed_a, d_qkv), halve(out_sum, z, far_last())
+
+    qkv_keep, out_halves = single(keep_halves, normed_a, d_qkv, far_steps(out_sum, z))
+    attn_far, qkv_got, gain_got, qkv_keep, out_halves = meet(attn_far, qkv_got, gain_got, qkv_keep, out_halves)
+
+    def near_halves(back_attn, attn_far, qkv_pair, gain_pair):
+        return scatter_prep(back_attn, attn_far), halve(qkv_pair, z, 1), halve(gain_pair, z, 1)
+
+    ready, qkv_halves, gain_halves = single(
+        near_halves, back_attn, attn_far, (qkv_keep, qkv_got), (gain_keep, gain_got)
+    )
+    mlp_near, ready, qkv_halves, gain_halves = meet(mlp_near, ready, qkv_halves, gain_halves)
+    attn_near = scatter_near(*ready)
+    qkv_sum, gain_sum = swapped(qkv_halves, 1), swapped(gain_halves, 1)
+    out_sum = swapped(out_halves, far)
+
+    def finish_out(mid, mlp_part, from_x, from_y):
+        return (mid + scatter_sum(mlp_part, (from_x, from_y))).astype(BF)
+
+    block_out = regroup(single(finish_out, mid, mlp_part, *mlp_near), block, c, True)
+    qkv_sum, gain_sum, block_out = meet(qkv_sum, gain_sum, block_out)
+
+    def far_halves(*pairs):
+        return [halve(p, z, far_last()) for p in pairs]
+
+    qkv_halves, gain_halves = single(far_halves, far_steps(qkv_sum, z), far_steps(gain_sum, z))
+    attn_near, qkv_halves, gain_halves, out_sum = meet(attn_near, qkv_halves, gain_halves, out_sum)
+    qkv_sum, gain_sum = swapped(qkv_halves, far), swapped(gain_halves, far)
     up_parts = reduce_y(up_sum, y)
     out_parts = reduce_y(out_sum, y)
-    block_out = (mid + scatter_sum(mlp_part, mlp_near)).astype(BF)
-    d_normed_a = scatter_sum(back_attn, attn_near)
-    sc_a = scale_a.reshape(micro, 4 * toks, 1)[:, :toks]
-    unit_a = hid.astype(F32) * sc_a
-    input_grad = d_mid + norm_back(d_normed_a, unit_a, gain_a, sc_a)
-
-    keep = (qkv_parts[0] + qkv_parts[1])[block : block + 2, :block]
+
+    def finish_grad(back_attn, from_x, from_y, hid, scale_a, gain_a, d_mid):
+        sc_a = scale_a.reshape(micro, 4 * toks, 1)[:, :toks]
+        d_normed_a = scatter_sum(back_attn, (from_x, from_y))
+        return d_mid + norm_back(d_normed_a, hid.astype(F32) * sc_a, gain_a, sc_a)
+
+    input_grad = single(finish_grad, back_attn, *attn_near, hid, scale_a, gain_a, d_mid)
+    input_grad = regroup(input_grad, block, c, True)
+    input_grad, qkv_sum, gain_sum, up_parts, out_parts = meet(
+        input_grad, qkv_sum, gain_sum, up_parts, out_parts
+    )
+    gain_parts = reduce_y(gain_sum, y)
+    qkv_parts = reduce_y(qkv_sum, y)
+    keep = add(*gain_parts)
     keep = keep + swap_x(keep)
-    qkv_parts = tuple(p[:block] for p in qkv_parts)
 
     def cut(parts, lo, hi):
         return join((parts[0][:, lo:hi], parts[1][:, lo:hi]), y)
 
     return (
-        regroup(block_out, block, c, True)[:, None],
-        regroup(input_grad, block, c, True)[:, None],
+        block_out[:, None],
+        input_grad[:, None],
         keep[0],
         keep[1],
         cut(qkv_parts, 0, q_cols),

time: 696 us -> 662 us (0.951)
  waiting for transfers between devices: 220 us -> 143 us
  other arithmetic: 114 us -> 137 us
  starting transfers between devices: 67.9 us -> 89.9 us
    ppermute x20 -> x27, waiting for transfers between devices: 136 us -> 65.4 us  [swap_z(): return lax.ppermute(a, 'z', [(i, i ^ bit) for i in range(n)])]
    convert_element_type x4 -> x21, other arithmetic: 15 us -> 48.8 us  [the longest x13 27.9 us: halve(): return (keep, send.astype(pair[1].dtype))]
    ppermute x17, waiting for transfers between devices: 43.6 us -> 13.9 us  [swap_x(): return lax.ppermute(a, 'x', [(0, 1), (1, 0)])]
    ppermute x25 -> x26, waiting for transfers between devices: 40.6 us -> 63.6 us  [swap_y(): return lax.ppermute(a, 'y', [(0, 1), (1, 0)])]
    add x15 -> x5, other arithmetic: 21.9 us -> 2.26 us  [add(): return a.astype(F32) + b.astype(F32)]
    ppermute x20 -> x27, starting transfers between devices: 24.7 us -> 44.2 us  [swap_z(): return lax.ppermute(a, 'z', [(i, i ^ bit) for i in range(n)])]
    squeeze x16 -> x1, local copies, waits for them, and re-layouts: 12.7 us -> 0.01 us  [qkv_back(): return (d_qkv, back, far_parts(back), gain_rows[1], gain_rows[0])]
    convert_element_type x15 -> x0, local copies, waits for them, and re-layouts: 11.3 us -> none  [the longest x10 7.03 us: reduce_step(): pick(pairs, 1, 1 - here).astype(BF)]
  transfers between devices with their start and end apart: 72 -> 82, of which waited for: 32 -> 29; matrix products, arithmetic and copies ran while one was open for 47% -> 51% of each run, Pallas kernels for 4% -> 4%
where the time goes in v3:
time: 662 us; the launch traced here: 651 us
  matrix products  156 us (24%)
  waiting for transfers between devices  143 us (22%)
  other arithmetic  137 us (21%)
  local copies, waits for them, and re-layouts  94.7 us (14%)
  starting transfers between devices  89.9 us (14%)
  Pallas kernels  27.9 us (4%)
    ppermute x27, waiting for transfers between devices, swap_z(): return lax.ppermute(a, 'z', [(i, i ^ bit) for i in range(n)])  65.4 us
    ppermute x26, waiting for transfers between devices, swap_y(): return lax.ppermute(a, 'y', [(0, 1), (1, 0)])  63.6 us
    dot_general x10, matrix products, rows_rows(): lax.dot_general(left, right, (((0,), (0,)), ((), ())), preferred_element_...  49.1 us
    ppermute x27, starting transfers between devices, swap_z(): return lax.ppermute(a, 'z', [(i, i ^ bit) for i in range(n)])  44.2 us
    dot_general x4, matrix products, cols_cols(): lax.dot_general(left, right, (((1,), (1,)), ((), ())), preferred_element_...  43 us
    convert_element_type x13, other arithmetic, halve(): return (keep, send.astype(pair[1].dtype))  27.9 us
    ppermute x26, starting transfers between devices, swap_y(): return lax.ppermute(a, 'y', [(0, 1), (1, 0)])  27.6 us
    unnamed x159, local copies, waits for them, and re-layouts  22.2 us
  transfers between devices with their start and end apart: 82, of which 29 were waited for; matrix products, arithmetic and copies ran while one was open for 51% of the time, Pallas kernels for 4%

profile of v3, /device:TPU:0, one launch (start us, length us, event | category | flops | bytes accessed | tf_op | source)
XLA Modules:
  0.0 650.8 jit_solution(6364736713573571755)
XLA Ops:
  37.0 14.2 %collective-permute-done.6 = bf16[2,128,2048]{2,1,0:T(8,128)(2,1)S(1)} collective-permute-done((bf16[2,128,2048]{2,1,0:T(8,128)(2,1)S(1)}, bf16[2,128,2048]{2,1,0:T(8,128)(2,1)S(1)}, u32[]{:S(2)}, u32[]{:S(2)}) %collective-permute-start.6) | collective-permute-done | bytes 1048608 | tf_op jit(solution)/shard_map/ppermute | solution.py:21
  65.2 23.0 %collective-permute-done.9 = bf16[2,128,1024]{2,1,0:T(8,128)(2,1)S(1)} collective-permute-done((bf16[2,128,1024]{2,1,0:T(8,128)(2,1)S(1)}, bf16[2,128,1024]{2,1,0:T(8,128)(2,1)S(1)}, u32[]{:S(2)}, u32[]{:S(2)}) %collective-permute-start.9) | collective-permute-done | bytes 524320 | tf_op jit(solution)/shard_map/ppermute | solution.py:21
  114.3 50.9 %conditional.16 = (f32[1024,1]{0,1:T(1,128)S(1)}, bf16[1024,2048]{1,0:T(8,128)(2,1)S(1)}, bf16[4,256,8,64]{1,3,2,0:T(8,128)(2,1)}, bf16[4,256,64]{1,2,0:T(8,128)...) conditional(s32[]{:T(128)} %convert_element_type.568, ...), branch_computations={%region_1.2_spmd, %region_2.6_spmd} | conditional | flops 5406032896 | bytes 196866416 | solution.py:56
  144.2 7.6 %broadcast_divide_fusion = f32[4,8,256,256]{2,3,1,0:T(8,128)} fusion(f32[4,8,256,256]{2,3,1,0:T(8,128)} %get-tuple-element.873, f32[4,8,256]{2,1,0:T(8,128)S(1)} %get-tuple-element.872), kind=kLoop, calls=%fused_computation.10 | loop fusion | flops 2097152 | bytes 16809984 | tf_op jit(solution)/shard_map/cond/branch_1_fun/div | solution.py:451
  168.7 9.7 %collective-permute-done.20 = bf16[2,128,1024]{2,1,0:T(8,128)(2,1)S(1)} collective-permute-done((bf16[2,128,1024]{2,1,0:T(8,128)(2,1)S(1)}, bf16[2,128,1024]{2,1,0:T(8,128)(2,1)S(1)}, u32[]{:S(2)}, u32[]{:S(2)}) %collective-permute-start.20) | collective-permute-done | bytes 524320 | tf_op jit(solution)/shard_map/ppermute | solution.py:17
  193.7 16.8 %collective-permute-done.25 = bf16[1,1,128,1408]{3,2,1,0:T(8,128)(2,1)S(1)} collective-permute-done((bf16[1,1,128,1408]{3,2,1,0:T(8,128)(2,1)S(1)}, bf16[1,1,128,1408]{3,2,1,0:T(8,128)(2,1)S(1)}, u32[]{:S(2)}, u32[]{:S(2)}) %collective-permute-start.25) | collective-permute-done | bytes 360480 | tf_op jit(solution)/shard_map/ppermute | solution.py:30
  224.3 19.6 %collective-permute-done.28 = bf16[2,128,2048]{2,1,0:T(8,128)(2,1)S(1)} collective-permute-done((bf16[2,128,2048]{2,1,0:T(8,128)(2,1)S(1)}, bf16[2,128,2048]{2,1,0:T(8,128)(2,1)S(1)}, u32[]{:S(2)}, u32[]{:S(2)}) %collective-permute-start.28) | collective-permute-done | bytes 1048608 | tf_op jit(solution)/shard_map/ppermute | solution.py:21
  258.1 9.3 %shard_map.260 = bf16[2,4,2,128,2816]{4,3,2,1,0:T(8,128)(2,1)} custom-call(s32[5]{0:T(128)} %xor_select_fusion.where_ref, bf16[4,1,128,2816]{3,2,1,0:T(8,128)(2,1)} %copy-done.14, bf16[4,1,128,2816]{3,2,1,0:T(8,128)(2,1)} %copy-done.44, bf16[4,1,128,2816]{3,2,1,0:T(8,128)(2,1)} %copy-done.22, bf16[4,1,128,2816]{3,2,1,0:T(8,128)(2,1)} %copy-done.45), custom_call_target="tpu_custom_call" | custom-call | bytes 23068672 | tf_op jit(solution)/shard_map/pallas_call | solution.py:178
  273.8 22.8 %conditional.17 = (f32[1024,2816]{1,0:T(8,128)}, bf16[1024,1408]{1,0:T(8,128)(2,1)S(1)}) conditional(s32[]{:T(128)} %convert_element_type.568, () %tuple.176, (bf16[1024,2048]{1,0:T(8,128)(2,1)S(1)}, bf16[2048,2816]{1,0:T(8,128)(2,1)}) %tuple.349), branch_computations={%region_7.8_spmd, %region_8.9_spmd} | conditional | flops 11819810816 | bytes 41680912 | solution.py:56
  273.8 17.6 %fusion.133 = f32[1024,2816]{1,0:T(8,128)} fusion(bf16[1024,2048]{1,0:T(8,128)(2,1)S(1)} %get-tuple-element.182, bf16[2048,2816]{1,0:T(8,128)(2,1)} %get-tuple-element.183), kind=kOutput, calls=%fused_computation.326 | convolution fusion | flops 11811160064 | bytes 27262976 | tf_op jit(solution)/shard_map/cond/branch_1_fun/dot_general | solution.py:498
  330.7 33.2 %conditional.19 = (bf16[1024,1408]{1,0:T(8,128)(2,1)}, bf16[1024,1408]{1,0:T(8,128)(2,1)}, bf16[2,512,2048]{2,1,0:T(8,128)(2,1)}, bf16[2,128,1024]{2,1,0:T(8,128)(2,1)}, bf16[2,128,1024]{2,1,0:T(8,128)(2,1)}) conditional(s32[]{:T(128)} %convert_element_type.568, () %tuple.175, (bf16[1024,2048]{1,0:T(8,128)(2,1)S(1)}, ...), branch_computations={%region_11.12_spmd, %region_12.13_spmd} | conditional | flops 17749114880 | bytes 50855976 | solution.py:56
  330.7 12.8 %multiply_convert_fusion = (bf16[1024,1408]{1,0:T(8,128)(2,1)}, bf16[1024,1408]{1,0:T(8,128)(2,1)}) fusion(f32[1024,2816]{1,0:T(8,128)} %get-tuple-element.188, bf16[1024,2048]{1,0:T(8,128)(2,1)S(1)} %get-tuple-element.186, bf16[2048,1408]{1,0:T(8,128)(2,1)S(1)} %get-tuple-element.187), kind=kOutput, calls=%fused_computation.43 | convolution fusion | flops 5924323328 | bytes 27262976 | tf_op jit(solution)/shard_map/cond/branch_1_fun/dot_general | solution.py:515
  343.5 18.1 %fusion.32 = bf16[1024,2048]{1,0:T(8,128)(2,1)} fusion(bf16[2048,2816]{1,0:T(8,128)(2,1)} %get-tuple-element.189, bf16[1024,1408]{1,0:T(8,128)(2,1)} %get-tuple-element.1022, bf16[1024,1408]{1,0:T(8,128)(2,1)} %get-tuple-element.1021), kind=kOutput, calls=%fused_computation.46 | convolution fusion | flops 11824791552 | bytes 21495808 | tf_op jit(solution)/shard_map/cond/branch_1_fun/dot_general | solution.py:318
  371.4 11.4 %conditional.20 = (bf16[4,2,128,1408]{3,2,1,0:T(8,128)(2,1)S(1)}, bf16[4,2,128,1408]{3,2,1,0:T(8,128)(2,1)S(1)}) conditional(s32[]{:T(128)} %convert_element_type.568, () %tuple.187, (bf16[1024,2048]{1,0:T(8,128)(2,1)S(1)}, bf16[1024,1408]{1,0:T(8,128)(2,1)}) %tuple.350), branch_computations={%region_13.14_spmd, %region_14.15_spmd} | conditional | flops 5908463616 | bytes 15728656 | solution.py:56
  400.4 12.4 %conditional.21 = (bf16[4,2,128,1408]{3,2,1,0:T(8,128)(2,1)}, bf16[4,2,128,1408]{3,2,1,0:T(8,128)(2,1)S(1)}) conditional(s32[]{:T(128)} %convert_element_type.568, () %tuple.192, (bf16[1024,2048]{1,0:T(8,128)(2,1)S(1)}, bf16[1024,1408]{1,0:T(8,128)(2,1)}) %tuple.351), branch_computations={%region_15.16_spmd, %region_16.17_spmd} | conditional | flops 5908463616 | bytes 15728656 | solution.py:56
  412.8 13.0 %collective-permute-done.46 = bf16[1,2,128,768]{3,2,1,0:T(8,128)(2,1)S(1)} collective-permute-done((bf16[1,2,128,768]{3,2,1,0:T(8,128)(2,1)}, bf16[1,2,128,768]{3,2,1,0:T(8,128)(2,1)S(1)}, u32[]{:S(2)}, u32[]{:S(2)}) %collective-permute-start.46) | collective-permute-done | bytes 393248 | tf_op jit(solution)/shard_map/ppermute | solution.py:30
  442.0 13.3 %conditional.23 = (bf16[2,512,2048]{2,1,0:T(8,128)(2,1)}, bf16[2,128,1024]{2,1,0:T(8,128)(2,1)}, bf16[2,128,1024]{2,1,0:T(8,128)(2,1)}) conditional(s32[]{:T(128)} %convert_element_type.568, () %tuple.197, (bf16[1024,1408]{1,0:T(8,128)(2,1)}, bf16[2048,1408]{1,0:T(8,128)(2,1)}) %tuple.358), branch_computations={%region_21.22_spmd, %region_22.23_spmd} | conditional | flops 5907677184 | bytes 14942232 | solution.py:56
  442.0 11.1 %convolution_convert_fusion.6 = bf16[1024,2048]{1,0:T(8,128)(2,1)} fusion(bf16[1024,1408]{1,0:T(8,128)(2,1)} %get-tuple-element.201, bf16[2048,1408]{1,0:T(8,128)(2,1)} %get-tuple-element.202), kind=kOutput, calls=%fused_computation.62 | convolution fusion | flops 5907677184 | bytes 12845056 | tf_op jit(solution)/shard_map/cond/branch_1_fun/dot_general | solution.py:318
  484.8 22.9 %conditional.24 = (bf16[4,256,8,64]{1,0,3,2:T(4,128)(2,1)S(1)}, bf16[4,8,256,256]{2,3,1,0:T(8,128)(2,1)}, bf16[4,2,128,512]{3,2,1,0:T(8,128)(2,1)S(1)}, bf16[2,2,2,128,512]{4,3,2,1,0:T(8,128)(2,1)S(1)}) conditional(s32[]{:T(128)} %convert_element_type.568, () %tuple.170, (bf16[2,512,2048]{2,1,0:T(8,128)(2,1)S(1)}, ...), branch_computations={%region_23.24_spmd, %region_24.26_spmd} | conditional | flops 4841807872 | bytes 75628688 | solution.py:56
  490.8 10.8 %fusion.42 = bf16[4,8,256,256]{2,3,1,0:T(8,128)(2,1)} fusion(f32[4,8,256,256]{2,3,1,0:T(8,128)} %get-tuple-element.205, bf16[4,256,8,64]{1,0,3,2:T(4,128)(2,1)S(1)} %reshape.613, bf16[4,256,64,1]{1,0,2,3:T(4,128)(2,1)} %bitcast.352), kind=kOutput, calls=%fused_computation.67 | convolution fusion | flops 545267968 | bytes 13762560 | tf_op jit(solution)/shard_map/cond/branch_1_fun/sub | solution.py:603
  530.6 32.7 %conditional.25 = (bf16[1024,640]{0,1:T(8,128)(2,1)}, bf16[2,512,2048]{2,1,0:T(8,128)(2,1)}, bf16[2,128,1024]{2,1,0:T(8,128)(2,1)}, bf16[2,128,1024]{2,1,0:T(8,1...) conditional(s32[]{:T(128)} %convert_element_type.568, () %tuple.164, ...), branch_computations={%region_26.27_spmd, %region_27.29_spmd} | conditional | flops 3503654912 | bytes 83062888 | solution.py:56
  552.3 8.1 %fusion.68 = (f32[2048]{0:T(1024)S(1)}, bf16[1024,2048]{1,0:T(8,128)(2,1)}) fusion(bf16[2,512,2048]{2,1,0:T(8,128)(2,1)S(1)} %copy-done.1, f32[1024]{0:T(1024)S(1)} %bitcast.376, bf16[1024,640]{0,1:T(8,128)(2,1)} %constant_dynamic-update-slice_fusion, bf16[2048,640]{1,0:T(8,128)(2,1)} %get-tuple-element.215), kind=kOutput, calls=%fused_computation.84 | convolution fusion | flops 2694838272 | bytes 12333056 | tf_op jit(solution)/shard_map/cond/branch_1_fun/dot_general | solution.py:318
  584.5 8.0 %conditional.28 = (bf16[2,128,2048]{2,1,0:T(8,128)(2,1)}, bf16[2,128,2048]{2,1,0:T(8,128)(2,1)}, f32[2,2,128,640]{3,2,1,0:T(8,128)S(1)}, bf16[2,2,128,640]{3,2,1...) conditional(s32[]{:T(128)} %convert_element_type.568, () %tuple.206, ...), branch_computations={%region_33.34_spmd, %region_34.35_spmd} | conditional | flops 8587282 | bytes 18260220 | solution.py:56
  609.6 8.3 %collective-permute-done.71 = f32[2,2,2,128]{3,2,1,0:T(2,128)S(1)} collective-permute-done((f32[2,2,2,128]{3,2,1,0:T(2,128)S(1)}, f32[2,2,2,128]{3,2,1,0:T(2,128)S(1)}, u32[]{:S(2)}, u32[]{:S(2)}) %collective-permute-start.71) | collective-permute-done | bytes 4128 | tf_op jit(solution)/shard_map/ppermute | solution.py:30
  (569 shorter events, 485.8 us)
Async XLA Ops:
  55.5 32.7 %collective-permute-start.7 = (bf16[2,1,144,1152]{3,2,1,0:T(8,128)(2,1)S(1)}, bf16[2,1,144,1152]{3,2,1,0:T(8,128)(2,1)S(1)}, u32[]{:S(2)}, u32[]{:S(2)}) collective-permute-start(bf16[2,1,144,1152]{3,2,1,0:T(8,128)(2,1)S(1)} %constant_dynamic-update-slice_fusion.5), channel_id=1, source_target_pairs={{0,8},{8,0},{16,24},{24,16},{1,9},{9,1},{17,25},{25,17},{2,10},{10... | collective-permute-start | bytes 1990664 | tf_op jit(solution)/shard_map/ppermute | solution.py:30
  58.8 33.0 %collective-permute-start.8 = (bf16[1,1,128,2816]{3,2,1,0:T(8,128)(2,1)S(1)}, bf16[1,1,128,2816]{3,2,1,0:T(8,128)(2,1)S(1)}, u32[]{:S(2)}, u32[]{:S(2)}) collective-permute-start(bf16[1,1,128,2816]{3,2,1,0:T(8,128)(2,1)S(1)} %bitcast.347), channel_id=1, source_target_pairs={{0,16},{8,24},{16,0},{24,8},{1,17},{9,25},{17,1},{25,9},{2,18},{10... | collective-permute-start | bytes 2162696 | tf_op jit(solution)/shard_map/ppermute | solution.py:30
  60.6 31.2 %collective-permute-start.11 = (bf16[128,2816]{1,0:T(8,128)(2,1)}, bf16[128,2816]{1,0:T(8,128)(2,1)}, u32[]{:S(2)}, u32[]{:S(2)}) collective-permute-start(bf16[128,2816]{1,0:T(8,128)(2,1)} %pad_maximum_fusion.15), channel_id=1, source_target_pairs={{0,4},{4,0},{1,5},{5,1},{2,6},{6,2},{3,7},{7,3},{8,12},{12,8},{9,1... | collective-permute-start | bytes 2162696 | tf_op jit(solution)/shard_map/ppermute | solution.py:21
  94.4 70.8 %collective-permute-start.14 = (bf16[2,1,128,2816]{3,2,1,0:T(8,128)(2,1)}, bf16[2,1,128,2816]{3,2,1,0:T(8,128)(2,1)}, u32[]{:S(2)}, u32[]{:S(2)}) collective-permute-start(bf16[2,1,128,2816]{3,2,1,0:T(8,128)(2,1)} %constant_dynamic-update-slice_fusion.9), channel_id=1, source_target_pairs={{0,8},{8,0},{16,24},{24,16},{1,9},{9,1},{17,25},{25,17},{2,10},{10... | collective-permute-start | bytes 4325384 | tf_op jit(solution)/shard_map/ppermute | solution.py:30
  95.9 69.3 %collective-permute-start.17 = (bf16[2,128,2048]{2,1,0:T(8,128)(2,1)}, bf16[2,128,2048]{2,1,0:T(8,128)(2,1)}, u32[]{:S(2)}, u32[]{:S(2)}) collective-permute-start(bf16[2,128,2048]{2,1,0:T(8,128)(2,1)} %bitcast.63), channel_id=1, source_target_pairs={{0,4},{4,0},{1,5},{5,1},{2,6},{6,2},{3,7},{7,3},{8,12},{12,8},{9,1... | collective-permute-start | bytes 3145736 | tf_op jit(solution)/shard_map/ppermute | solution.py:21
  96.4 68.8 %collective-permute-start.16 = (bf16[2,128,2048]{2,1,0:T(8,128)(2,1)}, bf16[2,128,2048]{2,1,0:T(8,128)(2,1)}, u32[]{:S(2)}, u32[]{:S(2)}) collective-permute-start(bf16[2,128,2048]{2,1,0:T(8,128)(2,1)} %bitcast.63), channel_id=1, source_target_pairs={{0,1},{1,0},{2,3},{3,2},{4,5},{5,4},{6,7},{7,6},{8,9},{9,8},{10,11... | collective-permute-start | bytes 3145736 | tf_op jit(solution)/shard_map/ppermute | solution.py:17
  98.8 66.3 %collective-permute-start.15 = (bf16[1,1,128,2816]{3,2,1,0:T(8,128)(2,1)}, bf16[1,1,128,2816]{3,2,1,0:T(8,128)(2,1)}, u32[]{:S(2)}, u32[]{:S(2)}) collective-permute-start(bf16[1,1,128,2816]{3,2,1,0:T(8,128)(2,1)} %bitcast.66), channel_id=1, source_target_pairs={{0,16},{8,24},{16,0},{24,8},{1,17},{9,25},{17,1},{25,9},{2,18},{10... | collective-permute-start | bytes 2162696 | tf_op jit(solution)/shard_map/ppermute | solution.py:30
  106.0 59.1 %collective-permute-start.18 = (bf16[128,1408]{1,0:T(8,128)(2,1)}, bf16[128,1408]{1,0:T(8,128)(2,1)}, u32[]{:S(2)}, u32[]{:S(2)}) collective-permute-start(bf16[128,1408]{1,0:T(8,128)(2,1)} %get-tuple-element.553), channel_id=1, source_target_pairs={{0,4},{4,0},{1,5},{5,1},{2,6},{6,2},{3,7},{7,3},{8,12},{12,8},{9,1... | collective-permute-start | bytes 1081352 | tf_op jit(solution)/shard_map/ppermute | solution.py:21
  214.5 32.0 %collective-permute-start.29 = (bf16[4,1,128,2816]{3,2,1,0:T(8,128)(2,1)S(1)}, bf16[4,1,128,2816]{3,2,1,0:T(8,128)(2,1)S(1)}, u32[]{:S(2)}, u32[]{:S(2)}) collective-permute-start(bf16[4,1,128,2816]{3,2,1,0:T(8,128)(2,1)S(1)} %constant_dynamic-update-slice_fusion.13.peer), channel_id=1, source_target_pairs={{0,2},{2,0},{1,3},{3,1},{4,6},{6,4},{5,7},{7,5},{8,10},{10,8},{9,1... | collective-permute-start | bytes 8650760 | tf_op jit(solution)/shard_map/ppermute | solution.py:25
  328.7 35.2 %collective-permute-start.40 = (bf16[2,2,128,1408]{3,2,1,0:T(8,128)(2,1)}, bf16[2,2,128,1408]{3,2,1,0:T(8,128)(2,1)}, u32[]{:S(2)}, u32[]{:S(2)}) collective-permute-start(bf16[2,2,128,1408]{3,2,1,0:T(8,128)(2,1)} %fusion.99), channel_id=1, source_target_pairs={{0,8},{8,0},{16,24},{24,16},{1,9},{9,1},{17,25},{25,17},{2,10},{10... | collective-permute-start | bytes 4325384 | tf_op jit(solution)/shard_map/ppermute | solution.py:30
  392.8 33.7 %collective-permute-start.44 = (bf16[2,128,2048]{2,1,0:T(8,128)(2,1)}, bf16[2,128,2048]{2,1,0:T(8,128)(2,1)S(1)}, u32[]{:S(2)}, u32[]{:S(2)}) collective-permute-start(bf16[2,128,2048]{2,1,0:T(8,128)(2,1)} %pad_maximum_fusion.10), channel_id=1, source_target_pairs={{0,1},{1,0},{2,3},{3,2},{4,5},{5,4},{6,7},{7,6},{8,9},{9,8},{10,11... | collective-permute-start | bytes 3145736 | tf_op jit(solution)/shard_map/ppermute | solution.py:17
  393.4 33.1 %collective-permute-start.45 = (bf16[2,128,2048]{2,1,0:T(8,128)(2,1)}, bf16[2,128,2048]{2,1,0:T(8,128)(2,1)}, u32[]{:S(2)}, u32[]{:S(2)}) collective-permute-start(bf16[2,128,2048]{2,1,0:T(8,128)(2,1)} %pad_maximum_fusion.11), channel_id=1, source_target_pairs={{0,4},{4,0},{1,5},{5,1},{2,6},{6,2},{3,7},{7,3},{8,12},{12,8},{9,1... | collective-permute-start | bytes 3145736 | tf_op jit(solution)/shard_map/ppermute | solution.py:21
  398.2 28.2 %collective-permute-start.47 = (bf16[2,2,128,768]{3,2,1,0:T(8,128)(2,1)}, bf16[2,2,128,768]{3,2,1,0:T(8,128)(2,1)}, u32[]{:S(2)}, u32[]{:S(2)}) collective-permute-start(bf16[2,2,128,768]{3,2,1,0:T(8,128)(2,1)} %get-tuple-element.632), channel_id=1, source_target_pairs={{0,8},{8,0},{16,24},{24,16},{1,9},{9,1},{17,25},{25,17},{2,10},{10... | collective-permute-start | bytes 2359304 | tf_op jit(solution)/shard_map/ppermute | solution.py:30
  464.4 48.3 %collective-permute-start.58 = (bf16[2,2,128,1408]{3,2,1,0:T(8,128)(2,1)}, bf16[2,2,128,1408]{3,2,1,0:T(8,128)(2,1)}, u32[]{:S(2)}, u32[]{:S(2)}) collective-permute-start(bf16[2,2,128,1408]{3,2,1,0:T(8,128)(2,1)} %get-tuple-element.682), channel_id=1, source_target_pairs={{0,8},{8,0},{16,24},{24,16},{1,9},{9,1},{17,25},{25,17},{2,10},{10... | collective-permute-start | bytes 4325384 | tf_op jit(solution)/shard_map/ppermute | solution.py:30
  476.1 31.6 %collective-permute-start.55 = (bf16[2,128,1024]{2,1,0:T(8,128)(2,1)}, bf16[2,128,1024]{2,1,0:T(8,128)(2,1)}, u32[]{:S(2)}, u32[]{:S(2)}) collective-permute-start(bf16[2,128,1024]{2,1,0:T(8,128)(2,1)} %get-tuple-element.677), channel_id=1, source_target_pairs={{0,4},{4,0},{1,5},{5,1},{2,6},{6,2},{3,7},{7,3},{8,12},{12,8},{9,1... | collective-permute-start | bytes 1572872 | tf_op jit(solution)/shard_map/ppermute | solution.py:21
  477.5 30.2 %collective-permute-start.56 = (bf16[2,128,1024]{2,1,0:T(8,128)(2,1)}, bf16[2,128,1024]{2,1,0:T(8,128)(2,1)}, u32[]{:S(2)}, u32[]{:S(2)}) collective-permute-start(bf16[2,128,1024]{2,1,0:T(8,128)(2,1)} %get-tuple-element.678), channel_id=1, source_target_pairs={{0,1},{1,0},{2,3},{3,2},{4,5},{5,4},{6,7},{7,6},{8,9},{9,8},{10,11... | collective-permute-start | bytes 1572872 | tf_op jit(solution)/shard_map/ppermute | solution.py:17
  478.1 33.2 %collective-permute-start.57 = (bf16[1,2,128,1408]{3,2,1,0:T(8,128)(2,1)}, bf16[1,2,128,1408]{3,2,1,0:T(8,128)(2,1)}, u32[]{:S(2)}, u32[]{:S(2)}) collective-permute-start(bf16[1,2,128,1408]{3,2,1,0:T(8,128)(2,1)} %pad_maximum_fusion.16), channel_id=1, source_target_pairs={{0,16},{8,24},{16,0},{24,8},{1,17},{9,25},{17,1},{25,9},{2,18},{10... | collective-permute-start | bytes 2162696 | tf_op jit(solution)/shard_map/ppermute | solution.py:30
  523.2 40.2 %collective-permute-start.61 = (bf16[2,128,2048]{2,1,0:T(8,128)(2,1)}, bf16[2,128,2048]{2,1,0:T(8,128)(2,1)}, u32[]{:S(2)}, u32[]{:S(2)}) collective-permute-start(bf16[2,128,2048]{2,1,0:T(8,128)(2,1)} %pad_maximum_fusion.12), channel_id=1, source_target_pairs={{0,1},{1,0},{2,3},{3,2},{4,5},{5,4},{6,7},{7,6},{8,9},{9,8},{10,11... | collective-permute-start | bytes 3145736 | tf_op jit(solution)/shard_map/ppermute | solution.py:17
  523.7 39.7 %collective-permute-start.62 = (bf16[2,128,2048]{2,1,0:T(8,128)(2,1)}, bf16[2,128,2048]{2,1,0:T(8,128)(2,1)}, u32[]{:S(2)}, u32[]{:S(2)}) collective-permute-start(bf16[2,128,2048]{2,1,0:T(8,128)(2,1)} %pad_maximum_fusion.13), channel_id=1, source_target_pairs={{0,4},{4,0},{1,5},{5,1},{2,6},{6,2},{3,7},{7,3},{8,12},{12,8},{9,1... | collective-permute-start | bytes 3145736 | tf_op jit(solution)/shard_map/ppermute | solution.py:21
  525.1 38.2 %collective-permute-start.64 = (bf16[1,2,128,1408]{3,2,1,0:T(8,128)(2,1)}, bf16[1,2,128,1408]{3,2,1,0:T(8,128)(2,1)}, u32[]{:S(2)}, u32[]{:S(2)}) collective-permute-start(bf16[1,2,128,1408]{3,2,1,0:T(8,128)(2,1)} %get-tuple-element.708), channel_id=1, source_target_pairs={{0,16},{8,24},{16,0},{24,8},{1,17},{9,25},{17,1},{25,9},{2,18},{10... | collective-permute-start | bytes 2162696 | tf_op jit(solution)/shard_map/ppermute | solution.py:30
  527.1 36.2 %collective-permute-start.63 = (bf16[2,2,128,512]{3,2,1,0:T(8,128)(2,1)}, bf16[2,2,128,512]{3,2,1,0:T(8,128)(2,1)S(1)}, u32[]{:S(2)}, u32[]{:S(2)}) collective-permute-start(bf16[2,2,128,512]{3,2,1,0:T(8,128)(2,1)} %get-tuple-element.706), channel_id=1, source_target_pairs={{0,8},{8,0},{16,24},{24,16},{1,9},{9,1},{17,25},{25,17},{2,10},{10... | collective-permute-start | bytes 1572872 | tf_op jit(solution)/shard_map/ppermute | solution.py:30
  529.6 33.7 %collective-permute-start.65 = (bf16[128,1408]{1,0:T(8,128)(2,1)}, bf16[128,1408]{1,0:T(8,128)(2,1)}, u32[]{:S(2)}, u32[]{:S(2)}) collective-permute-start(bf16[128,1408]{1,0:T(8,128)(2,1)} %get-tuple-element.934), channel_id=1, source_target_pairs={{0,4},{4,0},{1,5},{5,1},{2,6},{6,2},{3,7},{7,3},{8,12},{12,8},{9,1... | collective-permute-start | bytes 1081352 | tf_op jit(solution)/shard_map/ppermute | solution.py:21
  592.5 28.5 %collective-permute-start.72 = (bf16[2,128,2048]{2,1,0:T(8,128)(2,1)}, bf16[2,128,2048]{2,1,0:T(8,128)(2,1)}, u32[]{:S(2)}, u32[]{:S(2)}) collective-permute-start(bf16[2,128,2048]{2,1,0:T(8,128)(2,1)} %get-tuple-element.745), channel_id=1, source_target_pairs={{0,1},{1,0},{2,3},{3,2},{4,5},{5,4},{6,7},{7,6},{8,9},{9,8},{10,11... | collective-permute-start | bytes 3145736 | tf_op jit(solution)/shard_map/ppermute | solution.py:17
  593.5 27.5 %collective-permute-start.73 = (bf16[2,128,2048]{2,1,0:T(8,128)(2,1)}, bf16[2,128,2048]{2,1,0:T(8,128)(2,1)}, u32[]{:S(2)}, u32[]{:S(2)}) collective-permute-start(bf16[2,128,2048]{2,1,0:T(8,128)(2,1)} %get-tuple-element.746), channel_id=1, source_target_pairs={{0,4},{4,0},{1,5},{5,1},{2,6},{6,2},{3,7},{7,3},{8,12},{12,8},{9,1... | collective-permute-start | bytes 3145736 | tf_op jit(solution)/shard_map/ppermute | solution.py:21
  (152 other events, 2034.3 us)

commit v4 on v3

--- a/solution.py
+++ b/solution.py
@@ -91,17 +91,30 @@
 def scatter_prep(part, far):
     m, rows, f = part.shape
     half = f // 2
-    low, high = far
-    part = part.reshape(m, 4, rows // 4, f)
-    to_x = part[:, 1]
-    to_y = part[:, 2]
-    to_x = jnp.concatenate(
-        [(to_x[..., :half].astype(F32) + low.astype(F32)).astype(BF), to_x[..., half:]], axis=-1
-    )
-    to_y = jnp.concatenate(
-        [to_y[..., :half], (to_y[..., half:].astype(F32) + high.astype(F32)).astype(BF)], axis=-1
-    )
-    return to_x, to_y
+    toks = rows // 4
+
+    def kernel(x_ref, y_ref, low_ref, high_ref, to_x, to_y):
+        to_x[0, :, :half] = add(x_ref[0, 0, :, :half], low_ref[0]).astype(BF)
+        to_x[0, :, half:] = x_ref[0, 0, :, half:]
+        to_y[0, :, :half] = y_ref[0, 0, :, :half]
+        to_y[0, :, half:] = add(y_ref[0, 0, :, half:], high_ref[0]).astype(BF)
+
+    part = part.reshape(m, 4, toks, f)
+    small = pl.BlockSpec((1, toks, half), lambda i: (i, 0, 0))
+    large = pl.BlockSpec((1, toks, f), lambda i: (i, 0, 0))
+    return pl.pallas_call(
+        kernel,
+        out_shape=[jax.ShapeDtypeStruct((m, toks, f), BF)] * 2,
+        grid=(m,),
+        in_specs=[
+            pl.BlockSpec((1, 1, toks, f), lambda i: (i, 1, 0, 0)),
+            pl.BlockSpec((1, 1, toks, f), lambda i: (i, 2, 0, 0)),
+            small,
+            small,
+        ],
+        out_specs=[large, large],
+        cost_estimate=pl.CostEstimate(flops=0, bytes_accessed=10 * m * toks * f, transcendentals=0),
+    )(part, part, *far)
 
 
 def scatter_near(to_x, to_y):
@@ -318,17 +331,114 @@
     return lax.dot_general(left, right, (((1,), (1,)), ((), ())), preferred_element_type=F32)
 
 
-def rotate(v, cos, sin):
-    half = v.shape[-1] // 2
-    turned = jnp.concatenate([-v[..., half:], v[..., :half]], axis=-1)
-    return v * cos + turned * sin
-
-
-def rotate_back(v, cos, sin):
-    half = v.shape[-1] // 2
-    w = v * sin
-    turned = jnp.concatenate([w[..., half:], -w[..., :half]], axis=-1)
-    return v * cos + turned
+def turned(v, back=False):
+    half = HEAD_SIZE // 2
+    width = v.shape[-1]
+    low = lax.broadcasted_iota(jnp.int32, v.shape, 1) % HEAD_SIZE < half
+    up = pltpu.roll(v, width - half, 1)
+    down = pltpu.roll(v, half, 1)
+    return jnp.where(low, up, -down) if back else jnp.where(low, -up, down)
+
+
+def head_probs(q, k, allowed):
+    scores = jnp.where(allowed, cols_cols(k, q * BF(HEAD_SIZE ** (-0.5))), -1e30)
+    expo = jnp.exp(scores - jnp.max(scores, axis=0, keepdims=True))
+    return expo * (1.0 / jnp.sum(expo, axis=0, keepdims=True))
+
+
+def wide(table, width):
+    return jnp.concatenate([table] * (width // table.shape[1]), axis=1)
+
+
+def attend(qkv, cos, sin, allowed, q_cols):
+    groups, length, _ = cos.shape
+    cols = qkv.shape[1]
+
+    def kernel(qkv_ref, cos_ref, sin_ref, allowed_ref, q_out, kv_out, att_out):
+        cos, sin = cos_ref[0], sin_ref[0]
+        allowed = allowed_ref[0] > 0
+        q_lin = qkv_ref[:, :q_cols]
+        kv_lin = qkv_ref[:, q_cols:]
+        q = (q_lin * wide(cos, q_cols) + turned(q_lin) * wide(sin, q_cols)).astype(BF)
+        roped = kv_lin * cos + turned(kv_lin) * sin
+        is_key = lax.broadcasted_iota(jnp.int32, kv_lin.shape, 1) < HEAD_SIZE
+        kv = jnp.where(is_key, roped, kv_lin).astype(BF)
+        q_out[...] = q
+        kv_out[...] = kv
+        k = kv[:, :HEAD_SIZE]
+        v_t = kv_lin.T[HEAD_SIZE:].astype(BF)
+        for pair in range(q_cols // (2 * HEAD_SIZE)):
+            parts = []
+            for h in (2 * pair, 2 * pair + 1):
+                probs = head_probs(q[:, h * HEAD_SIZE : (h + 1) * HEAD_SIZE], k, allowed)
+                parts.append(jnp.dot(v_t, probs.astype(BF), preferred_element_type=F32))
+            at = pl.ds(pair * 2 * HEAD_SIZE, 2 * HEAD_SIZE)
+            att_out[:, at] = jnp.concatenate(parts, axis=0).T.astype(BF)
+
+    def rows(width):
+        return pl.BlockSpec((length, width), lambda g: (g, 0))
+
+    table = pl.BlockSpec((1, length, 2 * HEAD_SIZE), lambda g: (g, 0, 0))
+    out = [jax.ShapeDtypeStruct((groups * length, w), BF) for w in (q_cols, cols - q_cols, q_cols)]
+    return pl.pallas_call(
+        kernel,
+        out_shape=out,
+        grid=(groups,),
+        in_specs=[rows(cols), table, table, pl.BlockSpec((1, length, length), lambda g: (g, 0, 0))],
+        out_specs=[rows(q_cols), rows(cols - q_cols), rows(q_cols)],
+    )(qkv, cos, sin, allowed)
+
+
+def attend_back(queries, keys_values, d_att, cos, sin, allowed):
+    groups, length, _ = cos.shape
+    q_cols, kv_cols = queries.shape[1], keys_values.shape[1]
+    scale = HEAD_SIZE ** (-0.5)
+
+    def kernel(q_ref, kv_ref, d_ref, cos_ref, sin_ref, allowed_ref, out):
+        cos, sin = cos_ref[0], sin_ref[0]
+        allowed = allowed_ref[0] > 0
+        k, v = kv_ref[:, :HEAD_SIZE], kv_ref[:, HEAD_SIZE:]
+        k_t = kv_ref[...].astype(F32).T[:HEAD_SIZE].astype(BF)
+        d_k = jnp.zeros((length, HEAD_SIZE), F32)
+        d_v = jnp.zeros((length, HEAD_SIZE), F32)
+        for pair in range(q_cols // (2 * HEAD_SIZE)):
+            parts = []
+            for h in (2 * pair, 2 * pair + 1):
+                at = slice(h * HEAD_SIZE, (h + 1) * HEAD_SIZE)
+                q, d = q_ref[:, at], d_ref[:, at]
+                probs = head_probs(q, k, allowed)
+                d_probs = cols_cols(v, d)
+                inner_sum = jnp.sum(probs * d_probs, axis=0, keepdims=True)
+                d_scores = (probs * (d_probs - inner_sum)).astype(BF)
+                parts.append(jnp.dot(k_t, d_scores, preferred_element_type=F32) * scale)
+                d_k = d_k + jnp.dot(d_scores, q, preferred_element_type=F32)
+                d_v = d_v + jnp.dot(probs.astype(BF), d, preferred_element_type=F32)
+            d_q = jnp.concatenate(parts, axis=0).T
+            d_q = d_q * cos + turned(d_q * sin, True)
+            out[:, pl.ds(pair * 2 * HEAD_SIZE, 2 * HEAD_SIZE)] = d_q.astype(BF)
+        d_kv = jnp.concatenate([d_k * scale, d_v], axis=1)
+        is_key = lax.broadcasted_iota(jnp.int32, d_kv.shape, 1) < HEAD_SIZE
+        roped = d_kv * cos + turned(d_kv * sin, True)
+        out[:, q_cols:] = jnp.where(is_key, roped, d_kv).astype(BF)
+
+    def rows(width):
+        return pl.BlockSpec((length, width), lambda g: (g, 0))
+
+    table = pl.BlockSpec((1, length, 2 * HEAD_SIZE), lambda g: (g, 0, 0))
+    return pl.pallas_call(
+        kernel,
+        out_shape=jax.ShapeDtypeStruct((groups * length, q_cols + kv_cols), BF),
+        grid=(groups,),
+        in_specs=[
+            rows(q_cols),
+            rows(kv_cols),
+            rows(q_cols),
+            table,
+            table,
+            pl.BlockSpec((1, length, length), lambda g: (g, 0, 0)),
+        ],
+        out_specs=rows(q_cols + kv_cols),
+    )(queries, keys_values, d_att, cos, sin, allowed)
 
 
 def norm_back(d_normed, unit, gain, scale):
@@ -428,8 +538,9 @@
     freq = jnp.arange(HEAD_SIZE // 2, dtype=F32)
     inverse = 10000.0 ** (-2.0 * freq / HEAD_SIZE)
     angles = places[:, :, None] * inverse
-    cos = jnp.concatenate([jnp.cos(angles)] * 2, axis=-1)
-    sin = jnp.concatenate([jnp.sin(angles)] * 2, axis=-1)
+    cos = jnp.concatenate([jnp.cos(angles)] * 4, axis=-1)
+    sin = jnp.concatenate([jnp.sin(angles)] * 4, axis=-1)
+    allowed = allowed.swapaxes(1, 2).astype(F32)
 
     rows = micro * 4 * toks
     heads = q_cols // HEAD_SIZE
@@ -439,22 +550,11 @@
         scale_a = lax.rsqrt(jnp.mean(hid32 * hid32, axis=-1, keepdims=True) + EPS)
         normed_a = (hid32 * scale_a * gain_a).astype(BF)
         qkv = jnp.dot(normed_a, qkv_w, preferred_element_type=F32)
-        q_lin = qkv[:, :q_cols].reshape(groups, length, heads, HEAD_SIZE)
-        k_lin = qkv[:, q_cols : q_cols + kv_cols].reshape(groups, length, HEAD_SIZE)
-        values = qkv[:, q_cols + kv_cols :].astype(BF).reshape(groups, length, HEAD_SIZE)
-        queries = rotate(q_lin, cos[:, :, None], sin[:, :, None]).astype(BF)
-        keys = rotate(k_lin, cos, sin).astype(BF)
-        scores = jnp.einsum("gqhd,gsd->ghqs", queries, keys, preferred_element_type=F32) * scale
-        scores = jnp.where(allowed[:, None], scores, -1e30)
-        top = jnp.max(scores, axis=-1, keepdims=True)
-        expo = jnp.exp(scores - top)
-        probs = expo / jnp.sum(expo, axis=-1, keepdims=True)
-        attended = jnp.einsum("ghqs,gsd->gqhd", probs.astype(BF), values, preferred_element_type=F32)
-        attended = attended.reshape(rows, q_cols).astype(BF)
+        queries, keys_values, attended = attend(qkv, cos, sin, allowed, q_cols)
         attn_part = cols_cols(attended, out_w).astype(BF).reshape(micro, 4 * toks, width)
-        return scale_a, normed_a, queries, keys, values, probs, attended, attn_part, far_parts(attn_part)
-
-    scale_a, normed_a, queries, keys, values, probs, attended, attn_part, attn_far = single(
+        return scale_a, normed_a, queries, keys_values, attended, attn_part, far_parts(attn_part)
+
+    scale_a, normed_a, queries, keys_values, attended, attn_part, attn_far = single(
         attention, hid_all, gain_a, qkv_w, out_w, cos, sin, allowed
     )
     attn_part, attn_far, gu_own, gu_peer, cot_near, down_theirs, down_mine = meet(
@@ -532,20 +632,21 @@
     far = far_bits()[0]
     back_mlp, back_far, d_gate, down_sum = meet(back_mlp, back_far, d_gate, down_sum)
     back_far = scatter_far(back_far)
+    d_gate, down_low = meet(d_gate, halve_far(columns(down_sum, 0, cols), z))
+    down_low = swapped(down_low, far)
 
     def gate_grads(normed_m, d_gate):
         return grad_half(1, normed_m, d_gate), grad_half(0, normed_m, d_gate)
 
     gate_send, gate_keep = single(gate_grads, normed_m, d_gate)
-    down_low = halve_far(columns(down_sum, 0, cols), z)
     down_high = halve_far(columns(down_sum, cols, ff), z)
     back_far, gate_send, gate_keep, down_low, down_high = meet(
         back_far, gate_send, gate_keep, down_low, down_high
     )
     gate_got = swap_c(gate_send)
-    ready, gate_got = meet(scatter_prep(back_mlp, back_far), gate_got)
+    ready, gate_keep = meet(scatter_prep(back_mlp, back_far), gate_keep)
     back_near = scatter_near(*ready)
-    down_low = swapped(down_low, far)
+    down_high = swapped(down_high, far)
     gate_pair = gate_keep, gate_got
     d_up, gate_low, gate_high = meet(
         d_up, halve_near(columns(gate_pair, 0, cols), z), halve_near(columns(gate_pair, cols, ff), z)
@@ -571,7 +672,7 @@
     d_mid_low, up_got, inner = meet(d_mid_low, up_got, inner)
     d_mid_near = gather_near(d_mid_low)
     gate_high = swapped(gate_high, 1)
-    down_high = swapped(down_high, far)
+    gate_low = swapped(halve_far(gate_low, z), far)
 
     def mlp_out(inner, down_w):
         part = cols_cols(inner, down_w).astype(BF).reshape(micro, 4 * toks, width)
@@ -580,93 +681,75 @@
     mlp_part, mlp_far = single(mlp_out, inner, down_w)
     up_pair = up_keep, up_got
     up_halves = halve_near(up_pair, z)
-    gate_low = halve_far(gate_low, z)
-    d_mid_near, d_mid_parts, gate_high, down_high, up_halves, gate_low, mlp_part = meet(
-        d_mid_near, diag_parts(d_mid_near), gate_high, down_high, up_halves, gate_low, mlp_part
+    d_mid_near, d_mid_parts, gate_high, up_halves, gate_low, mlp_part = meet(
+        d_mid_near, diag_parts(d_mid_near), gate_high, up_halves, gate_low, mlp_part
     )
     d_mid_diag = gather_diag(d_mid_parts)
     up_sum = swapped(up_halves, 1)
-    gate_halves = side_by_side(gate_low, halve_far(gate_high, z))
-    mlp_far, d_mid_diag, gate_halves, down_sum = meet(
-        mlp_far, d_mid_diag, gate_halves, side_by_side(down_low, down_high)
+    mlp_far, d_mid_diag, gate_high, down_sum = meet(
+        mlp_far, d_mid_diag, halve_far(gate_high, z), side_by_side(down_low, down_high)
     )
     d_mid_all = gather_join(d_mid_near, d_mid_diag).reshape(rows, width)
     mlp_far = scatter_far(mlp_far)
-    gate_sum = swapped(gate_halves, far)
+    gate_high = swapped(gate_high, far)
     down_parts = reduce_y(down_sum, y)
 
-    def attention_back(d_mid_all, out_w, values, probs, attended):
+    def attention_back(d_mid_all, out_w, queries, keys_values, attended, cos, sin, allowed):
         d_att = jnp.dot(d_mid_all, out_w, preferred_element_type=F32).astype(BF)
-        d_att = d_att.reshape(groups, length, heads, HEAD_SIZE)
-        d_probs = jnp.einsum("gqhd,gsd->ghqs", d_att, values, preferred_element_type=F32)
-        inner_sum = jnp.sum(probs * d_probs, axis=-1, keepdims=True)
-        d_scores = (probs * (d_probs - inner_sum)).astype(BF)
-        return d_att, d_scores, grad_half(1, d_mid_all, attended), grad_half(0, d_mid_all, attended)
-
-    d_att, d_scores, out_send, out_keep = single(attention_back, d_mid_all, out_w, values, probs, attended)
-    d_scores, out_send, mlp_far, gate_sum, up_sum, down_parts = meet(
-        d_scores, out_send, mlp_far, gate_sum, up_sum, down_parts
+        d_qkv = attend_back(queries, keys_values, d_att, cos, sin, allowed)
+        return d_qkv, grad_half(1, d_mid_all, attended), grad_half(0, d_mid_all, attended)
+
+    d_qkv, out_send, out_keep = single(
+        attention_back, d_mid_all, out_w, queries, keys_values, attended, cos, sin, allowed
+    )
+    d_qkv, out_send, mlp_far, gate_high, up_sum, down_parts = meet(
+        d_qkv, out_send, mlp_far, gate_high, up_sum, down_parts
     )
     out_got = swap_c(out_send)
-    d_scores, ready, up_halves, out_halves = meet(
-        d_scores,
-        scatter_prep(mlp_part, mlp_far),
-        halve_far(up_sum, z),
-        halve_near((out_keep, out_got), z),
-    )
+    d_qkv, ready, up_halves = meet(d_qkv, scatter_prep(mlp_part, mlp_far), halve_far(up_sum, z))
     mlp_near = scatter_near(*ready)
     up_sum = swapped(up_halves, far)
+    d_qkv, out_halves = meet(d_qkv, halve_near((out_keep, out_got), z))
     out_sum = swapped(out_halves, 1)
-    gate_parts = reduce_y(gate_sum, y)
-
-    def qkv_back(d_scores, d_att, probs, queries, keys, cos, sin, qkv_w, hid_all, scale_a, gain_m_part):
-        d_queries = jnp.einsum("ghqs,gsd->gqhd", d_scores, keys, preferred_element_type=F32) * scale
-        d_keys = jnp.einsum("ghqs,gqhd->gsd", d_scores, queries, preferred_element_type=F32) * scale
-        d_values = jnp.einsum("ghqs,gqhd->gsd", probs.astype(BF), d_att, preferred_element_type=F32)
-        d_q = rotate_back(d_queries, cos[:, :, None], sin[:, :, None]).reshape(rows, q_cols)
-        d_k = rotate_back(d_keys, cos, sin).reshape(rows, kv_cols)
-        d_v = d_values.reshape(rows, kv_cols)
-        d_qkv = jnp.concatenate([d_q, d_k, d_v], axis=1).astype(BF)
+    gate_parts = reduce_y(side_by_side(gate_low, gate_high), y)
+
+    def qkv_back(d_qkv, qkv_w, hid_all, scale_a, gain_m_part, normed_a):
         back = cols_cols(d_qkv, qkv_w)
         unit_a = hid_all.astype(F32).reshape(rows, width) * scale_a
         gain_rows = jnp.stack([jnp.sum(back * unit_a, axis=0), gain_m_part]).reshape(2, 2, nz, 2, block)
         gain_rows = gain_rows.transpose(1, 2, 3, 0, 4)
         back = back.astype(BF).reshape(micro, 4 * toks, width)
-        return d_qkv, back, far_parts(back), gain_rows[1], gain_rows[0]
-
-    d_qkv, back_attn, attn_far, gain_send, gain_keep = single(
-        qkv_back, d_scores, d_att, probs, queries, keys, cos, sin, qkv_w, hid_all, scale_a, gain_m_part
-    )
-    back_attn, attn_far, d_qkv, gain_send, mlp_near, out_sum, up_sum, gate_parts = meet(
-        back_attn, attn_far, d_qkv, gain_send, mlp_near, out_sum, up_sum, gate_parts
+        grads = grad_half(1, normed_a, d_qkv), grad_half(0, normed_a, d_qkv)
+        return back, far_parts(back), gain_rows[1], gain_rows[0], *grads
+
+    back_attn, attn_far, gain_send, gain_keep, qkv_send, qkv_keep = single(
+        qkv_back, d_qkv, qkv_w, hid_all, scale_a, gain_m_part, normed_a
+    )
+    back_attn, attn_far, qkv_send, gain_send, mlp_near, out_sum, up_sum, gate_parts = meet(
+        back_attn, attn_far, qkv_send, gain_send, mlp_near, out_sum, up_sum, gate_parts
     )
     attn_far = scatter_far(attn_far)
     gain_got = swap_c(gain_send)
-    qkv_send = single(lambda a, b: grad_half(1, a, b), normed_a, d_qkv)
-    d_qkv, qkv_send = meet(d_qkv, qkv_send)
     qkv_got = swap_c(qkv_send)
 
-    def keep_halves(normed_a, d_qkv, out_sum):
-        return grad_half(0, normed_a, d_qkv), halve(out_sum, z, far_last())
-
-    qkv_keep, out_halves = single(keep_halves, normed_a, d_qkv, far_steps(out_sum, z))
-    attn_far, qkv_got, gain_got, qkv_keep, out_halves = meet(attn_far, qkv_got, gain_got, qkv_keep, out_halves)
-
-    def near_halves(back_attn, attn_far, qkv_pair, gain_pair):
-        return scatter_prep(back_attn, attn_far), halve(qkv_pair, z, 1), halve(gain_pair, z, 1)
-
-    ready, qkv_halves, gain_halves = single(
-        near_halves, back_attn, attn_far, (qkv_keep, qkv_got), (gain_keep, gain_got)
-    )
-    mlp_near, ready, qkv_halves, gain_halves = meet(mlp_near, ready, qkv_halves, gain_halves)
+    qkv_got, gain_got, out_sum = meet(qkv_got, gain_got, out_sum)
+
+    def tail_halves(qkv_pair, gain_pair, out_pair):
+        return halve(qkv_pair, z, 1), halve(gain_pair, z, 1), halve(out_pair, z, far_last())
+
+    qkv_halves, gain_halves, out_halves = single(
+        tail_halves, (qkv_keep, qkv_got), (gain_keep, gain_got), far_steps(out_sum, z)
+    )
+    attn_far, qkv_halves, gain_halves, out_halves = meet(attn_far, qkv_halves, gain_halves, out_halves)
+    qkv_sum, gain_sum = swapped(qkv_halves, 1), swapped(gain_halves, 1)
+    ready, mlp_near = meet(scatter_prep(back_attn, attn_far), mlp_near)
     attn_near = scatter_near(*ready)
-    qkv_sum, gain_sum = swapped(qkv_halves, 1), swapped(gain_halves, 1)
     out_sum = swapped(out_halves, far)
 
-    def finish_out(mid, mlp_part, from_x, from_y):
-        return (mid + scatter_sum(mlp_part, (from_x, from_y))).astype(BF)
-
-    block_out = regroup(single(finish_out, mid, mlp_part, *mlp_near), block, c, True)
+    def finish_out(mid, mlp_part, mlp_near):
+        return (mid + scatter_sum(mlp_part, mlp_near)).astype(BF)
+
+    block_out = regroup(single(finish_out, mid, mlp_part, mlp_near), block, c, True)
     qkv_sum, gain_sum, block_out = meet(qkv_sum, gain_sum, block_out)
 
     def far_halves(*pairs):

time: 662 us -> 632 us (0.955)
  Pallas kernels: 27.9 us -> 69.7 us
  local copies, waits for them, and re-layouts: 94.7 us -> 62.4 us
  other arithmetic: 137 us -> 109 us
  matrix products: 156 us -> 133 us
  waiting for transfers between devices: 143 us -> 156 us
    pallas_call x0 -> x6, Pallas kernels: none -> 42.9 us  [the longest x1 16.5 us: attend_back(): pl.pallas_call(kernel, out_shape=jax.ShapeDtypeStruct((groups * length, q...]
    ppermute x26, waiting for transfers between devices: 63.6 us -> 87 us  [swap_y(): return lax.ppermute(a, 'y', [(0, 1), (1, 0)])]
    dot_general x5 -> x0, matrix products: 16.9 us -> none  [the longest x1 4.22 us: attention(): jnp.einsum('ghqs,gsd->gqhd', probs.astype(BF), values, preferred_element_...]
    sub x1 -> x0, matrix products: 10.8 us -> none  [attention_back(): d_scores = (probs * (d_probs - inner_sum)).astype(BF)]
    convert_element_type x10 -> x2, other arithmetic: 12.9 us -> 2.74 us  [the longest x1 2.53 us: finish_out(): return (mid + scatter_sum(mlp_part, mlp_near)).astype(BF)]
    ppermute x17, waiting for transfers between devices: 13.9 us -> 4.79 us  [swap_x(): return lax.ppermute(a, 'x', [(0, 1), (1, 0)])]
    another operation x4 -> x2, local copies, waits for them, and re-layouts: 8.62 us -> 0.52 us
    cond x42 -> x10, local copies, waits for them, and re-layouts: 9.96 us -> 2.24 us
  transfers between devices with their start and end apart: 82 -> 83, of which waited for: 29 -> 28; matrix products, arithmetic and copies ran while one was open for 51% -> 44% of each run, Pallas kernels for 4% -> 10%
where the time goes in v4:
time: 632 us; the launch traced here: 621 us
  waiting for transfers between devices  156 us (25%)
  matrix products  133 us (21%)
  other arithmetic  109 us (17%)
  starting transfers between devices  88.3 us (14%)
  Pallas kernels  69.7 us (11%)
  local copies, waits for them, and re-layouts  62.4 us (10%)
    ppermute x26, waiting for transfers between devices, swap_y(): return lax.ppermute(a, 'y', [(0, 1), (1, 0)])  87 us
    ppermute x28, waiting for transfers between devices, swap_z(): return lax.ppermute(a, 'z', [(i, i ^ bit) for i in range(n)])  63.8 us
    dot_general x10, matrix products, rows_rows(): lax.dot_general(left, right, (((0,), (0,)), ((), ())), preferred_element_...  50.1 us
    dot_general x4, matrix products, cols_cols(): lax.dot_general(left, right, (((1,), (1,)), ((), ())), preferred_element_...  42.1 us
    ppermute x28, starting transfers between devices, swap_z(): return lax.ppermute(a, 'z', [(i, i ^ bit) for i in range(n)])  39.5 us
    convert_element_type x13, other arithmetic, halve(): return (keep, send.astype(pair[1].dtype))  30.8 us
    ppermute x26, starting transfers between devices, swap_y(): return lax.ppermute(a, 'y', [(0, 1), (1, 0)])  28.2 us
    pallas_call x3, Pallas kernels, assemble(): pl.pallas_call(kernel, out_shape=out_shape, grid_spec=pltpu.PrefetchScala...  21.6 us
  transfers between devices with their start and end apart: 83, of which 28 were waited for; matrix products, arithmetic and copies ran while one was open for 44% of the time, Pallas kernels for 10%

profile of v4, /device:TPU:0, one launch (start us, length us, event | category | flops | bytes accessed | tf_op | source)
XLA Modules:
  0.0 620.7 jit_solution(3418236495268843960)
XLA Ops:
  17.5 8.3 %collective-permute-done = bf16[1,1,144,1152]{3,2,1,0:T(8,128)(2,1)} collective-permute-done((bf16[1,1,144,1152]{3,2,1,0:T(8,128)(2,1)S(1)}, bf16[1,1,144,1152]{3,2,1,0:T(8,128)(2,1)}, u32[]{:S(2)}, u32[]{:S(2)}) %collective-permute-start) | collective-permute-done | bytes 331808 | tf_op jit(solution)/shard_map/ppermute | solution.py:30
  36.7 14.6 %collective-permute-done.6 = bf16[2,128,2048]{2,1,0:T(8,128)(2,1)} collective-permute-done((bf16[2,128,2048]{2,1,0:T(8,128)(2,1)S(1)}, bf16[2,128,2048]{2,1,0:T(8,128)(2,1)}, u32[]{:S(2)}, u32[]{:S(2)}) %collective-permute-start.6) | collective-permute-done | bytes 1048608 | tf_op jit(solution)/shard_map/ppermute | solution.py:21
  66.1 22.5 %collective-permute-done.9 = bf16[2,128,1024]{2,1,0:T(8,128)(2,1)S(1)} collective-permute-done((bf16[2,128,1024]{2,1,0:T(8,128)(2,1)S(1)}, bf16[2,128,1024]{2,1,0:T(8,128)(2,1)S(1)}, u32[]{:S(2)}, u32[]{:S(2)}) %collective-permute-start.9) | collective-permute-done | bytes 524320 | tf_op jit(solution)/shard_map/ppermute | solution.py:21
  117.9 33.4 %conditional.14 = (f32[1024,1]{0,1:T(1,128)S(1)}, bf16[1024,2048]{1,0:T(8,128)(2,1)}, bf16[1024,512]{1,0:T(8,128)(2,1)}, bf16[1024,128]{1,0:T(8,128)(2,1)}, bf16...) conditional(s32[]{:T(128)} %convert_element_type.471, ...), branch_computations={%region_1.2_spmd, %region_2.4_spmd} | conditional | flops 4848616448 | bytes 75542672 | solution.py:56
  129.3 14.4 %branch_1_fun.2 = (bf16[1024,512]{1,0:T(8,128)(2,1)}, bf16[1024,128]{1,0:T(8,128)(2,1)}, bf16[1024,512]{1,0:T(8,128)(2,1)}) custom-call(f32[1024,640]{1,0:T(8,128)} %fusion.73.qkv_ref, f32[4,256,128]{2,1,0:T(8,128)} %get-tuple-element.155.cos_ref, f32[4,256,128]{2,1,0:T(8,128)} %get-tuple-element.156.sin_ref, f32[4,256,256]{2,1,0:T(8,128)S(1)} %get-tuple-element.157.allowed_ref), custom_call_target="tpu_custom_call" | custom-call | tf_op jit(solution)/shard_map/cond/branch_1_fun/pallas_call | solution.py:383
  154.1 10.5 %collective-permute-done.19.low_ref = bf16[2,128,1024]{2,1,0:T(8,128)(2,1)S(1)} collective-permute-done((bf16[2,128,1024]{2,1,0:T(8,128)(2,1)S(1)}, bf16[2,128,1024]{2,1,0:T(8,128)(2,1)S(1)}, u32[]{:S(2)}, u32[]{:S(2)}) %collective-permute-start.19) | collective-permute-done | bytes 524320 | tf_op jit(solution)/shard_map/ppermute | solution.py:21
  178.7 19.0 %collective-permute-done.25 = bf16[1,1,128,1408]{3,2,1,0:T(8,128)(2,1)S(1)} collective-permute-done((bf16[1,1,128,1408]{3,2,1,0:T(8,128)(2,1)S(1)}, bf16[1,1,128,1408]{3,2,1,0:T(8,128)(2,1)S(1)}, u32[]{:S(2)}, u32[]{:S(2)}) %collective-permute-start.25) | collective-permute-done | bytes 360480 | tf_op jit(solution)/shard_map/ppermute | solution.py:30
  209.8 20.2 %collective-permute-done.28 = bf16[2,128,2048]{2,1,0:T(8,128)(2,1)S(1)} collective-permute-done((bf16[2,128,2048]{2,1,0:T(8,128)(2,1)S(1)}, bf16[2,128,2048]{2,1,0:T(8,128)(2,1)S(1)}, u32[]{:S(2)}, u32[]{:S(2)}) %collective-permute-start.28) | collective-permute-done | bytes 1048608 | tf_op jit(solution)/shard_map/ppermute | solution.py:21
  243.2 9.3 %shard_map.261 = bf16[2,4,2,128,2816]{4,3,2,1,0:T(8,128)(2,1)} custom-call(s32[5]{0:T(128)} %xor_select_fusion.where_ref, bf16[4,1,128,2816]{3,2,1,0:T(8,128)(2,1)} %copy-done.17, bf16[4,1,128,2816]{3,2,1,0:T(8,128)(2,1)} %copy-done.32, bf16[4,1,128,2816]{3,2,1,0:T(8,128)(2,1)} %copy-done.22, bf16[4,1,128,2816]{3,2,1,0:T(8,128)(2,1)} %copy-done.33), custom_call_target="tpu_custom_call" | custom-call | bytes 23068672 | tf_op jit(solution)/shard_map/pallas_call | solution.py:191
  258.9 22.9 %conditional.15 = (f32[1024,2816]{1,0:T(8,128)}, bf16[1024,1408]{1,0:T(8,128)(2,1)S(1)}) conditional(s32[]{:T(128)} %convert_element_type.471, () %tuple.164, (bf16[1024,2048]{1,0:T(8,128)(2,1)S(1)}, bf16[2048,2816]{1,0:T(8,128)(2,1)}) %tuple.314), branch_computations={%region_5.6_spmd, %region_6.7_spmd} | conditional | flops 11819810816 | bytes 41680912 | solution.py:56
  258.9 17.5 %fusion.72 = f32[1024,2816]{1,0:T(8,128)} fusion(bf16[1024,2048]{1,0:T(8,128)(2,1)S(1)} %get-tuple-element.162, bf16[2048,2816]{1,0:T(8,128)(2,1)} %get-tuple-element.163), kind=kOutput, calls=%fused_computation.238 | convolution fusion | flops 11811160064 | bytes 27262976 | tf_op jit(solution)/shard_map/cond/branch_1_fun/dot_general | solution.py:598
  313.0 36.0 %conditional.17 = (bf16[1024,1408]{1,0:T(8,128)(2,1)}, bf16[1024,1408]{1,0:T(8,128)(2,1)}, bf16[2,512,2048]{2,1,0:T(8,128)(2,1)}, bf16[2,128,1024]{2,1,0:T(8,128)(2,1)}, bf16[2,128,1024]{2,1,0:T(8,128)(2,1)}) conditional(s32[]{:T(128)} %convert_element_type.471, () %tuple.163, (bf16[1024,2048]{1,0:T(8,128)(2,1)}, bf16[2048,1408]{1,0:T(8,128)(2,1)}, ...), branch_computations={%region_9.10_spmd, %region_10.11_spmd} | conditional | flops 17749114880 | bytes 50855976 | solution.py:56
  313.0 15.4 %multiply_convert_fusion = (bf16[1024,1408]{1,0:T(8,128)(2,1)}, bf16[1024,1408]{1,0:T(8,128)(2,1)}) fusion(f32[1024,2816]{1,0:T(8,128)} %get-tuple-element.168, bf16[1024,2048]{1,0:T(8,128)(2,1)} %get-tuple-element.166, bf16[2048,1408]{1,0:T(8,128)(2,1)} %get-tuple-element.167), kind=kOutput, calls=%fused_computation.16 | convolution fusion | flops 5924323328 | bytes 27262976 | tf_op jit(solution)/shard_map/cond/branch_1_fun/dot_general | solution.py:615
  328.5 18.4 %fusion.10 = bf16[1024,2048]{1,0:T(8,128)(2,1)} fusion(bf16[2048,2816]{1,0:T(8,128)(2,1)} %get-tuple-element.169, bf16[1024,1408]{1,0:T(8,128)(2,1)} %get-tuple-element.910, bf16[1024,1408]{1,0:T(8,128)(2,1)} %get-tuple-element.909), kind=kOutput, calls=%fused_computation.19 | convolution fusion | flops 11824791552 | bytes 21495808 | tf_op jit(solution)/shard_map/cond/branch_1_fun/dot_general | solution.py:331
  356.1 12.4 %conditional.18 = (bf16[4,2,128,1408]{3,2,1,0:T(8,128)(2,1)}, bf16[4,2,128,1408]{3,2,1,0:T(8,128)(2,1)S(1)}) conditional(s32[]{:T(128)} %convert_element_type.471, () %tuple.175, (bf16[1024,2048]{1,0:T(8,128)(2,1)S(1)}, bf16[1024,1408]{1,0:T(8,128)(2,1)}) %tuple.315), branch_computations={%region_11.12_spmd, %region_12.13_spmd} | conditional | flops 5908463616 | bytes 15728656 | solution.py:56
  387.9 12.5 %conditional.19 = (bf16[4,2,128,1408]{3,2,1,0:T(8,128)(2,1)}, bf16[4,2,128,1408]{3,2,1,0:T(8,128)(2,1)S(1)}) conditional(s32[]{:T(128)} %convert_element_type.471, () %tuple.181, (bf16[1024,2048]{1,0:T(8,128)(2,1)S(1)}, bf16[1024,1408]{1,0:T(8,128)(2,1)}) %tuple.316), branch_computations={%region_13.14_spmd, %region_14.15_spmd} | conditional | flops 5908463616 | bytes 15728656 | solution.py:56
  400.4 9.6 %collective-permute-done.48 = bf16[1,2,128,640]{3,2,1,0:T(8,128)(2,1)S(1)} collective-permute-done((bf16[1,2,128,640]{3,2,1,0:T(8,128)(2,1)}, bf16[1,2,128,640]{3,2,1,0:T(8,128)(2,1)S(1)}, u32[]{:S(2)}, u32[]{:S(2)}) %collective-permute-start.48) | collective-permute-done | bytes 327712 | tf_op jit(solution)/shard_map/ppermute | solution.py:30
  426.2 13.1 %conditional.21 = (bf16[2,512,2048]{2,1,0:T(8,128)(2,1)}, bf16[2,128,1024]{2,1,0:T(8,128)(2,1)}, bf16[2,128,1024]{2,1,0:T(8,128)(2,1)}) conditional(s32[]{:T(128)} %convert_element_type.471, () %tuple.186, (bf16[1024,1408]{1,0:T(8,128)(2,1)S(1)}, bf16[2048,1408]{1,0:T(8,128)(2,1)}) %tuple.321), branch_computations={%region_19.20_spmd, %region_20.21_spmd} | conditional | flops 5907677184 | bytes 14942232 | solution.py:56
  426.2 10.9 %convolution_convert_fusion.6 = bf16[1024,2048]{1,0:T(8,128)(2,1)} fusion(bf16[1024,1408]{1,0:T(8,128)(2,1)S(1)} %get-tuple-element.181, bf16[2048,1408]{1,0:T(8,128)(2,1)} %get-tuple-element.182), kind=kOutput, calls=%fused_computation.35 | convolution fusion | flops 5907677184 | bytes 12845056 | tf_op jit(solution)/shard_map/cond/branch_1_fun/dot_general | solution.py:331
  471.5 26.9 %conditional.22 = (bf16[1024,640]{1,0:T(8,128)(2,1)}, bf16[4,2,128,512]{3,2,1,0:T(8,128)(2,1)}, bf16[2,2,2,128,512]{4,3,2,1,0:T(8,128)(2,1)}) conditional(s32[]{:T(128)} %convert_element_type.471, () %tuple.153, (bf16[2,512,2048]{2,1,0:T(8,128)(2,1)S(1)}, bf16[2048,512]{1,0:T(8,128)(2,1)S(1)}, bf16[1024,512]{1,0:T(8,128)(2,1)}, ...), branch_computations={%region_21.22_spmd, %region_22.23_spmd} | conditional | flops 4296540160 | bytes 15728664 | solution.py:56
  481.8 16.5 %branch_1_fun.3 = bf16[1024,640]{1,0:T(8,128)(2,1)} custom-call(bf16[1024,512]{1,0:T(8,128)(2,1)} %get-tuple-element.183.q_ref, bf16[1024,128]{1,0:T(8,128)(2,1)} %get-tuple-element.184.kv_ref, bf16[1024,512]{1,0:T(8,128)(2,1)} %convolution_convert_fusion.7.d_ref, f32[4,256,128]{2,1,0:T(8,128)} %get-tuple-element.187.cos_ref, ...), custom_call_target="tpu_custom_call" | custom-call | tf_op jit(solution)/shard_map/cond/branch_1_fun/pallas_call | solution.py:428
  518.4 16.3 %conditional.23 = (bf16[2,512,2048]{2,1,0:T(8,128)(2,1)}, bf16[2,128,1024]{2,1,0:T(8,128)(2,1)}, bf16[2,128,1024]{2,1,0:T(8,128)(2,1)}, f32[4,2,2,128]{3,1,0,2:T...) conditional(s32[]{:T(128)} %convert_element_type.471, ...), branch_computations={%region_23.24_spmd, %region_24.26_spmd} | conditional | flops 5380507648 | bytes 23932984 | solution.py:56
  578.0 10.2 %collective-permute-done.72 = f32[2,2,2,128]{3,2,1,0:T(2,128)S(1)} collective-permute-done((f32[2,2,2,128]{3,2,1,0:T(2,128)S(1)}, f32[2,2,2,128]{3,2,1,0:T(2,128)S(1)}, u32[]{:S(2)}, u32[]{:S(2)}) %collective-permute-start.72) | collective-permute-done | bytes 4128 | tf_op jit(solution)/shard_map/ppermute | solution.py:30
  599.6 6.9 %conditional.27 = (f32[256,2048]{1,0:T(8,128)S(1)}) conditional(s32[]{:T(128)} %convert_element_type.471, () %tuple.204, (f32[1024,1]{0,1:T(1,128)S(1)}, bf16[2,512,2048]{2,1,0:T(8,128)(2,1)}, bf16[2,128,2048]{2,1,0:T(8,128)(2,1)}, bf16[2,128,2048]{2,1,0:T(8,128)(2,1)}, f32[2,4,2,1,128]{4,3,2,1,0:T(1,128)S(1)}, ...), branch_computations={%region_32.33_spmd, %region_33.35_spmd} | conditional | flops 11534336 | bytes 21012528 | solution.py:56
  (485 shorter events, 422.8 us)
Async XLA Ops:
  55.8 32.8 %collective-permute-start.7 = (bf16[2,1,144,1152]{3,2,1,0:T(8,128)(2,1)S(1)}, bf16[2,1,144,1152]{3,2,1,0:T(8,128)(2,1)S(1)}, u32[]{:S(2)}, u32[]{:S(2)}) collective-permute-start(bf16[2,1,144,1152]{3,2,1,0:T(8,128)(2,1)S(1)} %constant_dynamic-update-slice_fusion.2), channel_id=1, source_target_pairs={{0,8},{8,0},{16,24},{24,16},{1,9},{9,1},{17,25},{25,17},{2,10},{10... | collective-permute-start | bytes 1990664 | tf_op jit(solution)/shard_map/ppermute | solution.py:30
  59.2 33.0 %collective-permute-start.8 = (bf16[1,1,128,2816]{3,2,1,0:T(8,128)(2,1)S(1)}, bf16[1,1,128,2816]{3,2,1,0:T(8,128)(2,1)S(1)}, u32[]{:S(2)}, u32[]{:S(2)}) collective-permute-start(bf16[1,1,128,2816]{3,2,1,0:T(8,128)(2,1)S(1)} %bitcast.239), channel_id=1, source_target_pairs={{0,16},{8,24},{16,0},{24,8},{1,17},{9,25},{17,1},{25,9},{2,18},{10... | collective-permute-start | bytes 2162696 | tf_op jit(solution)/shard_map/ppermute | solution.py:30
  60.9 31.3 %collective-permute-start.11 = (bf16[128,2816]{1,0:T(8,128)(2,1)S(1)}, bf16[128,2816]{1,0:T(8,128)(2,1)}, u32[]{:S(2)}, u32[]{:S(2)}) collective-permute-start(bf16[128,2816]{1,0:T(8,128)(2,1)S(1)} %copy-done.49), channel_id=1, source_target_pairs={{0,4},{4,0},{1,5},{5,1},{2,6},{6,2},{3,7},{7,3},{8,12},{12,8},{9,1... | collective-permute-start | bytes 2162696 | tf_op jit(solution)/shard_map/ppermute | solution.py:21
  94.8 56.6 %collective-permute-start.14 = (bf16[2,1,128,2816]{3,2,1,0:T(8,128)(2,1)}, bf16[2,1,128,2816]{3,2,1,0:T(8,128)(2,1)}, u32[]{:S(2)}, u32[]{:S(2)}) collective-permute-start(bf16[2,1,128,2816]{3,2,1,0:T(8,128)(2,1)} %constant_dynamic-update-slice_fusion.6), channel_id=1, source_target_pairs={{0,8},{8,0},{16,24},{24,16},{1,9},{9,1},{17,25},{25,17},{2,10},{10... | collective-permute-start | bytes 4325384 | tf_op jit(solution)/shard_map/ppermute | solution.py:30
  98.2 53.1 %collective-permute-start.17 = (bf16[2,128,2048]{2,1,0:T(8,128)(2,1)S(1)}, bf16[2,128,2048]{2,1,0:T(8,128)(2,1)}, u32[]{:S(2)}, u32[]{:S(2)}) collective-permute-start(bf16[2,128,2048]{2,1,0:T(8,128)(2,1)S(1)} %bitcast.216), channel_id=1, source_target_pairs={{0,4},{4,0},{1,5},{5,1},{2,6},{6,2},{3,7},{7,3},{8,12},{12,8},{9,1... | collective-permute-start | bytes 3145736 | tf_op jit(solution)/shard_map/ppermute | solution.py:21
  98.9 52.4 %collective-permute-start.16 = (bf16[2,128,2048]{2,1,0:T(8,128)(2,1)S(1)}, bf16[2,128,2048]{2,1,0:T(8,128)(2,1)}, u32[]{:S(2)}, u32[]{:S(2)}) collective-permute-start(bf16[2,128,2048]{2,1,0:T(8,128)(2,1)S(1)} %bitcast.217), channel_id=1, source_target_pairs={{0,1},{1,0},{2,3},{3,2},{4,5},{5,4},{6,7},{7,6},{8,9},{9,8},{10,11... | collective-permute-start | bytes 3145736 | tf_op jit(solution)/shard_map/ppermute | solution.py:17
  102.8 48.6 %collective-permute-start.15 = (bf16[1,1,128,2816]{3,2,1,0:T(8,128)(2,1)}, bf16[1,1,128,2816]{3,2,1,0:T(8,128)(2,1)}, u32[]{:S(2)}, u32[]{:S(2)}) collective-permute-start(bf16[1,1,128,2816]{3,2,1,0:T(8,128)(2,1)} %bitcast.49), channel_id=1, source_target_pairs={{0,16},{8,24},{16,0},{24,8},{1,17},{9,25},{17,1},{25,9},{2,18},{10... | collective-permute-start | bytes 2162696 | tf_op jit(solution)/shard_map/ppermute | solution.py:30
  110.2 41.1 %collective-permute-start.18 = (bf16[128,1408]{1,0:T(8,128)(2,1)}, bf16[128,1408]{1,0:T(8,128)(2,1)S(1)}, u32[]{:S(2)}, u32[]{:S(2)}) collective-permute-start(bf16[128,1408]{1,0:T(8,128)(2,1)} %get-tuple-element.526), channel_id=1, source_target_pairs={{0,4},{4,0},{1,5},{5,1},{2,6},{6,2},{3,7},{7,3},{8,12},{12,8},{9,1... | collective-permute-start | bytes 1081352 | tf_op jit(solution)/shard_map/ppermute | solution.py:21
  200.9 31.9 %collective-permute-start.29 = (bf16[4,1,128,2816]{3,2,1,0:T(8,128)(2,1)S(1)}, bf16[4,1,128,2816]{3,2,1,0:T(8,128)(2,1)S(1)}, u32[]{:S(2)}, u32[]{:S(2)}) collective-permute-start(bf16[4,1,128,2816]{3,2,1,0:T(8,128)(2,1)S(1)} %constant_dynamic-update-slice_fusion.10.peer), channel_id=1, source_target_pairs={{0,2},{2,0},{1,3},{3,1},{4,6},{6,4},{5,7},{7,5},{8,10},{10,8},{9,1... | collective-permute-start | bytes 8650760 | tf_op jit(solution)/shard_map/ppermute | solution.py:25
  311.4 37.7 %collective-permute-start.40 = (bf16[2,2,128,1408]{3,2,1,0:T(8,128)(2,1)}, bf16[2,2,128,1408]{3,2,1,0:T(8,128)(2,1)}, u32[]{:S(2)}, u32[]{:S(2)}) collective-permute-start(bf16[2,2,128,1408]{3,2,1,0:T(8,128)(2,1)} %fusion.42), channel_id=1, source_target_pairs={{0,8},{8,0},{16,24},{24,16},{1,9},{9,1},{17,25},{25,17},{2,10},{10... | collective-permute-start | bytes 4325384 | tf_op jit(solution)/shard_map/ppermute | solution.py:30
  376.8 33.2 %collective-permute-start.44 = (bf16[2,128,2048]{2,1,0:T(8,128)(2,1)}, bf16[2,128,2048]{2,1,0:T(8,128)(2,1)}, u32[]{:S(2)}, u32[]{:S(2)}) collective-permute-start(bf16[2,128,2048]{2,1,0:T(8,128)(2,1)} %get-tuple-element.604), channel_id=1, source_target_pairs={{0,1},{1,0},{2,3},{3,2},{4,5},{5,4},{6,7},{7,6},{8,9},{9,8},{10,11... | collective-permute-start | bytes 3145736 | tf_op jit(solution)/shard_map/ppermute | solution.py:17
  377.9 32.1 %collective-permute-start.45 = (bf16[2,128,2048]{2,1,0:T(8,128)(2,1)}, bf16[2,128,2048]{2,1,0:T(8,128)(2,1)}, u32[]{:S(2)}, u32[]{:S(2)}) collective-permute-start(bf16[2,128,2048]{2,1,0:T(8,128)(2,1)} %get-tuple-element.605), channel_id=1, source_target_pairs={{0,4},{4,0},{1,5},{5,1},{2,6},{6,2},{3,7},{7,3},{8,12},{12,8},{9,1... | collective-permute-start | bytes 3145736 | tf_op jit(solution)/shard_map/ppermute | solution.py:21
  421.1 27.6 %collective-permute-start.52 = (bf16[2,2,128,640]{3,2,1,0:T(8,128)(2,1)}, bf16[2,2,128,640]{3,2,1,0:T(8,128)(2,1)}, u32[]{:S(2)}, u32[]{:S(2)}) collective-permute-start(bf16[2,2,128,640]{3,2,1,0:T(8,128)(2,1)} %get-tuple-element.626), channel_id=1, source_target_pairs={{0,8},{8,0},{16,24},{24,16},{1,9},{9,1},{17,25},{25,17},{2,10},{10... | collective-permute-start | bytes 1966088 | tf_op jit(solution)/shard_map/ppermute | solution.py:30
  448.6 49.8 %collective-permute-start.59 = (bf16[2,2,128,1408]{3,2,1,0:T(8,128)(2,1)}, bf16[2,2,128,1408]{3,2,1,0:T(8,128)(2,1)}, u32[]{:S(2)}, u32[]{:S(2)}) collective-permute-start(bf16[2,2,128,1408]{3,2,1,0:T(8,128)(2,1)} %get-tuple-element.658), channel_id=1, source_target_pairs={{0,8},{8,0},{16,24},{24,16},{1,9},{9,1},{17,25},{25,17},{2,10},{10... | collective-permute-start | bytes 4325384 | tf_op jit(solution)/shard_map/ppermute | solution.py:30
  463.1 35.3 %collective-permute-start.58 = (bf16[1,2,128,640]{3,2,1,0:T(8,128)(2,1)}, bf16[1,2,128,640]{3,2,1,0:T(8,128)(2,1)}, u32[]{:S(2)}, u32[]{:S(2)}) collective-permute-start(bf16[1,2,128,640]{3,2,1,0:T(8,128)(2,1)} %get-tuple-element.656), channel_id=1, source_target_pairs={{0,16},{8,24},{16,0},{24,8},{1,17},{9,25},{17,1},{25,9},{2,18},{10... | collective-permute-start | bytes 983048 | tf_op jit(solution)/shard_map/ppermute | solution.py:30
  464.8 33.6 %collective-permute-start.56 = (bf16[2,128,1024]{2,1,0:T(8,128)(2,1)}, bf16[2,128,1024]{2,1,0:T(8,128)(2,1)}, u32[]{:S(2)}, u32[]{:S(2)}) collective-permute-start(bf16[2,128,1024]{2,1,0:T(8,128)(2,1)} %get-tuple-element.653), channel_id=1, source_target_pairs={{0,4},{4,0},{1,5},{5,1},{2,6},{6,2},{3,7},{7,3},{8,12},{12,8},{9,1... | collective-permute-start | bytes 1572872 | tf_op jit(solution)/shard_map/ppermute | solution.py:21
  466.3 32.1 %collective-permute-start.57 = (bf16[2,128,1024]{2,1,0:T(8,128)(2,1)}, bf16[2,128,1024]{2,1,0:T(8,128)(2,1)}, u32[]{:S(2)}, u32[]{:S(2)}) collective-permute-start(bf16[2,128,1024]{2,1,0:T(8,128)(2,1)} %get-tuple-element.654), channel_id=1, source_target_pairs={{0,1},{1,0},{2,3},{3,2},{4,5},{5,4},{6,7},{7,6},{8,9},{9,8},{10,11... | collective-permute-start | bytes 1572872 | tf_op jit(solution)/shard_map/ppermute | solution.py:17
  468.0 30.4 %collective-permute-start.60 = (bf16[128,1408]{1,0:T(8,128)(2,1)}, bf16[128,1408]{1,0:T(8,128)(2,1)}, u32[]{:S(2)}, u32[]{:S(2)}) collective-permute-start(bf16[128,1408]{1,0:T(8,128)(2,1)} %get-tuple-element.826), channel_id=1, source_target_pairs={{0,4},{4,0},{1,5},{5,1},{2,6},{6,2},{3,7},{7,3},{8,12},{12,8},{9,1... | collective-permute-start | bytes 1081352 | tf_op jit(solution)/shard_map/ppermute | solution.py:21
  506.5 37.7 %collective-permute-start.62 = (bf16[2,128,2048]{2,1,0:T(8,128)(2,1)}, bf16[2,128,2048]{2,1,0:T(8,128)(2,1)}, u32[]{:S(2)}, u32[]{:S(2)}) collective-permute-start(bf16[2,128,2048]{2,1,0:T(8,128)(2,1)} %get-tuple-element.681), channel_id=1, source_target_pairs={{0,1},{1,0},{2,3},{3,2},{4,5},{5,4},{6,7},{7,6},{8,9},{9,8},{10,11... | collective-permute-start | bytes 3145736 | tf_op jit(solution)/shard_map/ppermute | solution.py:17
  507.4 36.8 %collective-permute-start.63 = (bf16[2,128,2048]{2,1,0:T(8,128)(2,1)}, bf16[2,128,2048]{2,1,0:T(8,128)(2,1)}, u32[]{:S(2)}, u32[]{:S(2)}) collective-permute-start(bf16[2,128,2048]{2,1,0:T(8,128)(2,1)} %get-tuple-element.682), channel_id=1, source_target_pairs={{0,4},{4,0},{1,5},{5,1},{2,6},{6,2},{3,7},{7,3},{8,12},{12,8},{9,1... | collective-permute-start | bytes 3145736 | tf_op jit(solution)/shard_map/ppermute | solution.py:21
  509.7 34.5 %collective-permute-start.65 = (bf16[1,2,128,1408]{3,2,1,0:T(8,128)(2,1)}, bf16[1,2,128,1408]{3,2,1,0:T(8,128)(2,1)}, u32[]{:S(2)}, u32[]{:S(2)}) collective-permute-start(bf16[1,2,128,1408]{3,2,1,0:T(8,128)(2,1)} %get-tuple-element.686), channel_id=1, source_target_pairs={{0,16},{8,24},{16,0},{24,8},{1,17},{9,25},{17,1},{25,9},{2,18},{10... | collective-permute-start | bytes 2162696 | tf_op jit(solution)/shard_map/ppermute | solution.py:30
  514.9 29.3 %collective-permute-start.64 = (bf16[2,2,128,512]{3,2,1,0:T(8,128)(2,1)}, bf16[2,2,128,512]{3,2,1,0:T(8,128)(2,1)S(1)}, u32[]{:S(2)}, u32[]{:S(2)}) collective-permute-start(bf16[2,2,128,512]{3,2,1,0:T(8,128)(2,1)} %get-tuple-element.684), channel_id=1, source_target_pairs={{0,8},{8,0},{16,24},{24,16},{1,9},{9,1},{17,25},{25,17},{2,10},{10... | collective-permute-start | bytes 1572872 | tf_op jit(solution)/shard_map/ppermute | solution.py:30
  562.7 28.8 %collective-permute-start.73 = (bf16[2,128,2048]{2,1,0:T(8,128)(2,1)}, bf16[2,128,2048]{2,1,0:T(8,128)(2,1)}, u32[]{:S(2)}, u32[]{:S(2)}) collective-permute-start(bf16[2,128,2048]{2,1,0:T(8,128)(2,1)} %get-tuple-element.723), channel_id=1, source_target_pairs={{0,1},{1,0},{2,3},{3,2},{4,5},{5,4},{6,7},{7,6},{8,9},{9,8},{10,11... | collective-permute-start | bytes 3145736 | tf_op jit(solution)/shard_map/ppermute | solution.py:17
  564.0 27.5 %collective-permute-start.74 = (bf16[2,128,2048]{2,1,0:T(8,128)(2,1)}, bf16[2,128,2048]{2,1,0:T(8,128)(2,1)}, u32[]{:S(2)}, u32[]{:S(2)}) collective-permute-start(bf16[2,128,2048]{2,1,0:T(8,128)(2,1)} %get-tuple-element.724), channel_id=1, source_target_pairs={{0,4},{4,0},{1,5},{5,1},{2,6},{6,2},{3,7},{7,3},{8,12},{12,8},{9,1... | collective-permute-start | bytes 3145736 | tf_op jit(solution)/shard_map/ppermute | solution.py:21
  (137 other events, 2300.9 us)

commit v5 on v4

--- a/solution.py
+++ b/solution.py
@@ -496,6 +496,21 @@
     attn_theirs = swap_y(pack_attn(1 - y))
     other_ids = swap_y(segment_ids[:, 0])
     own_far, attn_theirs, other_ids, hid = meet(own_far, attn_theirs, other_ids, hidden_in[:, 0])
+    length = 2 * toks
+    groups = micro * 2
+    ids = jnp.stack([segment_ids[:, 0], other_ids], axis=1).reshape(groups, length)
+    ids = jnp.where(x == 0, ids, jnp.roll(ids, toks, axis=1))
+    pos = (jnp.arange(length, dtype=jnp.int32) + toks * x) % length
+    same = ids[:, :, None] == ids[:, None, :]
+    allowed = jnp.logical_and(same, (pos[None, :] <= pos[:, None])[None])
+    places = jnp.sum(allowed.astype(F32), axis=2) - 1.0
+    freq = jnp.arange(HEAD_SIZE // 2, dtype=F32)
+    inverse = 10000.0 ** (-2.0 * freq / HEAD_SIZE)
+    angles = places[:, :, None] * inverse
+    cos = jnp.concatenate([jnp.cos(angles)] * 4, axis=-1)
+    sin = jnp.concatenate([jnp.sin(angles)] * 4, axis=-1)
+    allowed = allowed.swapaxes(1, 2).astype(F32)
+
     peer_far = z_first(attn_theirs)
     attn_own = z_rest(own_far)
     hid = regroup(hid, block, c)
@@ -509,8 +524,8 @@
     gu_theirs = swap_y(gu_give)
     attn_own = both(attn_own)
     cot = regroup(out_cotangent[:, 0], block, c)
-    attn_peer, gu_far, hid_diag, gu_theirs, attn_own, cot, down_give = meet(
-        attn_peer, gu_far, hid_diag, gu_theirs, attn_own, cot, pack_down(1 - y)
+    attn_peer, gu_far, hid_diag, gu_theirs, attn_own, cot, down_give, cos, sin, allowed = meet(
+        attn_peer, gu_far, hid_diag, gu_theirs, attn_own, cot, pack_down(1 - y), cos, sin, allowed
     )
     attn_own_c = swap_c(attn_own)
     attn_peer = both(attn_peer)
@@ -527,21 +542,6 @@
     gain_a = gains[:, :, :, 0].reshape(width)
     gain_m = gains[:, :, :, 1].reshape(width)
 
-    length = 2 * toks
-    groups = micro * 2
-    ids = jnp.stack([segment_ids[:, 0], other_ids], axis=1).reshape(groups, length)
-    ids = jnp.where(x == 0, ids, jnp.roll(ids, toks, axis=1))
-    pos = (jnp.arange(length, dtype=jnp.int32) + toks * x) % length
-    same = ids[:, :, None] == ids[:, None, :]
-    allowed = jnp.logical_and(same, (pos[None, :] <= pos[:, None])[None])
-    places = jnp.sum(allowed.astype(F32), axis=2) - 1.0
-    freq = jnp.arange(HEAD_SIZE // 2, dtype=F32)
-    inverse = 10000.0 ** (-2.0 * freq / HEAD_SIZE)
-    angles = places[:, :, None] * inverse
-    cos = jnp.concatenate([jnp.cos(angles)] * 4, axis=-1)
-    sin = jnp.concatenate([jnp.sin(angles)] * 4, axis=-1)
-    allowed = allowed.swapaxes(1, 2).astype(F32)
-
     rows = micro * 4 * toks
     heads = q_cols // HEAD_SIZE
 
@@ -632,26 +632,24 @@
     far = far_bits()[0]
     back_mlp, back_far, d_gate, down_sum = meet(back_mlp, back_far, d_gate, down_sum)
     back_far = scatter_far(back_far)
-    d_gate, down_low = meet(d_gate, halve_far(columns(down_sum, 0, cols), z))
+    d_gate, down_low = meet(d_gate, halve_far(columns(down_sum, 0, ff - cols), z))
     down_low = swapped(down_low, far)
 
     def gate_grads(normed_m, d_gate):
         return grad_half(1, normed_m, d_gate), grad_half(0, normed_m, d_gate)
 
     gate_send, gate_keep = single(gate_grads, normed_m, d_gate)
-    down_high = halve_far(columns(down_sum, cols, ff), z)
+    down_high = halve_far(columns(down_sum, ff - cols, ff), z)
     back_far, gate_send, gate_keep, down_low, down_high = meet(
         back_far, gate_send, gate_keep, down_low, down_high
     )
     gate_got = swap_c(gate_send)
     ready, gate_keep = meet(scatter_prep(back_mlp, back_far), gate_keep)
     back_near = scatter_near(*ready)
-    down_high = swapped(down_high, far)
     gate_pair = gate_keep, gate_got
-    d_up, gate_low, gate_high = meet(
-        d_up, halve_near(columns(gate_pair, 0, cols), z), halve_near(columns(gate_pair, cols, ff), z)
-    )
+    d_up, gate_low, gate_pair = meet(d_up, halve_near(columns(gate_pair, 0, cols), z), gate_pair)
     gate_low = swapped(gate_low, 1)
+    gate_high = halve_near(columns(gate_pair, cols, ff), z)
 
     def up_grads(normed_m, d_up):
         return grad_half(1, normed_m, d_up), grad_half(0, normed_m, d_up)
@@ -672,7 +670,8 @@
     d_mid_low, up_got, inner = meet(d_mid_low, up_got, inner)
     d_mid_near = gather_near(d_mid_low)
     gate_high = swapped(gate_high, 1)
-    gate_low = swapped(halve_far(gate_low, z), far)
+    gate_low = far_steps(gate_low, z)
+    gate_low = swapped(single(lambda *p: halve(p, z, far_last()), *gate_low), far)
 
     def mlp_out(inner, down_w):
         part = cols_cols(inner, down_w).astype(BF).reshape(micro, 4 * toks, width)
@@ -680,19 +679,17 @@
 
     mlp_part, mlp_far = single(mlp_out, inner, down_w)
     up_pair = up_keep, up_got
-    up_halves = halve_near(up_pair, z)
+    up_halves = single(lambda *p: halve(p, z, 1), *up_pair)
     d_mid_near, d_mid_parts, gate_high, up_halves, gate_low, mlp_part = meet(
         d_mid_near, diag_parts(d_mid_near), gate_high, up_halves, gate_low, mlp_part
     )
     d_mid_diag = gather_diag(d_mid_parts)
     up_sum = swapped(up_halves, 1)
-    mlp_far, d_mid_diag, gate_high, down_sum = meet(
-        mlp_far, d_mid_diag, halve_far(gate_high, z), side_by_side(down_low, down_high)
-    )
+    mlp_far, d_mid_diag, gate_high, down_high = meet(mlp_far, d_mid_diag, halve_far(gate_high, z), down_high)
     d_mid_all = gather_join(d_mid_near, d_mid_diag).reshape(rows, width)
     mlp_far = scatter_far(mlp_far)
     gate_high = swapped(gate_high, far)
-    down_parts = reduce_y(down_sum, y)
+    down_high = swapped(down_high, far)
 
     def attention_back(d_mid_all, out_w, queries, keys_values, attended, cos, sin, allowed):
         d_att = jnp.dot(d_mid_all, out_w, preferred_element_type=F32).astype(BF)
@@ -702,16 +699,17 @@
     d_qkv, out_send, out_keep = single(
         attention_back, d_mid_all, out_w, queries, keys_values, attended, cos, sin, allowed
     )
-    d_qkv, out_send, mlp_far, gate_high, up_sum, down_parts = meet(
-        d_qkv, out_send, mlp_far, gate_high, up_sum, down_parts
+    d_qkv, out_send, mlp_far, gate_high, up_sum, down_high = meet(
+        d_qkv, out_send, mlp_far, gate_high, up_sum, down_high
     )
     out_got = swap_c(out_send)
-    d_qkv, ready, up_halves = meet(d_qkv, scatter_prep(mlp_part, mlp_far), halve_far(up_sum, z))
+    up_sum, ready = meet(up_sum, scatter_prep(mlp_part, mlp_far))
     mlp_near = scatter_near(*ready)
+    d_qkv, up_halves = meet(d_qkv, halve_far(up_sum, z))
     up_sum = swapped(up_halves, far)
     d_qkv, out_halves = meet(d_qkv, halve_near((out_keep, out_got), z))
     out_sum = swapped(out_halves, 1)
-    gate_parts = reduce_y(side_by_side(gate_low, gate_high), y)
+    down_parts = reduce_y(side_by_side(down_low, down_high), y)
 
     def qkv_back(d_qkv, qkv_w, hid_all, scale_a, gain_m_part, normed_a):
         back = cols_cols(d_qkv, qkv_w)
@@ -725,8 +723,16 @@
     back_attn, attn_far, gain_send, gain_keep, qkv_send, qkv_keep = single(
         qkv_back, d_qkv, qkv_w, hid_all, scale_a, gain_m_part, normed_a
     )
-    back_attn, attn_far, qkv_send, gain_send, mlp_near, out_sum, up_sum, gate_parts = meet(
-        back_attn, attn_far, qkv_send, gain_send, mlp_near, out_sum, up_sum, gate_parts
+    back_attn, attn_far, qkv_send, gain_send, mlp_near, out_sum, up_sum, down_parts, gate_sum = meet(
+        back_attn,
+        attn_far,
+        qkv_send,
+        gain_send,
+        mlp_near,
+        out_sum,
+        up_sum,
+        down_parts,
+        side_by_side(gate_low, gate_high),
     )
     attn_far = scatter_far(attn_far)
     gain_got = swap_c(gain_send)
@@ -759,6 +765,7 @@
     attn_near, qkv_halves, gain_halves, out_sum = meet(attn_near, qkv_halves, gain_halves, out_sum)
     qkv_sum, gain_sum = swapped(qkv_halves, far), swapped(gain_halves, far)
     up_parts = reduce_y(up_sum, y)
+    gate_parts = reduce_y(gate_sum, y)
     out_parts = reduce_y(out_sum, y)
 
     def finish_grad(back_attn, from_x, from_y, hid, scale_a, gain_a, d_mid):
@@ -768,8 +775,8 @@
 
     input_grad = single(finish_grad, back_attn, *attn_near, hid, scale_a, gain_a, d_mid)
     input_grad = regroup(input_grad, block, c, True)
-    input_grad, qkv_sum, gain_sum, up_parts, out_parts = meet(
-        input_grad, qkv_sum, gain_sum, up_parts, out_parts
+    input_grad, qkv_sum, gain_sum, up_parts, gate_parts, out_parts = meet(
+        input_grad, qkv_sum, gain_sum, up_parts, gate_parts, out_parts
     )
     gain_parts = reduce_y(gain_sum, y)
     qkv_parts = reduce_y(qkv_sum, y)

time: 632 us -> 619 us (0.979)
  waiting for transfers between devices: 156 us -> 145 us
    ppermute x28, waiting for transfers between devices: 63.8 us -> 47.1 us  [swap_z(): return lax.ppermute(a, 'z', [(i, i ^ bit) for i in range(n)])]
    unnamed x161 -> x183, local copies, waits for them, and re-layouts: 21 us -> 22.2 us
  transfers between devices with their start and end apart: 83 -> 83, of which waited for: 28 -> 31; matrix products, arithmetic and copies ran while one was open for 44% -> 45% of each run, Pallas kernels for 10% -> 11%
where the time goes in v5:
time: 619 us; the launch traced here: 608 us
  waiting for transfers between devices  145 us (23%)
  matrix products  128 us (21%)
  other arithmetic  114 us (18%)
  starting transfers between devices  85.6 us (14%)
  Pallas kernels  69.7 us (11%)
  local copies, waits for them, and re-layouts  63.2 us (10%)
    ppermute x26, waiting for transfers between devices, swap_y(): return lax.ppermute(a, 'y', [(0, 1), (1, 0)])  91.1 us
    dot_general x10, matrix products, rows_rows(): lax.dot_general(left, right, (((0,), (0,)), ((), ())), preferred_element_...  47.7 us
    ppermute x28, waiting for transfers between devices, swap_z(): return lax.ppermute(a, 'z', [(i, i ^ bit) for i in range(n)])  47.1 us
    dot_general x4, matrix products, cols_cols(): lax.dot_general(left, right, (((1,), (1,)), ((), ())), preferred_element_...  42.3 us
    ppermute x28, starting transfers between devices, swap_z(): return lax.ppermute(a, 'z', [(i, i ^ bit) for i in range(n)])  40.1 us
    convert_element_type x13, other arithmetic, halve(): return (keep, send.astype(pair[1].dtype))  33 us
    ppermute x26, starting transfers between devices, swap_y(): return lax.ppermute(a, 'y', [(0, 1), (1, 0)])  29.4 us
    unnamed x183, local copies, waits for them, and re-layouts  22.2 us
  transfers between devices with their start and end apart: 83, of which 31 were waited for; matrix products, arithmetic and copies ran while one was open for 45% of the time, Pallas kernels for 11%

profile of v5, /device:TPU:0, one launch (start us, length us, event | category | flops | bytes accessed | tf_op | source)
XLA Modules:
  0.0 608.5 jit_solution(3132661311264610913)
XLA Ops:
  17.7 8.1 %collective-permute-done = bf16[1,1,144,1152]{3,2,1,0:T(8,128)(2,1)} collective-permute-done((bf16[1,1,144,1152]{3,2,1,0:T(8,128)(2,1)S(1)}, bf16[1,1,144,1152]{3,2,1,0:T(8,128)(2,1)}, u32[]{:S(2)}, u32[]{:S(2)}) %collective-permute-start) | collective-permute-done | bytes 331808 | tf_op jit(solution)/shard_map/ppermute | solution.py:30
  39.7 11.5 %collective-permute-done.6 = bf16[2,128,2048]{2,1,0:T(8,128)(2,1)S(1)} collective-permute-done((bf16[2,128,2048]{2,1,0:T(8,128)(2,1)S(1)}, bf16[2,128,2048]{2,1,0:T(8,128)(2,1)S(1)}, u32[]{:S(2)}, u32[]{:S(2)}) %collective-permute-start.6) | collective-permute-done | bytes 1048608 | tf_op jit(solution)/shard_map/ppermute | solution.py:21
  66.7 20.6 %collective-permute-done.9 = bf16[2,128,1024]{2,1,0:T(8,128)(2,1)S(1)} collective-permute-done((bf16[2,128,1024]{2,1,0:T(8,128)(2,1)S(1)}, bf16[2,128,1024]{2,1,0:T(8,128)(2,1)S(1)}, u32[]{:S(2)}, u32[]{:S(2)}) %collective-permute-start.9) | collective-permute-done | bytes 524320 | tf_op jit(solution)/shard_map/ppermute | solution.py:21
  112.8 33.3 %conditional.16 = (f32[1024,1]{0,1:T(1,128)S(1)}, bf16[1024,2048]{1,0:T(8,128)(2,1)}, bf16[1024,512]{1,0:T(8,128)(2,1)}, bf16[1024,128]{1,0:T(8,128)(2,1)}, bf16...) conditional(s32[]{:T(128)} %convert_element_type.473, ...), branch_computations={%region_1.2_spmd, %region_2.4_spmd} | conditional | flops 4848616448 | bytes 75542672 | solution.py:56
  124.2 14.4 %branch_1_fun.2 = (bf16[1024,512]{1,0:T(8,128)(2,1)}, bf16[1024,128]{1,0:T(8,128)(2,1)}, bf16[1024,512]{1,0:T(8,128)(2,1)}) custom-call(f32[1024,640]{1,0:T(8,128)} %fusion.73.qkv_ref, f32[4,256,128]{2,1,0:T(8,128)} %get-tuple-element.167.cos_ref, f32[4,256,128]{2,1,0:T(8,128)} %get-tuple-element.168.sin_ref, f32[4,256,256]{2,1,0:T(8,128)S(1)} %get-tuple-element.169.allowed_ref), custom_call_target="tpu_custom_call" | custom-call | tf_op jit(solution)/shard_map/cond/branch_1_fun/pallas_call | solution.py:383
  149.0 10.9 %collective-permute-done.19.low_ref = bf16[2,128,1024]{2,1,0:T(8,128)(2,1)} collective-permute-done((bf16[2,128,1024]{2,1,0:T(8,128)(2,1)}, bf16[2,128,1024]{2,1,0:T(8,128)(2,1)}, u32[]{:S(2)}, u32[]{:S(2)}) %collective-permute-start.19) | collective-permute-done | bytes 524320 | tf_op jit(solution)/shard_map/ppermute | solution.py:21
  172.6 19.9 %collective-permute-done.25 = bf16[1,1,128,1408]{3,2,1,0:T(8,128)(2,1)S(1)} collective-permute-done((bf16[1,1,128,1408]{3,2,1,0:T(8,128)(2,1)S(1)}, bf16[1,1,128,1408]{3,2,1,0:T(8,128)(2,1)S(1)}, u32[]{:S(2)}, u32[]{:S(2)}) %collective-permute-start.25) | collective-permute-done | bytes 360480 | tf_op jit(solution)/shard_map/ppermute | solution.py:30
  204.9 20.4 %collective-permute-done.28 = bf16[2,128,2048]{2,1,0:T(8,128)(2,1)S(1)} collective-permute-done((bf16[2,128,2048]{2,1,0:T(8,128)(2,1)S(1)}, bf16[2,128,2048]{2,1,0:T(8,128)(2,1)S(1)}, u32[]{:S(2)}, u32[]{:S(2)}) %collective-permute-start.28) | collective-permute-done | bytes 1048608 | tf_op jit(solution)/shard_map/ppermute | solution.py:21
  239.3 9.3 %shard_map.261 = bf16[2,4,2,128,2816]{4,3,2,1,0:T(8,128)(2,1)} custom-call(s32[5]{0:T(128)} %xor_select_fusion.where_ref, bf16[4,1,128,2816]{3,2,1,0:T(8,128)(2,1)} %copy-done.15, bf16[4,1,128,2816]{3,2,1,0:T(8,128)(2,1)} %copy-done.38, bf16[4,1,128,2816]{3,2,1,0:T(8,128)(2,1)} %copy-done.22, bf16[4,1,128,2816]{3,2,1,0:T(8,128)(2,1)} %copy-done.39), custom_call_target="tpu_custom_call" | custom-call | bytes 23068672 | tf_op jit(solution)/shard_map/pallas_call | solution.py:191
  254.8 22.8 %conditional.17 = (f32[1024,2816]{1,0:T(8,128)}, bf16[1024,1408]{1,0:T(8,128)(2,1)S(1)}) conditional(s32[]{:T(128)} %convert_element_type.473, () %tuple.181, (bf16[1024,2048]{1,0:T(8,128)(2,1)S(1)}, bf16[2048,2816]{1,0:T(8,128)(2,1)}) %tuple.341), branch_computations={%region_5.6_spmd, %region_6.7_spmd} | conditional | flops 11819810816 | bytes 41680912 | solution.py:56
  254.8 17.4 %fusion.72 = f32[1024,2816]{1,0:T(8,128)} fusion(bf16[1024,2048]{1,0:T(8,128)(2,1)S(1)} %get-tuple-element.174, bf16[2048,2816]{1,0:T(8,128)(2,1)} %get-tuple-element.175), kind=kOutput, calls=%fused_computation.238 | convolution fusion | flops 11811160064 | bytes 27262976 | tf_op jit(solution)/shard_map/cond/branch_1_fun/dot_general | solution.py:598
  309.6 33.0 %conditional.19 = (bf16[1024,1408]{1,0:T(8,128)(2,1)}, bf16[1024,1408]{1,0:T(8,128)(2,1)}, bf16[2,512,2048]{2,1,0:T(8,128)(2,1)}, bf16[2,128,1024]{2,1,0:T(8,128)(2,1)}, bf16[2,128,1024]{2,1,0:T(8,128)(2,1)}) conditional(s32[]{:T(128)} %convert_element_type.473, () %tuple.180, (bf16[1024,2048]{1,0:T(8,128)(2,1)S(1)}, ...), branch_computations={%region_9.10_spmd, %region_10.11_spmd} | conditional | flops 17749114880 | bytes 50855976 | solution.py:56
  309.6 12.4 %multiply_convert_fusion = (bf16[1024,1408]{1,0:T(8,128)(2,1)}, bf16[1024,1408]{1,0:T(8,128)(2,1)}) fusion(f32[1024,2816]{1,0:T(8,128)} %get-tuple-element.180, bf16[1024,2048]{1,0:T(8,128)(2,1)S(1)} %get-tuple-element.178, bf16[2048,1408]{1,0:T(8,128)(2,1)S(1)} %get-tuple-element.179), kind=kOutput, calls=%fused_computation.16 | convolution fusion | flops 5924323328 | bytes 27262976 | tf_op jit(solution)/shard_map/cond/branch_1_fun/dot_general | solution.py:615
  322.0 18.4 %fusion.10 = bf16[1024,2048]{1,0:T(8,128)(2,1)} fusion(bf16[2048,2816]{1,0:T(8,128)(2,1)} %get-tuple-element.181, bf16[1024,1408]{1,0:T(8,128)(2,1)} %get-tuple-element.954, bf16[1024,1408]{1,0:T(8,128)(2,1)} %get-tuple-element.953), kind=kOutput, calls=%fused_computation.19 | convolution fusion | flops 11824791552 | bytes 21495808 | tf_op jit(solution)/shard_map/cond/branch_1_fun/dot_general | solution.py:331
  351.0 12.3 %conditional.20 = (bf16[4,2,128,1408]{3,2,1,0:T(8,128)(2,1)}, bf16[4,2,128,1408]{3,2,1,0:T(8,128)(2,1)S(1)}) conditional(s32[]{:T(128)} %convert_element_type.473, () %tuple.192, (bf16[1024,2048]{1,0:T(8,128)(2,1)S(1)}, bf16[1024,1408]{1,0:T(8,128)(2,1)}) %tuple.342), branch_computations={%region_11.12_spmd, %region_12.13_spmd} | conditional | flops 5908463616 | bytes 15728656 | solution.py:56
  379.3 12.4 %conditional.21 = (bf16[4,2,128,1408]{3,2,1,0:T(8,128)(2,1)}, bf16[4,2,128,1408]{3,2,1,0:T(8,128)(2,1)S(1)}) conditional(s32[]{:T(128)} %convert_element_type.473, () %tuple.198, (bf16[1024,2048]{1,0:T(8,128)(2,1)S(1)}, bf16[1024,1408]{1,0:T(8,128)(2,1)}) %tuple.343), branch_computations={%region_13.14_spmd, %region_14.15_spmd} | conditional | flops 5908463616 | bytes 15728656 | solution.py:56
  395.7 7.5 %conditional.22 = (f32[2,128,2048]{2,1,0:T(8,128)}, bf16[2,128,2048]{2,1,0:T(8,128)(2,1)}, f32[2048]{0:T(1024)S(1)}) conditional(s32[]{:T(128)} %convert_element_type.473, () %tuple.171, (bf16[2,128,2048]{2,1,0:T(8,128)(2,1)S(1)}, f32[2,128]{1,0:T(2,128)S(1)}, bf16[2,512,2048]{2,1,0:T(8,128)(2,1)}, bf16[2,128,2048]{2,1,0:T(8,128)(2,1)}, ...), branch_computations={%region_15.16_spmd, %region_16.19_spmd} | conditional | flops 11532800 | bytes 14711832 | solution.py:56
  414.1 13.3 %conditional.25 = (bf16[2,512,2048]{2,1,0:T(8,128)(2,1)}, bf16[2,128,1024]{2,1,0:T(8,128)(2,1)}, bf16[2,128,1024]{2,1,0:T(8,128)(2,1)}) conditional(s32[]{:T(128)} %convert_element_type.473, () %tuple.207, (bf16[1024,1408]{1,0:T(8,128)(2,1)}, bf16[2048,1408]{1,0:T(8,128)(2,1)}) %tuple.348), branch_computations={%region_23.24_spmd, %region_24.25_spmd} | conditional | flops 5907677184 | bytes 14942232 | solution.py:56
  414.1 11.0 %convolution_convert_fusion.6 = bf16[1024,2048]{1,0:T(8,128)(2,1)} fusion(bf16[1024,1408]{1,0:T(8,128)(2,1)} %get-tuple-element.199, bf16[2048,1408]{1,0:T(8,128)(2,1)} %get-tuple-element.200), kind=kOutput, calls=%fused_computation.40 | convolution fusion | flops 5907677184 | bytes 12845056 | tf_op jit(solution)/shard_map/cond/branch_1_fun/dot_general | solution.py:331
  436.7 9.3 %collective-permute-done.53 = bf16[2,128,1024]{2,1,0:T(8,128)(2,1)} collective-permute-done((bf16[2,128,1024]{2,1,0:T(8,128)(2,1)S(1)}, bf16[2,128,1024]{2,1,0:T(8,128)(2,1)}, u32[]{:S(2)}, u32[]{:S(2)}) %collective-permute-start.53) | collective-permute-done | bytes 524320 | tf_op jit(solution)/shard_map/ppermute | solution.py:21
  453.8 24.5 %conditional.26 = (bf16[1024,640]{1,0:T(8,128)(2,1)}, bf16[4,2,128,512]{3,2,1,0:T(8,128)(2,1)}, bf16[2,2,2,128,512]{4,3,2,1,0:T(8,128)(2,1)}) conditional(s32[]{:T(128)} %convert_element_type.473, () %tuple.170, (bf16[2,512,2048]{2,1,0:T(8,128)(2,1)S(1)}, bf16[2048,512]{1,0:T(8,128)(2,1)S(1)}, bf16[1024,512]{1,0:T(8,128)(2,1)}, ...), branch_computations={%region_25.26_spmd, %region_26.27_spmd} | conditional | flops 4296540160 | bytes 15728664 | solution.py:56
  461.7 16.5 %branch_1_fun.3 = bf16[1024,640]{1,0:T(8,128)(2,1)} custom-call(bf16[1024,512]{1,0:T(8,128)(2,1)} %get-tuple-element.201.q_ref, bf16[1024,128]{1,0:T(8,128)(2,1)} %get-tuple-element.202.kv_ref, bf16[1024,512]{1,0:T(8,128)(2,1)} %convolution_convert_fusion.7.d_ref, f32[4,256,128]{2,1,0:T(8,128)} %get-tuple-element.205.cos_ref, ...), custom_call_target="tpu_custom_call" | custom-call | tf_op jit(solution)/shard_map/cond/branch_1_fun/pallas_call | solution.py:428
  503.2 16.3 %conditional.27 = (bf16[2,512,2048]{2,1,0:T(8,128)(2,1)}, bf16[2,128,1024]{2,1,0:T(8,128)(2,1)}, bf16[2,128,1024]{2,1,0:T(8,128)(2,1)}, f32[4,2,2,128]{3,1,0,2:T...) conditional(s32[]{:T(128)} %convert_element_type.473, ...), branch_computations={%region_27.28_spmd, %region_28.30_spmd} | conditional | flops 5380507648 | bytes 23932984 | solution.py:56
  582.5 6.8 %conditional.31 = (f32[256,2048]{1,0:T(8,128)S(1)}) conditional(s32[]{:T(128)} %convert_element_type.473, () %tuple.226, (f32[1024,1]{0,1:T(1,128)S(1)}, bf16[2,512,2048]{2,1,0:T(8,128)(2,1)}, bf16[2,128,2048]{2,1,0:T(8,128)(2,1)S(1)}, bf16[2,128,2048]{2,1,0:T(8,128)(2,1)S(1)}, f32[2,4,2,1,128]{4,3,2,1,0:T(1,128)S(1)}, ...), branch_computations={%region_36.37_spmd, %region_37.39_spmd} | conditional | flops 11534336 | bytes 21012556 | solution.py:56
  (513 shorter events, 430.1 us)
Async XLA Ops:
  56.0 31.4 %collective-permute-start.7 = (bf16[2,1,144,1152]{3,2,1,0:T(8,128)(2,1)S(1)}, bf16[2,1,144,1152]{3,2,1,0:T(8,128)(2,1)S(1)}, u32[]{:S(2)}, u32[]{:S(2)}) collective-permute-start(bf16[2,1,144,1152]{3,2,1,0:T(8,128)(2,1)S(1)} %constant_dynamic-update-slice_fusion.2), channel_id=1, source_target_pairs={{0,8},{8,0},{16,24},{24,16},{1,9},{9,1},{17,25},{25,17},{2,10},{10... | collective-permute-start | bytes 1990664 | tf_op jit(solution)/shard_map/ppermute | solution.py:30
  56.1 34.3 %collective-permute-start.8 = (bf16[1,1,128,2816]{3,2,1,0:T(8,128)(2,1)}, bf16[1,1,128,2816]{3,2,1,0:T(8,128)(2,1)S(1)}, u32[]{:S(2)}, u32[]{:S(2)}) collective-permute-start(bf16[1,1,128,2816]{3,2,1,0:T(8,128)(2,1)} %bitcast.48), channel_id=1, source_target_pairs={{0,16},{8,24},{16,0},{24,8},{1,17},{9,25},{17,1},{25,9},{2,18},{10... | collective-permute-start | bytes 2162696 | tf_op jit(solution)/shard_map/ppermute | solution.py:30
  60.1 30.3 %collective-permute-start.11 = (bf16[128,2816]{1,0:T(8,128)(2,1)S(1)}, bf16[128,2816]{1,0:T(8,128)(2,1)S(1)}, u32[]{:S(2)}, u32[]{:S(2)}) collective-permute-start(bf16[128,2816]{1,0:T(8,128)(2,1)S(1)} %copy-done.56), channel_id=1, source_target_pairs={{0,4},{4,0},{1,5},{5,1},{2,6},{6,2},{3,7},{7,3},{8,12},{12,8},{9,1... | collective-permute-start | bytes 2162696 | tf_op jit(solution)/shard_map/ppermute | solution.py:21
  95.8 50.4 %collective-permute-start.14 = (bf16[2,1,128,2816]{3,2,1,0:T(8,128)(2,1)}, bf16[2,1,128,2816]{3,2,1,0:T(8,128)(2,1)}, u32[]{:S(2)}, u32[]{:S(2)}) collective-permute-start(bf16[2,1,128,2816]{3,2,1,0:T(8,128)(2,1)} %constant_dynamic-update-slice_fusion.6), channel_id=1, source_target_pairs={{0,8},{8,0},{16,24},{24,16},{1,9},{9,1},{17,25},{25,17},{2,10},{10... | collective-permute-start | bytes 4325384 | tf_op jit(solution)/shard_map/ppermute | solution.py:30
  95.8 50.4 %collective-permute-start.17 = (bf16[2,128,2048]{2,1,0:T(8,128)(2,1)S(1)}, bf16[2,128,2048]{2,1,0:T(8,128)(2,1)}, u32[]{:S(2)}, u32[]{:S(2)}) collective-permute-start(bf16[2,128,2048]{2,1,0:T(8,128)(2,1)S(1)} %bitcast.200), channel_id=1, source_target_pairs={{0,4},{4,0},{1,5},{5,1},{2,6},{6,2},{3,7},{7,3},{8,12},{12,8},{9,1... | collective-permute-start | bytes 3145736 | tf_op jit(solution)/shard_map/ppermute | solution.py:21
  96.4 49.8 %collective-permute-start.16 = (bf16[2,128,2048]{2,1,0:T(8,128)(2,1)S(1)}, bf16[2,128,2048]{2,1,0:T(8,128)(2,1)}, u32[]{:S(2)}, u32[]{:S(2)}) collective-permute-start(bf16[2,128,2048]{2,1,0:T(8,128)(2,1)S(1)} %bitcast.201), channel_id=1, source_target_pairs={{0,1},{1,0},{2,3},{3,2},{4,5},{5,4},{6,7},{7,6},{8,9},{9,8},{10,11... | collective-permute-start | bytes 3145736 | tf_op jit(solution)/shard_map/ppermute | solution.py:17
  98.1 48.0 %collective-permute-start.15 = (bf16[1,1,128,2816]{3,2,1,0:T(8,128)(2,1)}, bf16[1,1,128,2816]{3,2,1,0:T(8,128)(2,1)}, u32[]{:S(2)}, u32[]{:S(2)}) collective-permute-start(bf16[1,1,128,2816]{3,2,1,0:T(8,128)(2,1)} %bitcast.229), channel_id=1, source_target_pairs={{0,16},{8,24},{16,0},{24,8},{1,17},{9,25},{17,1},{25,9},{2,18},{10... | collective-permute-start | bytes 2162696 | tf_op jit(solution)/shard_map/ppermute | solution.py:30
  104.6 41.5 %collective-permute-start.18 = (bf16[128,1408]{1,0:T(8,128)(2,1)}, bf16[128,1408]{1,0:T(8,128)(2,1)}, u32[]{:S(2)}, u32[]{:S(2)}) collective-permute-start(bf16[128,1408]{1,0:T(8,128)(2,1)} %get-tuple-element.560), channel_id=1, source_target_pairs={{0,4},{4,0},{1,5},{5,1},{2,6},{6,2},{3,7},{7,3},{8,12},{12,8},{9,1... | collective-permute-start | bytes 1081352 | tf_op jit(solution)/shard_map/ppermute | solution.py:21
  167.2 27.2 %collective-permute-start.26 = (bf16[4,1,128,2816]{3,2,1,0:T(8,128)(2,1)S(1)}, bf16[4,1,128,2816]{3,2,1,0:T(8,128)(2,1)S(1)}, u32[]{:S(2)}, u32[]{:S(2)}) collective-permute-start(bf16[4,1,128,2816]{3,2,1,0:T(8,128)(2,1)S(1)} %constant_dynamic-update-slice_fusion.8.own), channel_id=1, source_target_pairs={{0,2},{2,0},{1,3},{3,1},{4,6},{6,4},{5,7},{7,5},{8,10},{10,8},{9,1... | collective-permute-start | bytes 8650760 | tf_op jit(solution)/shard_map/ppermute | solution.py:25
  167.3 26.5 %collective-permute-start.24 = (bf16[1,1,128,2816]{3,2,1,0:T(8,128)(2,1)}, bf16[1,1,128,2816]{3,2,1,0:T(8,128)(2,1)S(1)}, u32[]{:S(2)}, u32[]{:S(2)}) collective-permute-start(bf16[1,1,128,2816]{3,2,1,0:T(8,128)(2,1)} %collective-permute-done.15), channel_id=1, source_target_pairs={{0,8},{8,0},{16,24},{24,16},{1,9},{9,1},{17,25},{25,17},{2,10},{10... | collective-permute-start | bytes 2162696 | tf_op jit(solution)/shard_map/ppermute | solution.py:30
  195.9 31.9 %collective-permute-start.29 = (bf16[4,1,128,2816]{3,2,1,0:T(8,128)(2,1)S(1)}, bf16[4,1,128,2816]{3,2,1,0:T(8,128)(2,1)S(1)}, u32[]{:S(2)}, u32[]{:S(2)}) collective-permute-start(bf16[4,1,128,2816]{3,2,1,0:T(8,128)(2,1)S(1)} %constant_dynamic-update-slice_fusion.10.peer), channel_id=1, source_target_pairs={{0,2},{2,0},{1,3},{3,1},{4,6},{6,4},{5,7},{7,5},{8,10},{10,8},{9,1... | collective-permute-start | bytes 8650760 | tf_op jit(solution)/shard_map/ppermute | solution.py:25
  307.6 35.0 %collective-permute-start.40 = (bf16[2,2,128,1408]{3,2,1,0:T(8,128)(2,1)}, bf16[2,2,128,1408]{3,2,1,0:T(8,128)(2,1)}, u32[]{:S(2)}, u32[]{:S(2)}) collective-permute-start(bf16[2,2,128,1408]{3,2,1,0:T(8,128)(2,1)} %fusion.43), channel_id=1, source_target_pairs={{0,8},{8,0},{16,24},{24,16},{1,9},{9,1},{17,25},{25,17},{2,10},{10... | collective-permute-start | bytes 4325384 | tf_op jit(solution)/shard_map/ppermute | solution.py:30
  369.2 26.3 %collective-permute-start.44 = (bf16[2,128,2048]{2,1,0:T(8,128)(2,1)}, bf16[2,128,2048]{2,1,0:T(8,128)(2,1)}, u32[]{:S(2)}, u32[]{:S(2)}) collective-permute-start(bf16[2,128,2048]{2,1,0:T(8,128)(2,1)} %get-tuple-element.638), channel_id=1, source_target_pairs={{0,1},{1,0},{2,3},{3,2},{4,5},{5,4},{6,7},{7,6},{8,9},{9,8},{10,11... | collective-permute-start | bytes 3145736 | tf_op jit(solution)/shard_map/ppermute | solution.py:17
  404.9 26.3 %collective-permute-start.51 = (bf16[2,2,128,640]{3,2,1,0:T(8,128)(2,1)S(1)}, bf16[2,2,128,640]{3,2,1,0:T(8,128)(2,1)}, u32[]{:S(2)}, u32[]{:S(2)}) collective-permute-start(bf16[2,2,128,640]{3,2,1,0:T(8,128)(2,1)S(1)} %get-tuple-element.660), channel_id=1, source_target_pairs={{0,8},{8,0},{16,24},{24,16},{1,9},{9,1},{17,25},{25,17},{2,10},{10... | collective-permute-start | bytes 1966088 | tf_op jit(solution)/shard_map/ppermute | solution.py:30
  431.3 48.9 %collective-permute-start.58 = (bf16[2,2,128,1408]{3,2,1,0:T(8,128)(2,1)}, bf16[2,2,128,1408]{3,2,1,0:T(8,128)(2,1)}, u32[]{:S(2)}, u32[]{:S(2)}) collective-permute-start(bf16[2,2,128,1408]{3,2,1,0:T(8,128)(2,1)} %get-tuple-element.694), channel_id=1, source_target_pairs={{0,8},{8,0},{16,24},{24,16},{1,9},{9,1},{17,25},{25,17},{2,10},{10... | collective-permute-start | bytes 4325384 | tf_op jit(solution)/shard_map/ppermute | solution.py:30
  446.3 32.7 %collective-permute-start.55 = (bf16[2,128,1024]{2,1,0:T(8,128)(2,1)}, bf16[2,128,1024]{2,1,0:T(8,128)(2,1)}, u32[]{:S(2)}, u32[]{:S(2)}) collective-permute-start(bf16[2,128,1024]{2,1,0:T(8,128)(2,1)} %get-tuple-element.689), channel_id=1, source_target_pairs={{0,4},{4,0},{1,5},{5,1},{2,6},{6,2},{3,7},{7,3},{8,12},{12,8},{9,1... | collective-permute-start | bytes 1572872 | tf_op jit(solution)/shard_map/ppermute | solution.py:21
  447.7 31.4 %collective-permute-start.56 = (bf16[2,128,1024]{2,1,0:T(8,128)(2,1)}, bf16[2,128,1024]{2,1,0:T(8,128)(2,1)}, u32[]{:S(2)}, u32[]{:S(2)}) collective-permute-start(bf16[2,128,1024]{2,1,0:T(8,128)(2,1)} %get-tuple-element.690), channel_id=1, source_target_pairs={{0,1},{1,0},{2,3},{3,2},{4,5},{5,4},{6,7},{7,6},{8,9},{9,8},{10,11... | collective-permute-start | bytes 1572872 | tf_op jit(solution)/shard_map/ppermute | solution.py:17
  448.4 29.8 %collective-permute-start.57 = (bf16[1,2,128,640]{3,2,1,0:T(8,128)(2,1)}, bf16[1,2,128,640]{3,2,1,0:T(8,128)(2,1)}, u32[]{:S(2)}, u32[]{:S(2)}) collective-permute-start(bf16[1,2,128,640]{3,2,1,0:T(8,128)(2,1)} %get-tuple-element.692), channel_id=1, source_target_pairs={{0,16},{8,24},{16,0},{24,8},{1,17},{9,25},{17,1},{25,9},{2,18},{10... | collective-permute-start | bytes 983048 | tf_op jit(solution)/shard_map/ppermute | solution.py:30
  449.8 29.2 %collective-permute-start.59 = (bf16[1,2,128,768]{3,2,1,0:T(8,128)(2,1)}, bf16[1,2,128,768]{3,2,1,0:T(8,128)(2,1)}, u32[]{:S(2)}, u32[]{:S(2)}) collective-permute-start(bf16[1,2,128,768]{3,2,1,0:T(8,128)(2,1)} %get-tuple-element.696), channel_id=1, source_target_pairs={{0,16},{8,24},{16,0},{24,8},{1,17},{9,25},{17,1},{25,9},{2,18},{10... | collective-permute-start | bytes 1179656 | tf_op jit(solution)/shard_map/ppermute | solution.py:30
  489.9 36.2 %collective-permute-start.64 = (bf16[1,2,128,1408]{3,2,1,0:T(8,128)(2,1)}, bf16[1,2,128,1408]{3,2,1,0:T(8,128)(2,1)S(1)}, u32[]{:S(2)}, u32[]{:S(2)}) collective-permute-start(bf16[1,2,128,1408]{3,2,1,0:T(8,128)(2,1)} %get-tuple-element.724), channel_id=1, source_target_pairs={{0,16},{8,24},{16,0},{24,8},{1,17},{9,25},{17,1},{25,9},{2,18},{10... | collective-permute-start | bytes 2162696 | tf_op jit(solution)/shard_map/ppermute | solution.py:30
  492.2 33.8 %collective-permute-start.61 = (bf16[2,128,2048]{2,1,0:T(8,128)(2,1)}, bf16[2,128,2048]{2,1,0:T(8,128)(2,1)}, u32[]{:S(2)}, u32[]{:S(2)}) collective-permute-start(bf16[2,128,2048]{2,1,0:T(8,128)(2,1)} %get-tuple-element.719), channel_id=1, source_target_pairs={{0,1},{1,0},{2,3},{3,2},{4,5},{5,4},{6,7},{7,6},{8,9},{9,8},{10,11... | collective-permute-start | bytes 3145736 | tf_op jit(solution)/shard_map/ppermute | solution.py:17
  493.0 33.1 %collective-permute-start.62 = (bf16[2,128,2048]{2,1,0:T(8,128)(2,1)}, bf16[2,128,2048]{2,1,0:T(8,128)(2,1)}, u32[]{:S(2)}, u32[]{:S(2)}) collective-permute-start(bf16[2,128,2048]{2,1,0:T(8,128)(2,1)} %get-tuple-element.720), channel_id=1, source_target_pairs={{0,4},{4,0},{1,5},{5,1},{2,6},{6,2},{3,7},{7,3},{8,12},{12,8},{9,1... | collective-permute-start | bytes 3145736 | tf_op jit(solution)/shard_map/ppermute | solution.py:21
  496.5 29.5 %collective-permute-start.65 = (bf16[128,1408]{1,0:T(8,128)(2,1)}, bf16[128,1408]{1,0:T(8,128)(2,1)}, u32[]{:S(2)}, u32[]{:S(2)}) collective-permute-start(bf16[128,1408]{1,0:T(8,128)(2,1)} %get-tuple-element.870), channel_id=1, source_target_pairs={{0,4},{4,0},{1,5},{5,1},{2,6},{6,2},{3,7},{7,3},{8,12},{12,8},{9,1... | collective-permute-start | bytes 1081352 | tf_op jit(solution)/shard_map/ppermute | solution.py:21
  500.4 27.7 %collective-permute-start.63 = (bf16[2,2,128,512]{3,2,1,0:T(8,128)(2,1)}, bf16[2,2,128,512]{3,2,1,0:T(8,128)(2,1)}, u32[]{:S(2)}, u32[]{:S(2)}) collective-permute-start(bf16[2,2,128,512]{3,2,1,0:T(8,128)(2,1)} %get-tuple-element.722), channel_id=1, source_target_pairs={{0,8},{8,0},{16,24},{24,16},{1,9},{9,1},{17,25},{25,17},{2,10},{10... | collective-permute-start | bytes 1572872 | tf_op jit(solution)/shard_map/ppermute | solution.py:30
  (150 other events, 2289.2 us)

commit v6 on v5

--- a/solution.py
+++ b/solution.py
@@ -19,6 +19,10 @@
 
 def swap_y(a):
     return lax.ppermute(a, "y", [(0, 1), (1, 0)])
+
+
+def swap_diagonal(a):
+    return lax.ppermute(a, ("y", "x"), [(i, 3 - i) for i in range(4)])
 
 
 def swap_c(a):
@@ -778,10 +782,10 @@
     input_grad, qkv_sum, gain_sum, up_parts, gate_parts, out_parts = meet(
         input_grad, qkv_sum, gain_sum, up_parts, gate_parts, out_parts
     )
-    gain_parts = reduce_y(gain_sum, y)
+    gain_keep, gain_send = (add(*(pick(p[0], 0, at) for p in gain_sum)) for at in (y, 1 - y))
+    gain_parts = swap_x(gain_keep), swap_y(gain_send), swap_diagonal(gain_send)
     qkv_parts = reduce_y(qkv_sum, y)
-    keep = add(*gain_parts)
-    keep = keep + swap_x(keep)
+    keep = gain_keep + gain_parts[0] + (gain_parts[1] + gain_parts[2])
 
     def cut(parts, lo, hi):
         return join((parts[0][:, lo:hi], parts[1][:, lo:hi]), y)

time: 619 us -> 618 us (level)
  transfers between devices with their start and end apart: 83 -> 84, of which waited for: 31 -> 30; matrix products, arithmetic and copies ran while one was open for 45% -> 45% of each run, Pallas kernels for 11% -> 11%
where the time goes in v6:
time: 618 us; the launch traced here: 607 us
  waiting for transfers between devices  144 us (23%)
  matrix products  128 us (21%)
  other arithmetic  114 us (18%)
  starting transfers between devices  86.7 us (14%)
  Pallas kernels  69.7 us (11%)
  local copies, waits for them, and re-layouts  63.3 us (10%)
    ppermute x26, waiting for transfers between devices, swap_y(): return lax.ppermute(a, 'y', [(0, 1), (1, 0)])  91.1 us
    dot_general x10, matrix products, rows_rows(): lax.dot_general(left, right, (((0,), (0,)), ((), ())), preferred_element_...  47.7 us
    ppermute x28, waiting for transfers between devices, swap_z(): return lax.ppermute(a, 'z', [(i, i ^ bit) for i in range(n)])  47.1 us
    dot_general x4, matrix products, cols_cols(): lax.dot_general(left, right, (((1,), (1,)), ((), ())), preferred_element_...  42.2 us
    ppermute x28, starting transfers between devices, swap_z(): return lax.ppermute(a, 'z', [(i, i ^ bit) for i in range(n)])  40 us
    convert_element_type x13, other arithmetic, halve(): return (keep, send.astype(pair[1].dtype))  33.1 us
    ppermute x26, starting transfers between devices, swap_y(): return lax.ppermute(a, 'y', [(0, 1), (1, 0)])  28.8 us
    unnamed x183, local copies, waits for them, and re-layouts  22.2 us
  transfers between devices with their start and end apart: 84, of which 30 were waited for; matrix products, arithmetic and copies ran while one was open for 45% of the time, Pallas kernels for 11%

profile of v6, /device:TPU:0, one launch (start us, length us, event | category | flops | bytes accessed | tf_op | source)
XLA Modules:
  0.0 607.3 jit_solution(10686443570223720527)
XLA Ops:
  17.7 8.1 %collective-permute-done = bf16[1,1,144,1152]{3,2,1,0:T(8,128)(2,1)} collective-permute-done((bf16[1,1,144,1152]{3,2,1,0:T(8,128)(2,1)S(1)}, bf16[1,1,144,1152]{3,2,1,0:T(8,128)(2,1)}, u32[]{:S(2)}, u32[]{:S(2)}) %collective-permute-start) | collective-permute-done | bytes 331808 | tf_op jit(solution)/shard_map/ppermute | solution.py:34
  39.7 11.5 %collective-permute-done.6 = bf16[2,128,2048]{2,1,0:T(8,128)(2,1)S(1)} collective-permute-done((bf16[2,128,2048]{2,1,0:T(8,128)(2,1)S(1)}, bf16[2,128,2048]{2,1,0:T(8,128)(2,1)S(1)}, u32[]{:S(2)}, u32[]{:S(2)}) %collective-permute-start.6) | collective-permute-done | bytes 1048608 | tf_op jit(solution)/shard_map/ppermute | solution.py:21
  66.7 20.6 %collective-permute-done.9 = bf16[2,128,1024]{2,1,0:T(8,128)(2,1)S(1)} collective-permute-done((bf16[2,128,1024]{2,1,0:T(8,128)(2,1)S(1)}, bf16[2,128,1024]{2,1,0:T(8,128)(2,1)S(1)}, u32[]{:S(2)}, u32[]{:S(2)}) %collective-permute-start.9) | collective-permute-done | bytes 524320 | tf_op jit(solution)/shard_map/ppermute | solution.py:21
  112.8 33.3 %conditional.16 = (f32[1024,1]{0,1:T(1,128)S(1)}, bf16[1024,2048]{1,0:T(8,128)(2,1)}, bf16[1024,512]{1,0:T(8,128)(2,1)}, bf16[1024,128]{1,0:T(8,128)(2,1)}, bf16...) conditional(s32[]{:T(128)} %convert_element_type.473, ...), branch_computations={%region_1.2_spmd, %region_2.4_spmd} | conditional | flops 4848616448 | bytes 75542672 | solution.py:60
  124.1 14.4 %branch_1_fun.2 = (bf16[1024,512]{1,0:T(8,128)(2,1)}, bf16[1024,128]{1,0:T(8,128)(2,1)}, bf16[1024,512]{1,0:T(8,128)(2,1)}) custom-call(f32[1024,640]{1,0:T(8,128)} %fusion.72.qkv_ref, f32[4,256,128]{2,1,0:T(8,128)} %get-tuple-element.167.cos_ref, f32[4,256,128]{2,1,0:T(8,128)} %get-tuple-element.168.sin_ref, f32[4,256,256]{2,1,0:T(8,128)S(1)} %get-tuple-element.169.allowed_ref), custom_call_target="tpu_custom_call" | custom-call | tf_op jit(solution)/shard_map/cond/branch_1_fun/pallas_call | solution.py:387
  148.9 10.9 %collective-permute-done.19.low_ref = bf16[2,128,1024]{2,1,0:T(8,128)(2,1)} collective-permute-done((bf16[2,128,1024]{2,1,0:T(8,128)(2,1)}, bf16[2,128,1024]{2,1,0:T(8,128)(2,1)}, u32[]{:S(2)}, u32[]{:S(2)}) %collective-permute-start.19) | collective-permute-done | bytes 524320 | tf_op jit(solution)/shard_map/ppermute | solution.py:21
  172.5 19.9 %collective-permute-done.25 = bf16[1,1,128,1408]{3,2,1,0:T(8,128)(2,1)S(1)} collective-permute-done((bf16[1,1,128,1408]{3,2,1,0:T(8,128)(2,1)S(1)}, bf16[1,1,128,1408]{3,2,1,0:T(8,128)(2,1)S(1)}, u32[]{:S(2)}, u32[]{:S(2)}) %collective-permute-start.25) | collective-permute-done | bytes 360480 | tf_op jit(solution)/shard_map/ppermute | solution.py:34
  204.8 20.4 %collective-permute-done.28 = bf16[2,128,2048]{2,1,0:T(8,128)(2,1)S(1)} collective-permute-done((bf16[2,128,2048]{2,1,0:T(8,128)(2,1)S(1)}, bf16[2,128,2048]{2,1,0:T(8,128)(2,1)S(1)}, u32[]{:S(2)}, u32[]{:S(2)}) %collective-permute-start.28) | collective-permute-done | bytes 1048608 | tf_op jit(solution)/shard_map/ppermute | solution.py:21
  239.2 9.3 %shard_map.261 = bf16[2,4,2,128,2816]{4,3,2,1,0:T(8,128)(2,1)} custom-call(s32[5]{0:T(128)} %xor_select_fusion.where_ref, bf16[4,1,128,2816]{3,2,1,0:T(8,128)(2,1)} %copy-done.15, bf16[4,1,128,2816]{3,2,1,0:T(8,128)(2,1)} %copy-done.38, bf16[4,1,128,2816]{3,2,1,0:T(8,128)(2,1)} %copy-done.22, bf16[4,1,128,2816]{3,2,1,0:T(8,128)(2,1)} %copy-done.39), custom_call_target="tpu_custom_call" | custom-call | bytes 23068672 | tf_op jit(solution)/shard_map/pallas_call | solution.py:195
  254.8 22.8 %conditional.17 = (f32[1024,2816]{1,0:T(8,128)}, bf16[1024,1408]{1,0:T(8,128)(2,1)S(1)}) conditional(s32[]{:T(128)} %convert_element_type.473, () %tuple.181, (bf16[1024,2048]{1,0:T(8,128)(2,1)S(1)}, bf16[2048,2816]{1,0:T(8,128)(2,1)}) %tuple.342), branch_computations={%region_5.6_spmd, %region_6.7_spmd} | conditional | flops 11819810816 | bytes 41680912 | solution.py:60
  254.8 17.4 %fusion.71 = f32[1024,2816]{1,0:T(8,128)} fusion(bf16[1024,2048]{1,0:T(8,128)(2,1)S(1)} %get-tuple-element.174, bf16[2048,2816]{1,0:T(8,128)(2,1)} %get-tuple-element.175), kind=kOutput, calls=%fused_computation.238 | convolution fusion | flops 11811160064 | bytes 27262976 | tf_op jit(solution)/shard_map/cond/branch_1_fun/dot_general | solution.py:602
  309.6 33.0 %conditional.19 = (bf16[1024,1408]{1,0:T(8,128)(2,1)}, bf16[1024,1408]{1,0:T(8,128)(2,1)}, bf16[2,512,2048]{2,1,0:T(8,128)(2,1)}, bf16[2,128,1024]{2,1,0:T(8,128)(2,1)}, bf16[2,128,1024]{2,1,0:T(8,128)(2,1)}) conditional(s32[]{:T(128)} %convert_element_type.473, () %tuple.180, (bf16[1024,2048]{1,0:T(8,128)(2,1)S(1)}, ...), branch_computations={%region_9.10_spmd, %region_10.11_spmd} | conditional | flops 17749114880 | bytes 50855976 | solution.py:60
  309.6 12.4 %multiply_convert_fusion = (bf16[1024,1408]{1,0:T(8,128)(2,1)}, bf16[1024,1408]{1,0:T(8,128)(2,1)}) fusion(f32[1024,2816]{1,0:T(8,128)} %get-tuple-element.180, bf16[1024,2048]{1,0:T(8,128)(2,1)S(1)} %get-tuple-element.178, bf16[2048,1408]{1,0:T(8,128)(2,1)S(1)} %get-tuple-element.179), kind=kOutput, calls=%fused_computation.16 | convolution fusion | flops 5924323328 | bytes 27262976 | tf_op jit(solution)/shard_map/cond/branch_1_fun/dot_general | solution.py:619
  322.0 18.4 %fusion.10 = bf16[1024,2048]{1,0:T(8,128)(2,1)} fusion(bf16[2048,2816]{1,0:T(8,128)(2,1)} %get-tuple-element.181, bf16[1024,1408]{1,0:T(8,128)(2,1)} %get-tuple-element.956, bf16[1024,1408]{1,0:T(8,128)(2,1)} %get-tuple-element.955), kind=kOutput, calls=%fused_computation.19 | convolution fusion | flops 11824791552 | bytes 21495808 | tf_op jit(solution)/shard_map/cond/branch_1_fun/dot_general | solution.py:335
  350.9 12.3 %conditional.20 = (bf16[4,2,128,1408]{3,2,1,0:T(8,128)(2,1)}, bf16[4,2,128,1408]{3,2,1,0:T(8,128)(2,1)S(1)}) conditional(s32[]{:T(128)} %convert_element_type.473, () %tuple.192, (bf16[1024,2048]{1,0:T(8,128)(2,1)S(1)}, bf16[1024,1408]{1,0:T(8,128)(2,1)}) %tuple.343), branch_computations={%region_11.12_spmd, %region_12.13_spmd} | conditional | flops 5908463616 | bytes 15728656 | solution.py:60
  379.2 12.4 %conditional.21 = (bf16[4,2,128,1408]{3,2,1,0:T(8,128)(2,1)}, bf16[4,2,128,1408]{3,2,1,0:T(8,128)(2,1)S(1)}) conditional(s32[]{:T(128)} %convert_element_type.473, () %tuple.198, (bf16[1024,2048]{1,0:T(8,128)(2,1)S(1)}, bf16[1024,1408]{1,0:T(8,128)(2,1)}) %tuple.344), branch_computations={%region_13.14_spmd, %region_14.15_spmd} | conditional | flops 5908463616 | bytes 15728656 | solution.py:60
  395.6 7.6 %conditional.22 = (f32[2,128,2048]{2,1,0:T(8,128)}, bf16[2,128,2048]{2,1,0:T(8,128)(2,1)}, f32[2048]{0:T(1024)S(1)}) conditional(s32[]{:T(128)} %convert_element_type.473, () %tuple.171, (bf16[2,128,2048]{2,1,0:T(8,128)(2,1)S(1)}, f32[2,128]{1,0:T(2,128)S(1)}, bf16[2,512,2048]{2,1,0:T(8,128)(2,1)}, bf16[2,128,2048]{2,1,0:T(8,128)(2,1)}, ...), branch_computations={%region_15.16_spmd, %region_16.19_spmd} | conditional | flops 11532800 | bytes 14711832 | solution.py:60
  414.0 13.3 %conditional.25 = (bf16[2,512,2048]{2,1,0:T(8,128)(2,1)}, bf16[2,128,1024]{2,1,0:T(8,128)(2,1)}, bf16[2,128,1024]{2,1,0:T(8,128)(2,1)}) conditional(s32[]{:T(128)} %convert_element_type.473, () %tuple.207, (bf16[1024,1408]{1,0:T(8,128)(2,1)}, bf16[2048,1408]{1,0:T(8,128)(2,1)}) %tuple.349), branch_computations={%region_23.24_spmd, %region_24.25_spmd} | conditional | flops 5907677184 | bytes 14942232 | solution.py:60
  414.0 11.0 %convolution_convert_fusion.6 = bf16[1024,2048]{1,0:T(8,128)(2,1)} fusion(bf16[1024,1408]{1,0:T(8,128)(2,1)} %get-tuple-element.199, bf16[2048,1408]{1,0:T(8,128)(2,1)} %get-tuple-element.200), kind=kOutput, calls=%fused_computation.40 | convolution fusion | flops 5907677184 | bytes 12845056 | tf_op jit(solution)/shard_map/cond/branch_1_fun/dot_general | solution.py:335
  436.7 9.2 %collective-permute-done.53 = bf16[2,128,1024]{2,1,0:T(8,128)(2,1)} collective-permute-done((bf16[2,128,1024]{2,1,0:T(8,128)(2,1)S(1)}, bf16[2,128,1024]{2,1,0:T(8,128)(2,1)}, u32[]{:S(2)}, u32[]{:S(2)}) %collective-permute-start.53) | collective-permute-done | bytes 524320 | tf_op jit(solution)/shard_map/ppermute | solution.py:21
  453.7 24.5 %conditional.26 = (bf16[1024,640]{1,0:T(8,128)(2,1)}, bf16[4,2,128,512]{3,2,1,0:T(8,128)(2,1)}, bf16[2,2,2,128,512]{4,3,2,1,0:T(8,128)(2,1)}) conditional(s32[]{:T(128)} %convert_element_type.473, () %tuple.170, (bf16[2,512,2048]{2,1,0:T(8,128)(2,1)S(1)}, bf16[2048,512]{1,0:T(8,128)(2,1)S(1)}, bf16[1024,512]{1,0:T(8,128)(2,1)}, ...), branch_computations={%region_25.26_spmd, %region_26.27_spmd} | conditional | flops 4296540160 | bytes 15728664 | solution.py:60
  461.7 16.5 %branch_1_fun.3 = bf16[1024,640]{1,0:T(8,128)(2,1)} custom-call(bf16[1024,512]{1,0:T(8,128)(2,1)} %get-tuple-element.201.q_ref, bf16[1024,128]{1,0:T(8,128)(2,1)} %get-tuple-element.202.kv_ref, bf16[1024,512]{1,0:T(8,128)(2,1)} %convolution_convert_fusion.7.d_ref, f32[4,256,128]{2,1,0:T(8,128)} %get-tuple-element.205.cos_ref, ...), custom_call_target="tpu_custom_call" | custom-call | tf_op jit(solution)/shard_map/cond/branch_1_fun/pallas_call | solution.py:432
  503.2 16.3 %conditional.27 = (bf16[2,512,2048]{2,1,0:T(8,128)(2,1)}, bf16[2,128,1024]{2,1,0:T(8,128)(2,1)}, bf16[2,128,1024]{2,1,0:T(8,128)(2,1)}, f32[4,2,2,128]{3,1,0,2:T...) conditional(s32[]{:T(128)} %convert_element_type.473, ...), branch_computations={%region_27.28_spmd, %region_28.30_spmd} | conditional | flops 5380507648 | bytes 23932984 | solution.py:60
  582.5 6.8 %conditional.31 = (f32[256,2048]{1,0:T(8,128)S(1)}) conditional(s32[]{:T(128)} %convert_element_type.473, () %tuple.226, (f32[1024,1]{0,1:T(1,128)S(1)}, bf16[2,512,2048]{2,1,0:T(8,128)(2,1)}, bf16[2,128,2048]{2,1,0:T(8,128)(2,1)S(1)}, bf16[2,128,2048]{2,1,0:T(8,128)(2,1)S(1)}, f32[2,4,2,1,128]{4,3,2,1,0:T(1,128)S(1)}, ...), branch_computations={%region_36.37_spmd, %region_37.39_spmd} | conditional | flops 11534336 | bytes 21012556 | solution.py:60
  (514 shorter events, 429.0 us)
Async XLA Ops:
  56.0 31.4 %collective-permute-start.7 = (bf16[2,1,144,1152]{3,2,1,0:T(8,128)(2,1)S(1)}, bf16[2,1,144,1152]{3,2,1,0:T(8,128)(2,1)S(1)}, u32[]{:S(2)}, u32[]{:S(2)}) collective-permute-start(bf16[2,1,144,1152]{3,2,1,0:T(8,128)(2,1)S(1)} %constant_dynamic-update-slice_fusion.2), channel_id=1, source_target_pairs={{0,8},{8,0},{16,24},{24,16},{1,9},{9,1},{17,25},{25,17},{2,10},{10... | collective-permute-start | bytes 1990664 | tf_op jit(solution)/shard_map/ppermute | solution.py:34
  56.1 34.3 %collective-permute-start.8 = (bf16[1,1,128,2816]{3,2,1,0:T(8,128)(2,1)}, bf16[1,1,128,2816]{3,2,1,0:T(8,128)(2,1)S(1)}, u32[]{:S(2)}, u32[]{:S(2)}) collective-permute-start(bf16[1,1,128,2816]{3,2,1,0:T(8,128)(2,1)} %bitcast.48), channel_id=1, source_target_pairs={{0,16},{8,24},{16,0},{24,8},{1,17},{9,25},{17,1},{25,9},{2,18},{10... | collective-permute-start | bytes 2162696 | tf_op jit(solution)/shard_map/ppermute | solution.py:34
  60.1 30.3 %collective-permute-start.11 = (bf16[128,2816]{1,0:T(8,128)(2,1)S(1)}, bf16[128,2816]{1,0:T(8,128)(2,1)S(1)}, u32[]{:S(2)}, u32[]{:S(2)}) collective-permute-start(bf16[128,2816]{1,0:T(8,128)(2,1)S(1)} %copy-done.56), channel_id=1, source_target_pairs={{0,4},{4,0},{1,5},{5,1},{2,6},{6,2},{3,7},{7,3},{8,12},{12,8},{9,1... | collective-permute-start | bytes 2162696 | tf_op jit(solution)/shard_map/ppermute | solution.py:21
  95.8 50.3 %collective-permute-start.14 = (bf16[2,1,128,2816]{3,2,1,0:T(8,128)(2,1)}, bf16[2,1,128,2816]{3,2,1,0:T(8,128)(2,1)}, u32[]{:S(2)}, u32[]{:S(2)}) collective-permute-start(bf16[2,1,128,2816]{3,2,1,0:T(8,128)(2,1)} %constant_dynamic-update-slice_fusion.6), channel_id=1, source_target_pairs={{0,8},{8,0},{16,24},{24,16},{1,9},{9,1},{17,25},{25,17},{2,10},{10... | collective-permute-start | bytes 4325384 | tf_op jit(solution)/shard_map/ppermute | solution.py:34
  95.8 50.3 %collective-permute-start.17 = (bf16[2,128,2048]{2,1,0:T(8,128)(2,1)S(1)}, bf16[2,128,2048]{2,1,0:T(8,128)(2,1)}, u32[]{:S(2)}, u32[]{:S(2)}) collective-permute-start(bf16[2,128,2048]{2,1,0:T(8,128)(2,1)S(1)} %bitcast.198), channel_id=1, source_target_pairs={{0,4},{4,0},{1,5},{5,1},{2,6},{6,2},{3,7},{7,3},{8,12},{12,8},{9,1... | collective-permute-start | bytes 3145736 | tf_op jit(solution)/shard_map/ppermute | solution.py:21
  96.4 49.7 %collective-permute-start.16 = (bf16[2,128,2048]{2,1,0:T(8,128)(2,1)S(1)}, bf16[2,128,2048]{2,1,0:T(8,128)(2,1)}, u32[]{:S(2)}, u32[]{:S(2)}) collective-permute-start(bf16[2,128,2048]{2,1,0:T(8,128)(2,1)S(1)} %bitcast.199), channel_id=1, source_target_pairs={{0,1},{1,0},{2,3},{3,2},{4,5},{5,4},{6,7},{7,6},{8,9},{9,8},{10,11... | collective-permute-start | bytes 3145736 | tf_op jit(solution)/shard_map/ppermute | solution.py:17
  98.1 48.0 %collective-permute-start.15 = (bf16[1,1,128,2816]{3,2,1,0:T(8,128)(2,1)}, bf16[1,1,128,2816]{3,2,1,0:T(8,128)(2,1)}, u32[]{:S(2)}, u32[]{:S(2)}) collective-permute-start(bf16[1,1,128,2816]{3,2,1,0:T(8,128)(2,1)} %bitcast.227), channel_id=1, source_target_pairs={{0,16},{8,24},{16,0},{24,8},{1,17},{9,25},{17,1},{25,9},{2,18},{10... | collective-permute-start | bytes 2162696 | tf_op jit(solution)/shard_map/ppermute | solution.py:34
  104.5 41.5 %collective-permute-start.18 = (bf16[128,1408]{1,0:T(8,128)(2,1)}, bf16[128,1408]{1,0:T(8,128)(2,1)}, u32[]{:S(2)}, u32[]{:S(2)}) collective-permute-start(bf16[128,1408]{1,0:T(8,128)(2,1)} %get-tuple-element.560), channel_id=1, source_target_pairs={{0,4},{4,0},{1,5},{5,1},{2,6},{6,2},{3,7},{7,3},{8,12},{12,8},{9,1... | collective-permute-start | bytes 1081352 | tf_op jit(solution)/shard_map/ppermute | solution.py:21
  167.1 27.2 %collective-permute-start.26 = (bf16[4,1,128,2816]{3,2,1,0:T(8,128)(2,1)S(1)}, bf16[4,1,128,2816]{3,2,1,0:T(8,128)(2,1)S(1)}, u32[]{:S(2)}, u32[]{:S(2)}) collective-permute-start(bf16[4,1,128,2816]{3,2,1,0:T(8,128)(2,1)S(1)} %constant_dynamic-update-slice_fusion.8.own), channel_id=1, source_target_pairs={{0,2},{2,0},{1,3},{3,1},{4,6},{6,4},{5,7},{7,5},{8,10},{10,8},{9,1... | collective-permute-start | bytes 8650760 | tf_op jit(solution)/shard_map/ppermute | solution.py:29
  167.2 26.5 %collective-permute-start.24 = (bf16[1,1,128,2816]{3,2,1,0:T(8,128)(2,1)}, bf16[1,1,128,2816]{3,2,1,0:T(8,128)(2,1)S(1)}, u32[]{:S(2)}, u32[]{:S(2)}) collective-permute-start(bf16[1,1,128,2816]{3,2,1,0:T(8,128)(2,1)} %collective-permute-done.15), channel_id=1, source_target_pairs={{0,8},{8,0},{16,24},{24,16},{1,9},{9,1},{17,25},{25,17},{2,10},{10... | collective-permute-start | bytes 2162696 | tf_op jit(solution)/shard_map/ppermute | solution.py:34
  195.8 31.9 %collective-permute-start.29 = (bf16[4,1,128,2816]{3,2,1,0:T(8,128)(2,1)S(1)}, bf16[4,1,128,2816]{3,2,1,0:T(8,128)(2,1)S(1)}, u32[]{:S(2)}, u32[]{:S(2)}) collective-permute-start(bf16[4,1,128,2816]{3,2,1,0:T(8,128)(2,1)S(1)} %constant_dynamic-update-slice_fusion.10.peer), channel_id=1, source_target_pairs={{0,2},{2,0},{1,3},{3,1},{4,6},{6,4},{5,7},{7,5},{8,10},{10,8},{9,1... | collective-permute-start | bytes 8650760 | tf_op jit(solution)/shard_map/ppermute | solution.py:29
  307.6 35.0 %collective-permute-start.40 = (bf16[2,2,128,1408]{3,2,1,0:T(8,128)(2,1)}, bf16[2,2,128,1408]{3,2,1,0:T(8,128)(2,1)}, u32[]{:S(2)}, u32[]{:S(2)}) collective-permute-start(bf16[2,2,128,1408]{3,2,1,0:T(8,128)(2,1)} %fusion.43), channel_id=1, source_target_pairs={{0,8},{8,0},{16,24},{24,16},{1,9},{9,1},{17,25},{25,17},{2,10},{10... | collective-permute-start | bytes 4325384 | tf_op jit(solution)/shard_map/ppermute | solution.py:34
  369.1 26.3 %collective-permute-start.44 = (bf16[2,128,2048]{2,1,0:T(8,128)(2,1)}, bf16[2,128,2048]{2,1,0:T(8,128)(2,1)}, u32[]{:S(2)}, u32[]{:S(2)}) collective-permute-start(bf16[2,128,2048]{2,1,0:T(8,128)(2,1)} %get-tuple-element.638), channel_id=1, source_target_pairs={{0,1},{1,0},{2,3},{3,2},{4,5},{5,4},{6,7},{7,6},{8,9},{9,8},{10,11... | collective-permute-start | bytes 3145736 | tf_op jit(solution)/shard_map/ppermute | solution.py:17
  404.9 26.3 %collective-permute-start.51 = (bf16[2,2,128,640]{3,2,1,0:T(8,128)(2,1)S(1)}, bf16[2,2,128,640]{3,2,1,0:T(8,128)(2,1)}, u32[]{:S(2)}, u32[]{:S(2)}) collective-permute-start(bf16[2,2,128,640]{3,2,1,0:T(8,128)(2,1)S(1)} %get-tuple-element.660), channel_id=1, source_target_pairs={{0,8},{8,0},{16,24},{24,16},{1,9},{9,1},{17,25},{25,17},{2,10},{10... | collective-permute-start | bytes 1966088 | tf_op jit(solution)/shard_map/ppermute | solution.py:34
  431.2 48.9 %collective-permute-start.58 = (bf16[2,2,128,1408]{3,2,1,0:T(8,128)(2,1)}, bf16[2,2,128,1408]{3,2,1,0:T(8,128)(2,1)}, u32[]{:S(2)}, u32[]{:S(2)}) collective-permute-start(bf16[2,2,128,1408]{3,2,1,0:T(8,128)(2,1)} %get-tuple-element.694), channel_id=1, source_target_pairs={{0,8},{8,0},{16,24},{24,16},{1,9},{9,1},{17,25},{25,17},{2,10},{10... | collective-permute-start | bytes 4325384 | tf_op jit(solution)/shard_map/ppermute | solution.py:34
  446.3 32.7 %collective-permute-start.55 = (bf16[2,128,1024]{2,1,0:T(8,128)(2,1)}, bf16[2,128,1024]{2,1,0:T(8,128)(2,1)}, u32[]{:S(2)}, u32[]{:S(2)}) collective-permute-start(bf16[2,128,1024]{2,1,0:T(8,128)(2,1)} %get-tuple-element.689), channel_id=1, source_target_pairs={{0,4},{4,0},{1,5},{5,1},{2,6},{6,2},{3,7},{7,3},{8,12},{12,8},{9,1... | collective-permute-start | bytes 1572872 | tf_op jit(solution)/shard_map/ppermute | solution.py:21
  447.6 31.4 %collective-permute-start.56 = (bf16[2,128,1024]{2,1,0:T(8,128)(2,1)}, bf16[2,128,1024]{2,1,0:T(8,128)(2,1)}, u32[]{:S(2)}, u32[]{:S(2)}) collective-permute-start(bf16[2,128,1024]{2,1,0:T(8,128)(2,1)} %get-tuple-element.690), channel_id=1, source_target_pairs={{0,1},{1,0},{2,3},{3,2},{4,5},{5,4},{6,7},{7,6},{8,9},{9,8},{10,11... | collective-permute-start | bytes 1572872 | tf_op jit(solution)/shard_map/ppermute | solution.py:17
  448.4 29.8 %collective-permute-start.57 = (bf16[1,2,128,640]{3,2,1,0:T(8,128)(2,1)}, bf16[1,2,128,640]{3,2,1,0:T(8,128)(2,1)}, u32[]{:S(2)}, u32[]{:S(2)}) collective-permute-start(bf16[1,2,128,640]{3,2,1,0:T(8,128)(2,1)} %get-tuple-element.692), channel_id=1, source_target_pairs={{0,16},{8,24},{16,0},{24,8},{1,17},{9,25},{17,1},{25,9},{2,18},{10... | collective-permute-start | bytes 983048 | tf_op jit(solution)/shard_map/ppermute | solution.py:34
  449.8 29.2 %collective-permute-start.59 = (bf16[1,2,128,768]{3,2,1,0:T(8,128)(2,1)}, bf16[1,2,128,768]{3,2,1,0:T(8,128)(2,1)}, u32[]{:S(2)}, u32[]{:S(2)}) collective-permute-start(bf16[1,2,128,768]{3,2,1,0:T(8,128)(2,1)} %get-tuple-element.696), channel_id=1, source_target_pairs={{0,16},{8,24},{16,0},{24,8},{1,17},{9,25},{17,1},{25,9},{2,18},{10... | collective-permute-start | bytes 1179656 | tf_op jit(solution)/shard_map/ppermute | solution.py:34
  489.8 36.1 %collective-permute-start.64 = (bf16[1,2,128,1408]{3,2,1,0:T(8,128)(2,1)}, bf16[1,2,128,1408]{3,2,1,0:T(8,128)(2,1)S(1)}, u32[]{:S(2)}, u32[]{:S(2)}) collective-permute-start(bf16[1,2,128,1408]{3,2,1,0:T(8,128)(2,1)} %get-tuple-element.724), channel_id=1, source_target_pairs={{0,16},{8,24},{16,0},{24,8},{1,17},{9,25},{17,1},{25,9},{2,18},{10... | collective-permute-start | bytes 2162696 | tf_op jit(solution)/shard_map/ppermute | solution.py:34
  492.1 33.8 %collective-permute-start.61 = (bf16[2,128,2048]{2,1,0:T(8,128)(2,1)}, bf16[2,128,2048]{2,1,0:T(8,128)(2,1)}, u32[]{:S(2)}, u32[]{:S(2)}) collective-permute-start(bf16[2,128,2048]{2,1,0:T(8,128)(2,1)} %get-tuple-element.719), channel_id=1, source_target_pairs={{0,1},{1,0},{2,3},{3,2},{4,5},{5,4},{6,7},{7,6},{8,9},{9,8},{10,11... | collective-permute-start | bytes 3145736 | tf_op jit(solution)/shard_map/ppermute | solution.py:17
  492.9 33.1 %collective-permute-start.62 = (bf16[2,128,2048]{2,1,0:T(8,128)(2,1)}, bf16[2,128,2048]{2,1,0:T(8,128)(2,1)}, u32[]{:S(2)}, u32[]{:S(2)}) collective-permute-start(bf16[2,128,2048]{2,1,0:T(8,128)(2,1)} %get-tuple-element.720), channel_id=1, source_target_pairs={{0,4},{4,0},{1,5},{5,1},{2,6},{6,2},{3,7},{7,3},{8,12},{12,8},{9,1... | collective-permute-start | bytes 3145736 | tf_op jit(solution)/shard_map/ppermute | solution.py:21
  496.4 29.6 %collective-permute-start.65 = (bf16[128,1408]{1,0:T(8,128)(2,1)}, bf16[128,1408]{1,0:T(8,128)(2,1)}, u32[]{:S(2)}, u32[]{:S(2)}) collective-permute-start(bf16[128,1408]{1,0:T(8,128)(2,1)} %get-tuple-element.870), channel_id=1, source_target_pairs={{0,4},{4,0},{1,5},{5,1},{2,6},{6,2},{3,7},{7,3},{8,12},{12,8},{9,1... | collective-permute-start | bytes 1081352 | tf_op jit(solution)/shard_map/ppermute | solution.py:21
  500.3 27.7 %collective-permute-start.63 = (bf16[2,2,128,512]{3,2,1,0:T(8,128)(2,1)}, bf16[2,2,128,512]{3,2,1,0:T(8,128)(2,1)}, u32[]{:S(2)}, u32[]{:S(2)}) collective-permute-start(bf16[2,2,128,512]{3,2,1,0:T(8,128)(2,1)} %get-tuple-element.722), channel_id=1, source_target_pairs={{0,8},{8,0},{16,24},{24,16},{1,9},{9,1},{17,25},{25,17},{2,10},{10... | collective-permute-start | bytes 1572872 | tf_op jit(solution)/shard_map/ppermute | solution.py:34
  (151 other events, 2312.5 us)
